TPU v7x, 32 devices: a whole 2x2x4 slice. The times are simulated.
32 devices in a mesh: dp: 2 (over x), seq: 4 (over y, core), mp: 4 (over z).
Axes of the slice: x: 2, y: 2, z: 4, core: 2. Of those that a mesh axis runs over, the one named last changes fastest.
Arguments:
- source: bfloat16 [4, 1024, 1024], P('dp', ('seq', 'mp')), may hold values from -6 to 6
- target: bfloat16 [4, 1024, 1024], P('dp', ('seq', 'mp')), may hold values from -6 to 6
- cotangent: bfloat16 [4, 1024, 1024], P('dp', ('seq', 'mp')), may hold values from -6 to 6
- source_len: int32 [4], P('dp'), may hold values from 512 to 1024, as said below
- target_len: int32 [4], P('dp'), may hold values from 512 to 1024, as said below
- source_seg: int32 [4, 1024], P('dp'), may hold values from 0 to 7, as said below
- target_seg: int32 [4, 1024], P('dp'), may hold values from 0 to 7, as said below
- enc_qkv: bfloat16 [3, 1024, 1024], P(None, ('dp', 'seq'), 'mp'), may hold values from -0.1875 to 0.1875
- enc_proj: bfloat16 [1024, 1024], P('mp', ('dp', 'seq')), may hold values from -0.75 to 0.75
- enc_up: bfloat16 [1024, 4096], P(('dp', 'seq'), 'mp'), may hold values from -0.1875 to 0.1875
- enc_down: bfloat16 [4096, 1024], P('mp', ('dp', 'seq')), may hold values from -0.125 to 0.125
- enc_gain: float32 [3, 1024], P(None, ('dp', 'seq', 'mp')), may hold values from 0.1 to 1.9
- enc_shift: float32 [3, 1024], P(None, ('dp', 'seq', 'mp')), may hold values from -1.8 to 1.8
- dec_qkv: bfloat16 [3, 1024, 1024], P(None, ('dp', 'seq'), 'mp'), may hold values from -0.1875 to 0.1875
- dec_proj: bfloat16 [1024, 1024], P('mp', ('dp', 'seq')), may hold values from -0.75 to 0.75
- cross_qkv: bfloat16 [3, 1024, 1024], P(None, ('dp', 'seq'), 'mp'), may hold values from -0.1875 to 0.1875
- cross_proj: bfloat16 [1024, 1024], P('mp', ('dp', 'seq')), may hold values from -0.75 to 0.75
- dec_up: bfloat16 [1024, 4096], P(('dp', 'seq'), 'mp'), may hold values from -0.1875 to 0.1875
- dec_down: bfloat16 [4096, 1024], P('mp', ('dp', 'seq')), may hold values from -0.125 to 0.125
- dec_gain: float32 [4, 1024], P(None, ('dp', 'seq', 'mp')), may hold values from 0.1 to 1.9
- dec_shift: float32 [4, 1024], P(None, ('dp', 'seq', 'mp')), may hold values from -1.8 to 1.8
Outputs:
- decoded: bfloat16 [4, 1024, 1024], P('dp', ('seq', 'mp'))
- source_grad: float32 [4, 1024, 1024], P('dp', ('seq', 'mp'))
- target_grad: float32 [4, 1024, 1024], P('dp', ('seq', 'mp'))
- grad_enc_qkv: float32 [3, 1024, 1024], P(None, ('dp', 'seq'), 'mp')
- grad_enc_proj: float32 [1024, 1024], P('mp', ('dp', 'seq'))
- grad_enc_up: float32 [1024, 4096], P(('dp', 'seq'), 'mp')
- grad_enc_down: float32 [4096, 1024], P('mp', ('dp', 'seq'))
- grad_enc_gain: float32 [3, 1024], P(None, ('dp', 'seq', 'mp'))
- grad_enc_shift: float32 [3, 1024], P(None, ('dp', 'seq', 'mp'))
- grad_dec_qkv: float32 [3, 1024, 1024], P(None, ('dp', 'seq'), 'mp')
- grad_dec_proj: float32 [1024, 1024], P('mp', ('dp', 'seq'))
- grad_cross_qkv: float32 [3, 1024, 1024], P(None, ('dp', 'seq'), 'mp')
- grad_cross_proj: float32 [1024, 1024], P('mp', ('dp', 'seq'))
- grad_dec_up: float32 [1024, 4096], P(('dp', 'seq'), 'mp')
- grad_dec_down: float32 [4096, 1024], P('mp', ('dp', 'seq'))
- grad_dec_gain: float32 [4, 1024], P(None, ('dp', 'seq', 'mp'))
- grad_dec_shift: float32 [4, 1024], P(None, ('dp', 'seq', 'mp'))
Inputs may be any that keep to these rules, and one draw needn't show every extreme that they name: `source_len`: rows of a slot from its length on are padding; some slot of every draw has 1024 live rows. `target_len`: rows of a slot from its length on are padding; some slot of every draw has 1024 live rows. `source_seg`: ids never fall along a slot. A slot holds one pair (id 0 throughout) or 8 pairs, each with live rows; padding rows carry the last id. A slot's source and target hold the same number of pairs, and some slot of every draw holds 8. `target_seg`: ids never fall along a slot. A slot holds one pair (id 0 throughout) or 8 pairs, each with live rows; padding rows carry the last id. A slot's source and target hold the same number of pairs, and some slot of every draw holds 8.
All inputs are finite; a program needn't handle non-finite values.
Results may differ from a plain program's by a relative error of at most 0.035.
Values may be sent and summed in bfloat16 or wider, within the bound.
A program may use at most 192 MiB of HBM per device.

v0:
```python
import jax
import jax.numpy as jnp
from jax import lax
from jax.sharding import PartitionSpec as P

HEAD_DIM = 64
MICRO = 2


EPSILON = 1e-05
MASKED = -1000000000.0


def layer_norm(stream, norm_gain, norm_shift):
    average = jnp.mean(stream, -1, keepdims=True)
    centred = stream - average
    spread = jnp.mean(centred * centred, -1, keepdims=True)
    return centred * lax.rsqrt(spread + EPSILON) * norm_gain + norm_shift


def norm_back(stream, norm_gain, norm_shift, upstream):
    unused, pullback = jax.vjp(layer_norm, stream, norm_gain, norm_shift)
    return pullback(upstream)


def gelu_exact(values):
    return jax.nn.gelu(values, approximate=False)


def gather_rows(values):
    return lax.all_gather(values, "mp", axis=1, tiled=True)


def sum_rows(partial_sum):
    return lax.psum_scatter(
        partial_sum.astype(jnp.bfloat16), "mp", scatter_dimension=1, tiled=True
    ).astype(jnp.float32)


def project(inputs, weight):
    return jnp.einsum("brd,de->bre", inputs, weight, preferred_element_type=jnp.float32)


def project_back(grads, weight):
    return jnp.einsum("bre,de->brd", grads, weight, preferred_element_type=jnp.float32)


def weight_grad(inputs, grads):
    return jnp.einsum("brd,bre->de", inputs, grads, preferred_element_type=jnp.float32)


def split_heads(values):
    return values.reshape(values.shape[0], values.shape[1], values.shape[2] // HEAD_DIM, HEAD_DIM)


def join_heads(values):
    return values.reshape(values.shape[0], values.shape[1], values.shape[2] * values.shape[3])


def attention_scores(queries, keys_all, allowed):
    raw = jnp.einsum("bqhd,bkhd->bhqk", queries, keys_all, preferred_element_type=jnp.float32)
    return jnp.where(allowed[:, None], raw * HEAD_DIM ** (-0.5), MASKED)


def attention_forward(query_rows, key_rows, w_query, w_key, w_value, w_out, allowed):
    queries = split_heads(project(query_rows, w_query).astype(jnp.bfloat16))
    keys_own = project(key_rows, w_key).astype(jnp.bfloat16)
    values_own = project(key_rows, w_value).astype(jnp.bfloat16)
    keys_all, values_all = (
        lax.all_gather(keys_own, "seq", axis=1, tiled=True),
        lax.all_gather(values_own, "seq", axis=1, tiled=True),
    )
    keys_all = split_heads(keys_all)
    values_all = split_heads(values_all)
    scores = attention_scores(queries, keys_all, allowed)
    row_max = jnp.max(scores, -1, keepdims=True)
    raised = jnp.exp(scores - row_max)
    row_total = jnp.sum(raised, -1, keepdims=True)
    attn_probs = raised / row_total
    log_total = row_max + jnp.log(row_total)
    mixed_heads = jnp.einsum(
        "bhqk,bkhd->bqhd",
        attn_probs.astype(jnp.bfloat16),
        values_all,
        preferred_element_type=jnp.float32,
    )
    mixed_heads = join_heads(mixed_heads).astype(jnp.bfloat16)
    branch = sum_rows(project(mixed_heads, w_out))
    return (branch, (queries, keys_all, values_all, log_total, mixed_heads))


def attention_backward(
    upstream, kept, query_rows, key_rows, w_query, w_key, w_value, w_out, allowed
):
    queries, keys_all, values_all, log_total, mixed_heads = kept
    grad_branch = gather_rows(upstream.astype(jnp.bfloat16))
    grad_w_out = weight_grad(mixed_heads, grad_branch)
    grad_mixed = split_heads(project_back(grad_branch, w_out).astype(jnp.bfloat16))
    scores = attention_scores(queries, keys_all, allowed)
    attn_probs = jnp.exp(scores - log_total)
    grad_values = jnp.einsum(
        "bhqk,bqhd->bkhd",
        attn_probs.astype(jnp.bfloat16),
        grad_mixed,
        preferred_element_type=jnp.float32,
    )
    grad_probs = jnp.einsum(
        "bqhd,bkhd->bhqk", grad_mixed, values_all, preferred_element_type=jnp.float32
    )
    grad_scores = attn_probs * grad_probs - attn_probs * jnp.sum(
        attn_probs * grad_probs, -1, keepdims=True
    )
    grad_raw = (grad_scores * HEAD_DIM ** (-0.5)).astype(jnp.bfloat16)
    grad_query = jnp.einsum(
        "bhqk,bkhd->bqhd", grad_raw, keys_all, preferred_element_type=jnp.float32
    )
    grad_query = join_heads(grad_query).astype(jnp.bfloat16)
    grad_keys = jnp.einsum("bhqk,bqhd->bkhd", grad_raw, queries, preferred_element_type=jnp.float32)
    grad_keys, grad_values = (
        lax.psum_scatter(
            join_heads(grad_keys).astype(jnp.bfloat16), "seq", scatter_dimension=1, tiled=True
        ).astype(jnp.float32),
        lax.psum_scatter(
            join_heads(grad_values).astype(jnp.bfloat16), "seq", scatter_dimension=1, tiled=True
        ).astype(jnp.float32),
    )
    grad_keys = grad_keys.astype(jnp.bfloat16)
    grad_values = grad_values.astype(jnp.bfloat16)
    weight_grads = (
        weight_grad(query_rows, grad_query),
        weight_grad(key_rows, grad_keys),
        weight_grad(key_rows, grad_values),
        grad_w_out,
    )
    grad_query_rows = project_back(grad_query, w_query)
    grad_key_rows = project_back(grad_keys, w_key) + project_back(grad_values, w_value)
    return (weight_grads, grad_query_rows, grad_key_rows)


def ffn_forward(normed, w_up, w_down):
    activation = project(normed, w_up)
    hidden = gelu_exact(activation).astype(jnp.bfloat16)
    return (sum_rows(project(hidden, w_down)), (activation, hidden))


def ffn_backward(upstream, kept, normed, w_up, w_down):
    activation, hidden = kept
    grad_branch = gather_rows(upstream.astype(jnp.bfloat16))
    grad_down = weight_grad(hidden, grad_branch)
    grad_hidden = project_back(grad_branch, w_down)
    unused, pullback = jax.vjp(gelu_exact, activation)
    grad_act = pullback(grad_hidden)[0].astype(jnp.bfloat16)
    grad_up = weight_grad(normed, grad_act)
    return ((grad_up, grad_down), sum_rows(project_back(grad_act, w_up)))


def gather_weights(shards):
    (
        enc_qkv_s,
        enc_proj_s,
        enc_up_s,
        enc_down_s,
        dec_qkv_s,
        dec_proj_s,
        cross_qkv_s,
        cross_proj_s,
        dec_up_s,
        dec_down_s,
    ) = shards
    return (
        lax.all_gather(enc_qkv_s, ("dp", "seq"), axis=1, tiled=True),
        lax.all_gather(enc_proj_s, ("dp", "seq"), axis=1, tiled=True),
        lax.all_gather(enc_up_s, ("dp", "seq"), axis=0, tiled=True),
        lax.all_gather(enc_down_s, ("dp", "seq"), axis=1, tiled=True),
        lax.all_gather(dec_qkv_s, ("dp", "seq"), axis=1, tiled=True),
        lax.all_gather(dec_proj_s, ("dp", "seq"), axis=1, tiled=True),
        lax.all_gather(cross_qkv_s, ("dp", "seq"), axis=1, tiled=True),
        lax.all_gather(cross_proj_s, ("dp", "seq"), axis=1, tiled=True),
        lax.all_gather(dec_up_s, ("dp", "seq"), axis=0, tiled=True),
        lax.all_gather(dec_down_s, ("dp", "seq"), axis=1, tiled=True),
    )


def scatter_weights(grads_full):
    (
        enc_qkv_g,
        enc_proj_g,
        enc_up_g,
        enc_down_g,
        dec_qkv_g,
        dec_proj_g,
        cross_qkv_g,
        cross_proj_g,
        dec_up_g,
        dec_down_g,
    ) = grads_full
    return (
        lax.psum_scatter(enc_qkv_g, ("dp", "seq"), scatter_dimension=1, tiled=True),
        lax.psum_scatter(enc_proj_g, ("dp", "seq"), scatter_dimension=1, tiled=True),
        lax.psum_scatter(enc_up_g, ("dp", "seq"), scatter_dimension=0, tiled=True),
        lax.psum_scatter(enc_down_g, ("dp", "seq"), scatter_dimension=1, tiled=True),
        lax.psum_scatter(dec_qkv_g, ("dp", "seq"), scatter_dimension=1, tiled=True),
        lax.psum_scatter(dec_proj_g, ("dp", "seq"), scatter_dimension=1, tiled=True),
        lax.psum_scatter(cross_qkv_g, ("dp", "seq"), scatter_dimension=1, tiled=True),
        lax.psum_scatter(cross_proj_g, ("dp", "seq"), scatter_dimension=1, tiled=True),
        lax.psum_scatter(dec_up_g, ("dp", "seq"), scatter_dimension=0, tiled=True),
        lax.psum_scatter(dec_down_g, ("dp", "seq"), scatter_dimension=1, tiled=True),
    )


def gather_norms(norm_shards):
    enc_gain_s, enc_shift_s, dec_gain_s, dec_shift_s = norm_shards
    return (
        lax.all_gather(enc_gain_s, ("dp", "seq", "mp"), axis=1, tiled=True),
        lax.all_gather(enc_shift_s, ("dp", "seq", "mp"), axis=1, tiled=True),
        lax.all_gather(dec_gain_s, ("dp", "seq", "mp"), axis=1, tiled=True),
        lax.all_gather(dec_shift_s, ("dp", "seq", "mp"), axis=1, tiled=True),
    )


def scatter_norms(norm_grads):
    enc_gain_g, enc_shift_g, dec_gain_g, dec_shift_g = norm_grads
    return (
        lax.psum_scatter(enc_gain_g, ("dp", "seq", "mp"), scatter_dimension=1, tiled=True),
        lax.psum_scatter(enc_shift_g, ("dp", "seq", "mp"), scatter_dimension=1, tiled=True),
        lax.psum_scatter(dec_gain_g, ("dp", "seq", "mp"), scatter_dimension=1, tiled=True),
        lax.psum_scatter(dec_shift_g, ("dp", "seq", "mp"), scatter_dimension=1, tiled=True),
    )


def slot_masks(src_length, tgt_length, src_segment, tgt_segment, row_count):
    seq_index = lax.axis_index("seq")
    key_pos = jnp.arange(src_segment.shape[1])
    query_pos = seq_index * row_count + jnp.arange(row_count)
    source_query = lax.dynamic_slice_in_dim(src_segment, seq_index * row_count, row_count, 1)
    target_query = lax.dynamic_slice_in_dim(tgt_segment, seq_index * row_count, row_count, 1)
    source_live = key_pos[None, None, :] < src_length[:, None, None]
    target_live = key_pos[None, None, :] < tgt_length[:, None, None]
    enc_allowed = (source_query[:, :, None] == src_segment[:, None, :]) & source_live
    self_allowed = (
        (target_query[:, :, None] == tgt_segment[:, None, :])
        & target_live
        & (key_pos[None, None, :] <= query_pos[None, :, None])
    )
    cross_allowed = (target_query[:, :, None] == src_segment[:, None, :]) & source_live
    return (enc_allowed, self_allowed, cross_allowed)


def run_micro(source_rows, target_rows, grad_out, allowed_sets, weights, norm_vectors):
    enc_allowed, self_allowed, cross_allowed = allowed_sets
    (
        enc_qkv_w,
        enc_proj_w,
        enc_up_w,
        enc_down_w,
        dec_qkv_w,
        dec_proj_w,
        cross_qkv_w,
        cross_proj_w,
        dec_up_w,
        dec_down_w,
    ) = weights
    enc_gain_w, enc_shift_w, dec_gain_w, dec_shift_w = norm_vectors
    stream_in = source_rows.astype(jnp.float32)
    normed_a = gather_rows(
        layer_norm(stream_in, enc_gain_w[0], enc_shift_w[0]).astype(jnp.bfloat16)
    )
    branch, kept_a = attention_forward(
        normed_a, normed_a, enc_qkv_w[0], enc_qkv_w[1], enc_qkv_w[2], enc_proj_w, enc_allowed
    )
    stream_mid = stream_in + branch
    normed_b = gather_rows(
        layer_norm(stream_mid, enc_gain_w[1], enc_shift_w[1]).astype(jnp.bfloat16)
    )
    branch, kept_b = ffn_forward(normed_b, enc_up_w, enc_down_w)
    stream_end = stream_mid + branch
    memory = gather_rows(layer_norm(stream_end, enc_gain_w[2], enc_shift_w[2]).astype(jnp.bfloat16))
    target_in = target_rows.astype(jnp.float32)
    normed_c = gather_rows(
        layer_norm(target_in, dec_gain_w[0], dec_shift_w[0]).astype(jnp.bfloat16)
    )
    branch, kept_c = attention_forward(
        normed_c, normed_c, dec_qkv_w[0], dec_qkv_w[1], dec_qkv_w[2], dec_proj_w, self_allowed
    )
    target_mid = target_in + branch
    normed_d = gather_rows(
        layer_norm(target_mid, dec_gain_w[1], dec_shift_w[1]).astype(jnp.bfloat16)
    )
    branch, kept_d = attention_forward(
        normed_d,
        memory,
        cross_qkv_w[0],
        cross_qkv_w[1],
        cross_qkv_w[2],
        cross_proj_w,
        cross_allowed,
    )
    target_late = target_mid + branch
    normed_e = gather_rows(
        layer_norm(target_late, dec_gain_w[2], dec_shift_w[2]).astype(jnp.bfloat16)
    )
    branch, kept_e = ffn_forward(normed_e, dec_up_w, dec_down_w)
    target_end = target_late + branch
    decoded = layer_norm(target_end, dec_gain_w[3], dec_shift_w[3]).astype(jnp.bfloat16)
    grad_end, gain_three, shift_three = norm_back(
        target_end, dec_gain_w[3], dec_shift_w[3], grad_out.astype(jnp.float32)
    )
    dec_ffn_grads, grad_normed = ffn_backward(grad_end, kept_e, normed_e, dec_up_w, dec_down_w)
    grad_piece, gain_two, shift_two = norm_back(
        target_late, dec_gain_w[2], dec_shift_w[2], grad_normed
    )
    grad_late = grad_end + grad_piece
    cross_grads, grad_query_rows, grad_key_rows = attention_backward(
        grad_late,
        kept_d,
        normed_d,
        memory,
        cross_qkv_w[0],
        cross_qkv_w[1],
        cross_qkv_w[2],
        cross_proj_w,
        cross_allowed,
    )
    grad_piece, gain_one, shift_one = norm_back(
        target_mid, dec_gain_w[1], dec_shift_w[1], sum_rows(grad_query_rows)
    )
    grad_mid = grad_late + grad_piece
    grad_memory = sum_rows(grad_key_rows)
    self_grads, grad_query_rows, grad_key_rows = attention_backward(
        grad_mid,
        kept_c,
        normed_c,
        normed_c,
        dec_qkv_w[0],
        dec_qkv_w[1],
        dec_qkv_w[2],
        dec_proj_w,
        self_allowed,
    )
    grad_piece, gain_zero, shift_zero = norm_back(
        target_in, dec_gain_w[0], dec_shift_w[0], sum_rows(grad_query_rows + grad_key_rows)
    )
    target_grad = grad_mid + grad_piece
    grad_stream, enc_gain_two, enc_shift_two = norm_back(
        stream_end, enc_gain_w[2], enc_shift_w[2], grad_memory
    )
    enc_ffn_grads, grad_normed = ffn_backward(grad_stream, kept_b, normed_b, enc_up_w, enc_down_w)
    grad_piece, enc_gain_one, enc_shift_one = norm_back(
        stream_mid, enc_gain_w[1], enc_shift_w[1], grad_normed
    )
    grad_stream = grad_stream + grad_piece
    enc_grads, grad_query_rows, grad_key_rows = attention_backward(
        grad_stream,
        kept_a,
        normed_a,
        normed_a,
        enc_qkv_w[0],
        enc_qkv_w[1],
        enc_qkv_w[2],
        enc_proj_w,
        enc_allowed,
    )
    grad_piece, enc_gain_zero, enc_shift_zero = norm_back(
        stream_in, enc_gain_w[0], enc_shift_w[0], sum_rows(grad_query_rows + grad_key_rows)
    )
    source_grad = grad_stream + grad_piece
    weight_grads = (
        jnp.stack(enc_grads[:3]),
        enc_grads[3],
        enc_ffn_grads[0],
        enc_ffn_grads[1],
        jnp.stack(self_grads[:3]),
        self_grads[3],
        jnp.stack(cross_grads[:3]),
        cross_grads[3],
        dec_ffn_grads[0],
        dec_ffn_grads[1],
    )
    norm_grads = (
        jnp.stack((enc_gain_zero, enc_gain_one, enc_gain_two)),
        jnp.stack((enc_shift_zero, enc_shift_one, enc_shift_two)),
        jnp.stack((gain_zero, gain_one, gain_two, gain_three)),
        jnp.stack((shift_zero, shift_one, shift_two, shift_three)),
    )
    return ((decoded, source_grad, target_grad), weight_grads, norm_grads)


def local(
    source,
    target,
    cotangent,
    source_len,
    target_len,
    source_seg,
    target_seg,
    enc_qkv,
    enc_proj,
    enc_up,
    enc_down,
    enc_gain,
    enc_shift,
    dec_qkv,
    dec_proj,
    cross_qkv,
    cross_proj,
    dec_up,
    dec_down,
    dec_gain,
    dec_shift,
):
    shards = (
        enc_qkv,
        enc_proj,
        enc_up,
        enc_down,
        dec_qkv,
        dec_proj,
        cross_qkv,
        cross_proj,
        dec_up,
        dec_down,
    )
    norm_shards = (enc_gain, enc_shift, dec_gain, dec_shift)
    per_batch = source.shape[0] // MICRO
    row_count = source_seg.shape[1] // lax.axis_size("seq")
    pieces = []
    summed = None
    for micro_index in range(MICRO):
        start_slot = micro_index * per_batch
        end_slot = start_slot + per_batch
        allowed_sets = slot_masks(
            source_len[start_slot:end_slot],
            target_len[start_slot:end_slot],
            source_seg[start_slot:end_slot],
            target_seg[start_slot:end_slot],
            row_count,
        )
        result, weight_grads, norm_grads = run_micro(
            source[start_slot:end_slot],
            target[start_slot:end_slot],
            cotangent[start_slot:end_slot],
            allowed_sets,
            gather_weights(shards),
            gather_norms(norm_shards),
        )
        pieces.append(result)
        shares = (scatter_weights(weight_grads), scatter_norms(norm_grads))
        summed = shares if summed is None else jax.tree.map(jnp.add, summed, shares)
    decoded = jnp.concatenate([micro_out[0] for micro_out in pieces], 0)
    source_grad = jnp.concatenate([micro_out[1] for micro_out in pieces], 0)
    target_grad = jnp.concatenate([micro_out[2] for micro_out in pieces], 0)
    weight_shares, norm_shares = summed
    return (
        decoded,
        source_grad,
        target_grad,
        weight_shares[0],
        weight_shares[1],
        weight_shares[2],
        weight_shares[3],
        norm_shares[0],
        norm_shares[1],
        weight_shares[4],
        weight_shares[5],
        weight_shares[6],
        weight_shares[7],
        weight_shares[8],
        weight_shares[9],
        norm_shares[2],
        norm_shares[3],
    )


def solution(mesh):
    return jax.shard_map(
        local,
        mesh=mesh,
        in_specs=(
            P("dp", ("seq", "mp"), None),
            P("dp", ("seq", "mp"), None),
            P("dp", ("seq", "mp"), None),
            P("dp"),
            P("dp"),
            P("dp", None),
            P("dp", None),
            P(None, ("dp", "seq"), "mp"),
            P("mp", ("dp", "seq")),
            P(("dp", "seq"), "mp"),
            P("mp", ("dp", "seq")),
            P(None, ("dp", "seq", "mp")),
            P(None, ("dp", "seq", "mp")),
            P(None, ("dp", "seq"), "mp"),
            P("mp", ("dp", "seq")),
            P(None, ("dp", "seq"), "mp"),
            P("mp", ("dp", "seq")),
            P(("dp", "seq"), "mp"),
            P("mp", ("dp", "seq")),
            P(None, ("dp", "seq", "mp")),
            P(None, ("dp", "seq", "mp")),
        ),
        out_specs=(
            P("dp", ("seq", "mp"), None),
            P("dp", ("seq", "mp"), None),
            P("dp", ("seq", "mp"), None),
            P(None, ("dp", "seq"), "mp"),
            P("mp", ("dp", "seq")),
            P(("dp", "seq"), "mp"),
            P("mp", ("dp", "seq")),
            P(None, ("dp", "seq", "mp")),
            P(None, ("dp", "seq", "mp")),
            P(None, ("dp", "seq"), "mp"),
            P("mp", ("dp", "seq")),
            P(None, ("dp", "seq"), "mp"),
            P("mp", ("dp", "seq")),
            P(("dp", "seq"), "mp"),
            P("mp", ("dp", "seq")),
            P(None, ("dp", "seq", "mp")),
            P(None, ("dp", "seq", "mp")),
        ),
        check_vma=False,
    )
```

profile of v0, /device:TPU:0, one launch (start us, length us, event | category | flops | bytes accessed | tf_op | source)
XLA Modules:
  0.0 2588.7 jit_solution(3686987285542393900)
XLA Ops:
  17.5 70.7 %all-gather.14 = f32[32,32,3]{1,2,0:T(4,128)S(1)} all-gather(f32[1,32,3]{1,2,0:T(4,128)} %bitcast.873), channel_id=1, replica_groups=mesh['dp'=2,'seq'=4,'mp'=4] {'dp','seq','mp'}, dimensions={0}, use_global_device_ids=true | all-gather | bytes 12672 | tf_op jit(solution)/shard_map/all_gather | solution.py:214
  88.9 64.1 %all-gather.15 = f32[32,32,3]{1,2,0:T(4,128)S(1)} all-gather(f32[1,32,3]{1,2,0:T(4,128)} %bitcast.874), channel_id=1, replica_groups=mesh['dp'=2,'seq'=4,'mp'=4] {'dp','seq','mp'}, dimensions={0}, use_global_device_ids=true | all-gather | bytes 12672 | tf_op jit(solution)/shard_map/all_gather | solution.py:215
  153.6 66.2 %all-gather.12 = f32[32,32,4]{1,2,0:T(4,128)S(1)} all-gather(f32[1,32,4]{1,2,0:T(4,128)} %bitcast.875), channel_id=1, replica_groups=mesh['dp'=2,'seq'=4,'mp'=4] {'dp','seq','mp'}, dimensions={0}, use_global_device_ids=true | all-gather | bytes 16896 | tf_op jit(solution)/shard_map/all_gather | solution.py:216
  220.0 64.1 %all-gather.13 = f32[32,32,4]{1,2,0:T(4,128)S(1)} all-gather(f32[1,32,4]{1,2,0:T(4,128)} %bitcast.876), channel_id=1, replica_groups=mesh['dp'=2,'seq'=4,'mp'=4] {'dp','seq','mp'}, dimensions={0}, use_global_device_ids=true | all-gather | bytes 16896 | tf_op jit(solution)/shard_map/all_gather | solution.py:217
  411.4 18.7 all_gather.187
  458.5 21.7 all_gather.184
  611.8 19.2 all_gather.193
  637.1 23.0 reduce-scatter.61.cloned.1.call-done
  765.8 22.3 reduce-scatter.63.cloned.1.call-done
  874.2 19.1 reduce-scatter.65.cloned.1.call-done
  921.7 18.4 all_gather.200
  948.3 19.7 reduce-scatter.93.cloned.1.call-done
  1103.1 21.1 reduce-scatter.117.cloned.1.call-done
  1124.2 22.1 reduce-scatter.109.cloned.1.call-done
  1168.9 22.6 reduce-scatter.83.cloned.1.call-done
  1472.9 20.0 reduce-scatter.115.cloned.1.call-done
  1492.9 22.2 reduce-scatter.123.cloned.1.call-done
  1537.8 22.7 reduce-scatter.107.cloned.1.call-done
  1617.5 78.2 %reduce-scatter.149.cloned.1.call-done = f32[32,4]{1,0:T(8,128)} async-done(((f32[1024,4]{1,0:T(8,128)}), f32[32,4]{1,0:T(8,128)}) %reduce-scatter.149.cloned.1.call-update) | async-done | bytes 528
  1697.1 131.2 %reduce-scatter.151.cloned.1.call-done = f32[32,4]{1,0:T(8,128)} async-done(((f32[1024,4]{1,0:T(8,128)}), f32[32,4]{1,0:T(8,128)}) %reduce-scatter.151.cloned.1.call-update) | async-done | bytes 528
  1831.1 129.9 %reduce-scatter.145.cloned.1.call-done = f32[32,3]{1,0:T(8,128)} async-done(((f32[1024,3]{1,0:T(8,128)}), f32[32,3]{1,0:T(8,128)}) %reduce-scatter.145.cloned.1.call-update) | async-done | bytes 400
  1962.4 131.3 %reduce-scatter.147.cloned.1.call-done = f32[32,3]{1,0:T(8,128)} async-done(((f32[1024,3]{1,0:T(8,128)}), f32[32,3]{1,0:T(8,128)}) %reduce-scatter.147.cloned.1.call-update) | async-done | bytes 400
  2095.0 34.7 %reduce-scatter.139.cloned.1.call-done = f32[256,128]{1,0:T(8,128)} async-done(((f32[256,1024]{1,0:T(8,128)}), f32[256,128]{1,0:T(8,128)}) %reduce-scatter.139.cloned.1.call-update) | async-done | bytes 131088 | tf_op jit(solution)/shard_map/reduce_scatter | solution.py:205
  2129.6 39.6 %reduce-scatter.135.cloned.1.call-done = f32[256,128]{1,0:T(8,128)} async-done(((f32[256,1024]{1,0:T(8,128)}), f32[256,128]{1,0:T(8,128)}) %reduce-scatter.135.cloned.1.call-update) | async-done | bytes 131088 | tf_op jit(solution)/shard_map/reduce_scatter | solution.py:203
  2169.3 39.7 %reduce-scatter.127.cloned.1.call-done = f32[256,128]{1,0:T(8,128)} async-done(((f32[256,1024]{1,0:T(8,128)}), f32[256,128]{1,0:T(8,128)}) %reduce-scatter.127.cloned.1.call-update) | async-done | bytes 131088 | tf_op jit(solution)/shard_map/reduce_scatter | solution.py:199
  2208.9 55.1 %reduce-scatter.141.cloned.1.call-done = f32[128,1024]{1,0:T(8,128)} async-done(((f32[1024,1024]{1,0:T(8,128)}), f32[128,1024]{1,0:T(8,128)}) %reduce-scatter.141.cloned.1.call-update) | async-done | bytes 524304 | tf_op jit(solution)/shard_map/reduce_scatter | solution.py:206
  2264.1 55.6 %reduce-scatter.143.cloned.1.call-done = f32[1024,128]{1,0:T(8,128)} async-done(((f32[1024,1024]{1,0:T(8,128)}), f32[1024,128]{1,0:T(8,128)}) %reduce-scatter.143.cloned.1.call-update) | async-done | bytes 524304 | tf_op jit(solution)/shard_map/reduce_scatter | solution.py:207
  2319.7 50.1 %reduce-scatter.137.cloned.1.call-done = f32[3,128,256]{2,1,0:T(8,128)} async-done(((f32[3,1024,256]{2,1,0:T(8,128)}), f32[3,128,256]{2,1,0:T(8,128)}) %reduce-scatter.137.cloned.1.call-update) | async-done | bytes 393232 | tf_op jit(solution)/shard_map/reduce_scatter | solution.py:204
  2369.8 50.6 %reduce-scatter.133.cloned.1.call-done = f32[3,128,256]{2,1,0:T(8,128)} async-done(((f32[3,1024,256]{2,1,0:T(8,128)}), f32[3,128,256]{2,1,0:T(8,128)}) %reduce-scatter.133.cloned.1.call-update) | async-done | bytes 393232 | tf_op jit(solution)/shard_map/reduce_scatter | solution.py:202
  2420.4 55.1 %reduce-scatter.129.cloned.1.call-done = f32[128,1024]{1,0:T(8,128)} async-done(((f32[1024,1024]{1,0:T(8,128)}), f32[128,1024]{1,0:T(8,128)}) %reduce-scatter.129.cloned.1.call-update) | async-done | bytes 524304 | tf_op jit(solution)/shard_map/reduce_scatter | solution.py:200
  2475.5 55.6 %reduce-scatter.131.cloned.1.call-done = f32[1024,128]{1,0:T(8,128)} async-done(((f32[1024,1024]{1,0:T(8,128)}), f32[1024,128]{1,0:T(8,128)}) %reduce-scatter.131.cloned.1.call-update) | async-done | bytes 524304 | tf_op jit(solution)/shard_map/reduce_scatter | solution.py:201
  2531.2 50.2 %reduce-scatter.125.cloned.1.call-done = f32[3,128,256]{2,1,0:T(8,128)} async-done(((f32[3,1024,256]{2,1,0:T(8,128)}), f32[3,128,256]{2,1,0:T(8,128)}) %reduce-scatter.125.cloned.1.call-update) | async-done | bytes 393232 | tf_op jit(solution)/shard_map/reduce_scatter | solution.py:198
  (1062 shorter events, 1054.5 us)
Async XLA Ops:
  7.2 336.2 %all-gather.24.cloned.1.call-start = ((), (), s32[]{:S(2)}) async-start(), calls=%async_computation.48 | async-start | bytes 1769472 | tf_op jit(solution)/shard_map/all_gather | solution.py:175
  7.9 353.9 %all-gather.26.cloned.1.call-start = ((), (), s32[]{:S(2)}) async-start(), calls=%async_computation.50 | async-start | bytes 1769472 | tf_op jit(solution)/shard_map/all_gather | solution.py:171
  8.7 400.5 %reduce-scatter.59.cloned.1.call-start = ((), (), s32[]{:S(2)}) async-start(), calls=%async_computation.51 | async-start | bytes 655360 | tf_op jit(solution)/shard_map/reduce_scatter | solution.py:35
  394.9 123.1 %reduce-scatter.69.cloned.1.call-start = ((), (), s32[]{:S(2)}) async-start(), calls=%async_computation.61 | async-start | bytes 655360 | tf_op jit(solution)/shard_map/reduce_scatter | solution.py:35
  506.9 124.0 %all-gather.32.cloned.1.call-start = ((), (), s32[]{:S(2)}) async-start(), calls=%async_computation.55 | async-start | bytes 1769472 | tf_op jit(solution)/shard_map/all_gather | solution.py:177
  507.7 129.4 %reduce-scatter.71.cloned.1.call-start = ((), (), s32[]{:S(2)}) async-start(), calls=%async_computation.62 | async-start | bytes 655360 | tf_op jit(solution)/shard_map/reduce_scatter | solution.py:35
  595.4 170.4 %reduce-scatter.73.cloned.1.call-start = ((), (), s32[]{:S(2)}) async-start(), calls=%async_computation.63 | async-start | bytes 655360 | tf_op jit(solution)/shard_map/reduce_scatter | solution.py:35
  752.7 118.6 %reduce-scatter.75.cloned.1.call-start = ((), (), s32[]{:S(2)}) async-start(), calls=%async_computation.64 | async-start | bytes 655360 | tf_op jit(solution)/shard_map/reduce_scatter | solution.py:35
  946.5 132.4 %reduce-scatter.95.cloned.1.call-start = ((), (), s32[]{:S(2)}) async-start(), calls=%async_computation.74 | async-start | bytes 655360 | tf_op jit(solution)/shard_map/reduce_scatter | solution.py:120
  1103.0 214.2 %reduce-scatter.101.cloned.1.call-start = ((), (), s32[]{:S(2)}) async-start(), calls=%async_computation.77 | async-start | bytes 655360 | tf_op jit(solution)/shard_map/reduce_scatter | solution.py:35
  1240.8 160.0 %reduce-scatter.111.cloned.1.call-start = ((), (), s32[]{:S(2)}) async-start(), calls=%async_computation.82 | async-start | bytes 655360 | tf_op jit(solution)/shard_map/reduce_scatter | solution.py:120
  1275.7 127.4 %reduce-scatter.113.cloned.1.call-start = ((), (), s32[]{:S(2)}) async-start(), calls=%async_computation.83 | async-start | bytes 655360 | tf_op jit(solution)/shard_map/reduce_scatter | solution.py:123
  1280.9 139.7 %reduce-scatter.119.cloned.1.call-start = ((), (), s32[]{:S(2)}) async-start(), calls=%async_computation.86 | async-start | bytes 655360 | tf_op jit(solution)/shard_map/reduce_scatter | solution.py:120
  1312.5 110.3 %reduce-scatter.121.cloned.1.call-start = ((), (), s32[]{:S(2)}) async-start(), calls=%async_computation.87 | async-start | bytes 655360 | tf_op jit(solution)/shard_map/reduce_scatter | solution.py:123
  1317.1 121.7 %reduce-scatter.87.cloned.1.call-start = ((), (), s32[]{:S(2)}) async-start(), calls=%async_computation.70 | async-start | bytes 655360 | tf_op jit(solution)/shard_map/reduce_scatter | solution.py:120
  1405.9 109.1 %reduce-scatter.123.cloned.1.call-start = ((), (), s32[]{:S(2)}) async-start(), calls=%async_computation.88 | async-start | bytes 655360 | tf_op jit(solution)/shard_map/reduce_scatter | solution.py:35
  1425.6 112.3 %reduce-scatter.91.cloned.1.call-start = ((), (), s32[]{:S(2)}) async-start(), calls=%async_computation.72 | async-start | bytes 655360 | tf_op jit(solution)/shard_map/reduce_scatter | solution.py:35
  1443.9 116.7 %reduce-scatter.107.cloned.1.call-start = ((), (), s32[]{:S(2)}) async-start(), calls=%async_computation.80 | async-start | bytes 655360 | tf_op jit(solution)/shard_map/reduce_scatter | solution.py:35
  1471.3 224.4 %reduce-scatter.149.cloned.1.call-start = ((), (), s32[]{:S(2)}) async-start(), calls=%async_computation.101 | async-start | bytes 540672
  1521.5 306.8 %reduce-scatter.151.cloned.1.call-start = ((), (), s32[]{:S(2)}) async-start(), calls=%async_computation.102 | async-start | bytes 540672
  1522.7 438.3 %reduce-scatter.145.cloned.1.call-start = ((), (), s32[]{:S(2)}) async-start(), calls=%async_computation.99 | async-start | bytes 540672
  1565.1 528.5 %reduce-scatter.147.cloned.1.call-start = ((), (), s32[]{:S(2)}) async-start(), calls=%async_computation.100 | async-start | bytes 540672
  1566.4 563.3 %reduce-scatter.139.cloned.1.call-start = ((), (), s32[]{:S(2)}) async-start(), calls=%async_computation.96 | async-start | bytes 1179648 | tf_op jit(solution)/shard_map/reduce_scatter | solution.py:205
  1569.1 600.2 %reduce-scatter.135.cloned.1.call-start = ((), (), s32[]{:S(2)}) async-start(), calls=%async_computation.94 | async-start | bytes 1179648 | tf_op jit(solution)/shard_map/reduce_scatter | solution.py:203
  1570.8 638.1 %reduce-scatter.127.cloned.1.call-start = ((), (), s32[]{:S(2)}) async-start(), calls=%async_computation.90 | async-start | bytes 1179648 | tf_op jit(solution)/shard_map/reduce_scatter | solution.py:199
  1573.4 690.6 %reduce-scatter.141.cloned.1.call-start = ((), (), s32[]{:S(2)}) async-start(), calls=%async_computation.97 | async-start | bytes 4718592 | tf_op jit(solution)/shard_map/reduce_scatter | solution.py:206
  1578.2 741.5 %reduce-scatter.143.cloned.1.call-start = ((), (), s32[]{:S(2)}) async-start(), calls=%async_computation.98 | async-start | bytes 4718592 | tf_op jit(solution)/shard_map/reduce_scatter | solution.py:207
  1582.9 786.8 %reduce-scatter.137.cloned.1.call-start = ((), (), s32[]{:S(2)}) async-start(), calls=%async_computation.95 | async-start | bytes 3538944 | tf_op jit(solution)/shard_map/reduce_scatter | solution.py:204
  1590.3 830.1 %reduce-scatter.133.cloned.1.call-start = ((), (), s32[]{:S(2)}) async-start(), calls=%async_computation.93 | async-start | bytes 3538944 | tf_op jit(solution)/shard_map/reduce_scatter | solution.py:202
  1596.2 879.3 %reduce-scatter.129.cloned.1.call-start = ((), (), s32[]{:S(2)}) async-start(), calls=%async_computation.91 | async-start | bytes 4718592 | tf_op jit(solution)/shard_map/reduce_scatter | solution.py:200
  1601.1 930.0 %reduce-scatter.131.cloned.1.call-start = ((), (), s32[]{:S(2)}) async-start(), calls=%async_computation.92 | async-start | bytes 4718592 | tf_op jit(solution)/shard_map/reduce_scatter | solution.py:201
  1605.8 975.6 %reduce-scatter.125.cloned.1.call-start = ((), (), s32[]{:S(2)}) async-start(), calls=%async_computation.89 | async-start | bytes 3538944 | tf_op jit(solution)/shard_map/reduce_scatter | solution.py:198
  (314 other events, 13577.2 us)
Sparse Core Ops, SparseCore 0:
  9.9 28.4 all-gather.23
  40.3 25.7 all-gather.25
  411.9 22.0 reduce-scatter.56
  456.3 24.7 reduce-scatter.68
  527.9 26.1 all-gather.27
  556.0 28.1 all-gather.29
  586.1 25.6 all-gather.31
  614.5 22.5 reduce-scatter.70
  789.9 26.2 all-gather.33
  817.9 28.1 all-gather.35
  920.6 22.0 reduce-scatter.76
  1054.3 21.7 reduce-scatter.78
  1216.7 21.8 reduce-scatter.100
  1241.5 21.8 reduce-scatter.84
  1299.0 21.7 reduce-scatter.112
  1347.4 21.7 reduce-scatter.120
  1421.8 21.7 reduce-scatter.102
  1446.6 21.6 reduce-scatter.104
  1563.4 132.2 reduce-scatter.148
  1697.9 130.3 reduce-scatter.150
  1830.6 130.3 reduce-scatter.144
  1963.2 130.3 reduce-scatter.146
  2097.2 32.3 reduce-scatter.138
  2133.2 35.9 reduce-scatter.134
  2172.9 36.0 reduce-scatter.126
  2212.7 51.2 reduce-scatter.140
  2268.4 51.2 reduce-scatter.142
  2323.5 46.2 reduce-scatter.136
  2374.1 46.2 reduce-scatter.132
  2424.2 51.3 reduce-scatter.128
  2479.8 51.2 reduce-scatter.130
  2535.1 46.2 reduce-scatter.124
  (23 shorter events, 473.1 us)
where the time goes:
time: 2600 us; the launch traced here: 2590 us
  waiting for transfers between devices  1310 us (50%)
  blocking collectives  750 us (29%)
  matrix products  367 us (14%)
  other arithmetic  86.8 us (3%)
  local copies, waits for them, and re-layouts  49 us (2%)
    unnamed x59, waiting for transfers between devices  476 us
    all_gather x22, blocking collectives, gather_rows(): return lax.all_gather(values, 'mp', axis=1, tiled=True)  368 us
    reduce_scatter x22, waiting for transfers between devices, sum_rows(): lax.psum_scatter(partial_sum.astype(jnp.bfloat16), 'mp', scatter_dimensio...  297 us
    dot_general x6, matrix products, attention_backward(): jnp.einsum('bhqk,bkhd->bqhd', grad_raw, keys_all, preferred_element_type=...  72.1 us
    all_gather x1, blocking collectives, gather_norms(): lax.all_gather(enc_gain_s, ('dp', 'seq', 'mp'), axis=1, tiled=True)  70.7 us
    dot_general x6, matrix products, attention_backward(): jnp.einsum('bhqk,bqhd->bkhd', grad_raw, queries, preferred_element_type=j...  70 us
    dot_general x32, matrix products, project(): jnp.einsum('brd,de->bre', inputs, weight, preferred_element_type=jnp.floa...  67.4 us
    all_gather x1, blocking collectives, gather_norms(): lax.all_gather(dec_gain_s, ('dp', 'seq', 'mp'), axis=1, tiled=True)  66.2 us
  transfers between devices with their start and end apart: 55, of which 35 were waited for; matrix products, arithmetic and copies ran while one was open for 16% of the time, Pallas kernels for 0%

commit v1 on v0

v1 whole, which is shorter than its diff:
```python
import jax
import jax.numpy as jnp
from jax import lax
from jax.experimental import pallas as pl
from jax.experimental.pallas import tpu as pltpu
from jax.sharding import Mesh, PartitionSpec as P

HEAD_DIM = 64
EPSILON = 1e-05
MASKED = -1000000000.0
AXES = ("hi", "k", "y", "c", "mp")
MESH_ID = pl.DeviceIdType.MESH
F32 = jnp.float32
BF16 = jnp.bfloat16
SWAP = [(0, 1), (1, 0)]


def plane_place():
    hi, k, y, c, z = (lax.axis_index(name) for name in AXES)
    partners = ((1 - hi, k, 1 - y, c, z), (1 - hi, k, y, c, z), (hi, k, 1 - y, c, z))
    blocks = ((1 - y) * 2 + 1 - hi, y * 2 + 1 - hi, (1 - y) * 2 + hi)
    return partners, blocks, y * 2 + hi


def greet(partners):
    barrier = pltpu.get_barrier_semaphore()
    for partner in partners:
        pl.semaphore_signal(barrier, inc=1, device_id=partner, device_id_type=MESH_ID)
    pl.semaphore_wait(barrier, len(partners))


def gather_kernel(h_ref, out_ref, send_sem, recv_sem):
    partners, unused, mine = plane_place()
    greet(partners)
    copies = []
    for i, partner in enumerate(partners):
        copy = pltpu.make_async_remote_copy(
            src_ref=h_ref,
            dst_ref=out_ref.at[mine],
            send_sem=send_sem.at[i],
            recv_sem=recv_sem.at[i],
            device_id=partner,
            device_id_type=MESH_ID,
        )
        copy.start()
        copies.append(copy)
    out_ref[mine] = h_ref[...]
    for copy in copies:
        copy.wait()


def gather_rows(own):
    rows, width = own.shape
    out = pl.pallas_call(
        gather_kernel,
        out_shape=jax.ShapeDtypeStruct((4, rows, width), own.dtype),
        in_specs=[pl.BlockSpec(memory_space=pltpu.VMEM)],
        out_specs=pl.BlockSpec(memory_space=pltpu.VMEM),
        scratch_shapes=[pltpu.SemaphoreType.DMA((3,)), pltpu.SemaphoreType.DMA((3,))],
        compiler_params=pltpu.CompilerParams(collective_id=0, has_side_effects=True),
        name="gather_rows",
    )(own)
    return out.reshape(4 * rows, width)


def scatter_kernel(p_ref, out_ref, landed, send_sem, recv_sem):
    partners, blocks, mine = plane_place()
    greet(partners)
    copies = []
    for i, partner in enumerate(partners):
        copy = pltpu.make_async_remote_copy(
            src_ref=p_ref.at[blocks[i]],
            dst_ref=landed.at[i],
            send_sem=send_sem.at[i],
            recv_sem=recv_sem.at[i],
            device_id=partner,
            device_id_type=MESH_ID,
        )
        copy.start()
        copies.append(copy)
    for copy in copies:
        copy.wait()
    total = p_ref[mine].astype(F32) + landed[0].astype(F32)
    out_ref[...] = total + landed[1].astype(F32) + landed[2].astype(F32)


def sum_rows(partial):
    rows, width = partial.shape[0] // 4, partial.shape[1]
    return pl.pallas_call(
        scatter_kernel,
        out_shape=jax.ShapeDtypeStruct((rows, width), F32),
        in_specs=[pl.BlockSpec(memory_space=pltpu.VMEM)],
        out_specs=pl.BlockSpec(memory_space=pltpu.VMEM),
        scratch_shapes=[
            pltpu.VMEM((3, rows, width), BF16),
            pltpu.SemaphoreType.DMA((3,)),
            pltpu.SemaphoreType.DMA((3,)),
        ],
        compiler_params=pltpu.CompilerParams(collective_id=1, has_side_effects=True),
        name="sum_rows",
    )(partial.astype(BF16).reshape(4, rows, width))


def norm_forward(stream, gain, shift):
    average = jnp.mean(stream, -1, keepdims=True)
    centred = stream - average
    scale = lax.rsqrt(jnp.mean(centred * centred, -1, keepdims=True) + EPSILON)
    unit = centred * scale
    return unit * gain + shift, (unit, scale)


def norm_back(kept, gain, upstream):
    unit, scale = kept
    inner = upstream * gain
    grad = scale * (
        inner - jnp.mean(inner, -1, keepdims=True) - unit * jnp.mean(inner * unit, -1, keepdims=True)
    )
    return grad, jnp.sum(upstream * unit, 0), jnp.sum(upstream, 0)


def nt(left, right):
    return lax.dot_general(left, right, (((1,), (1,)), ((), ())), preferred_element_type=F32)


def nn(left, right):
    return lax.dot_general(left, right, (((1,), (0,)), ((), ())), preferred_element_type=F32)


def tn(left, right):
    return lax.dot_general(left, right, (((0,), (0,)), ((), ())), preferred_element_type=F32)


def heads(values):
    return values.reshape(values.shape[0], values.shape[1] // HEAD_DIM, HEAD_DIM)


def swap_core(values):
    return lax.ppermute(values, "c", SWAP)


def whole_keys(own):
    return jnp.concatenate([own, swap_core(own)], 0)


def own_keys(partial):
    half = partial.shape[0] // 2
    partial = partial.astype(BF16)
    return (partial[:half].astype(F32) + swap_core(partial[half:]).astype(F32)).astype(BF16)


def attend(queries, keys, values, allowed):
    raw = jnp.einsum("qhd,khd->hqk", heads(queries), heads(keys), preferred_element_type=F32)
    scores = jnp.where(allowed[None], raw * HEAD_DIM ** (-0.5), MASKED)
    row_max = jnp.max(scores, -1, keepdims=True)
    raised = jnp.exp(scores - row_max)
    total = jnp.sum(raised, -1, keepdims=True)
    probs = raised / total
    mixed = jnp.einsum(
        "hqk,khd->qhd", probs.astype(BF16), heads(values), preferred_element_type=F32
    )
    mixed = mixed.reshape(queries.shape).astype(BF16)
    return mixed, (queries, keys, values, row_max + jnp.log(total))


def attend_back(kept, grad_mixed, allowed):
    queries, keys, values, log_total = kept
    raw = jnp.einsum("qhd,khd->hqk", heads(queries), heads(keys), preferred_element_type=F32)
    scores = jnp.where(allowed[None], raw * HEAD_DIM ** (-0.5), MASKED)
    probs = jnp.exp(scores - log_total)
    grad_mixed = heads(grad_mixed)
    grad_values = jnp.einsum(
        "hqk,qhd->khd", probs.astype(BF16), grad_mixed, preferred_element_type=F32
    )
    grad_probs = jnp.einsum(
        "qhd,khd->hqk", grad_mixed, heads(values), preferred_element_type=F32
    )
    weighted = probs * grad_probs
    grad_scores = weighted - probs * jnp.sum(weighted, -1, keepdims=True)
    grad_raw = (grad_scores * HEAD_DIM ** (-0.5)).astype(BF16)
    grad_queries = jnp.einsum("hqk,khd->qhd", grad_raw, heads(keys), preferred_element_type=F32)
    grad_keys = jnp.einsum("hqk,qhd->khd", grad_raw, heads(queries), preferred_element_type=F32)
    return (
        grad_queries.reshape(queries.shape).astype(BF16),
        own_keys(grad_keys.reshape(keys.shape)),
        own_keys(grad_values.reshape(values.shape)),
    )


def gelu(values):
    return jax.nn.gelu(values, approximate=False)


def gelu_back(activation, upstream):
    unused, pullback = jax.vjp(gelu, activation)
    return pullback(upstream)[0]


def pack_attend(qkv, proj):
    stacked = jnp.concatenate([jnp.swapaxes(qkv, 1, 2), proj[None]], 0)
    count, units, width = stacked.shape
    return jnp.swapaxes(stacked.reshape(count, 4, units // 4, width), 0, 1).reshape(4, -1, width)


def pack_feed(up, down):
    stacked = jnp.stack([up.T, down])
    count, units, width = stacked.shape
    return jnp.swapaxes(stacked.reshape(count, 4, units // 4, width), 0, 1).reshape(4, -1, width)


def unpack(packed, count):
    parts, rows, width = packed.shape
    unpacked = packed.reshape(parts, count, rows // count, width)
    return jnp.swapaxes(unpacked, 0, 1).reshape(count, parts * rows // count, width)


def gather_weights(packed, count):
    rows, width = packed.shape[1:]
    copies = lax.axis_size("k")
    if copies > 1:
        packed = lax.all_gather(packed, "k", axis=2, tiled=True)
    packed = lax.all_to_all(packed, ("hi", "y"), 0, 0, tiled=True)
    packed = lax.all_gather(lax.all_gather(packed, "mp"), "c")
    packed = packed.reshape(2, 4, 2, 2, rows, copies, width)
    packed = packed.transpose(1, 4, 2, 5, 3, 0, 6).reshape(4, rows, 8 * copies * width)
    return unpack(packed, count)


def scatter_weights(grads):
    parts, rows, total = grads.shape
    copies = lax.axis_size("k")
    width = total // (8 * copies)
    grads = grads.astype(BF16).reshape(4, rows, 2, copies, 2, 2, width)
    grads = grads.transpose(5, 0, 2, 4, 1, 3, 6).reshape(2, 4, 4, rows, copies * width)
    grads = lax.psum_scatter(grads, "c", scatter_dimension=0)
    grads = lax.psum_scatter(grads, "mp", scatter_dimension=0)
    grads = lax.all_to_all(grads, ("hi", "y"), 0, 0, tiled=True).astype(F32)
    if copies > 1:
        grads = lax.psum_scatter(grads, "k", scatter_dimension=2, tiled=True)
    return grads


def by_z(stacked):
    count, units, width = stacked.shape
    return jnp.swapaxes(stacked.reshape(count, 4, units // 4, width), 0, 1).reshape(4, -1, width)


def slot_perm(step):
    copies = lax.axis_size("k")
    sizes = (2, copies, 2, 2, 4)

    def flat(hi, k, y, c, z):
        return (((hi * sizes[1] + k) * 2 + y) * 2 + c) * 4 + z

    pairs = []
    for hi in range(2):
        for k in range(copies):
            for y in range(2):
                for c in range(2):
                    for z in range(4):
                        pairs.append(
                            (flat(hi, k, y, c, z), flat(z // 2, k, y, c, 2 * hi + (z % 2 ^ step)))
                        )
    return pairs


def to_slot(rows):
    odd = lax.axis_index("mp") % 2
    first, second = (
        lax.ppermute(jnp.where(odd == step, rows[0], rows[1]), AXES, slot_perm(step))
        for step in range(2)
    )
    return jnp.concatenate(
        [jnp.where(odd == 0, first, second), jnp.where(odd == 0, second, first)], 0
    )


def from_slot(rows):
    half = rows.shape[0] // 2
    odd = lax.axis_index("mp") % 2
    first, second = (
        lax.ppermute(jnp.where(odd == step, rows[:half], rows[half:]), AXES, slot_perm(step))
        for step in range(2)
    )
    return jnp.stack([jnp.where(odd == 0, first, second), jnp.where(odd == 0, second, first)])


def slot_facts(lengths, segments):
    packed = jnp.concatenate([segments, jnp.broadcast_to(lengths[:, None], (2, 128))], 1)
    z = lax.axis_index("mp")
    other = lax.ppermute(packed, "hi", SWAP)
    chosen = jnp.where(lax.axis_index("hi") == z // 2, packed, other)
    chosen = jnp.where(z % 2 == 0, chosen[0], chosen[1])
    length = segments.shape[1]
    return chosen[length], chosen[:length]


def row_order(values):
    c = lax.axis_index("c")
    split = values.reshape(2, 2, values.shape[0] // 4)
    own = jnp.where(c == 0, split[:, 0], split[:, 1]).reshape(-1)
    other = jnp.where(c == 0, split[:, 1], split[:, 0]).reshape(-1)
    return own, jnp.concatenate([own, other])


def local(
    source,
    target,
    cotangent,
    source_len,
    target_len,
    source_seg,
    target_seg,
    enc_qkv,
    enc_proj,
    enc_up,
    enc_down,
    enc_gain,
    enc_shift,
    dec_qkv,
    dec_proj,
    cross_qkv,
    cross_proj,
    dec_up,
    dec_down,
    dec_gain,
    dec_shift,
):
    vectors = jnp.concatenate([enc_gain, enc_shift, dec_gain, dec_shift], 0)
    for name in ("mp", "c", "y", "k", "hi"):
        if lax.axis_size(name) > 1:
            vectors = lax.all_gather(vectors, name, axis=1, tiled=True)
    enc_g, enc_b, dec_g, dec_b = vectors[:3], vectors[3:6], vectors[6:10], vectors[10:]

    enc_w = gather_weights(pack_attend(enc_qkv, enc_proj), 4)
    self_w = gather_weights(pack_attend(dec_qkv, dec_proj), 4)
    enc_f = gather_weights(pack_feed(enc_up, enc_down), 2)
    cross_w = gather_weights(pack_attend(cross_qkv, cross_proj), 4)
    dec_f = gather_weights(pack_feed(dec_up, dec_down), 2)

    source_length, source_ids = slot_facts(source_len, source_seg)
    target_length, target_ids = slot_facts(target_len, target_seg)
    place, key_place = row_order(jnp.arange(source_ids.shape[0]))
    source_query, source_key = row_order(source_ids)
    target_query, target_key = row_order(target_ids)
    source_live = key_place[None] < source_length
    enc_allowed = (source_query[:, None] == source_key[None]) & source_live
    self_allowed = (
        (target_query[:, None] == target_key[None])
        & (key_place[None] < target_length)
        & (key_place[None] <= place[:, None])
    )
    cross_allowed = (target_query[:, None] == source_key[None]) & source_live

    stream_in = to_slot(source).astype(F32)
    target_in = to_slot(target).astype(F32)
    grad_out = to_slot(cotangent).astype(F32)

    def projections(rows, weights, keys_only=False):
        made = nt(rows, weights).astype(BF16)
        return made

    normed, kept_a = norm_forward(stream_in, enc_g[0], enc_b[0])
    rows_a = gather_rows(normed.astype(BF16))
    normed, kept_c = norm_forward(target_in, dec_g[0], dec_b[0])
    rows_c = gather_rows(normed.astype(BF16))
    width = enc_w.shape[1]

    def self_attend(rows, weights, allowed):
        made = nt(rows, weights[:3].reshape(3 * width, -1)).astype(BF16)
        key_value = whole_keys(made[:, width:])
        mixed, kept = attend(made[:, :width], key_value[:, :width], key_value[:, width:], allowed)
        return sum_rows(nn(mixed, weights[3])), (mixed, kept)

    branch, enc_kept = self_attend(rows_a, enc_w, enc_allowed)
    stream_mid = stream_in + branch
    normed, kept_b = norm_forward(stream_mid, enc_g[1], enc_b[1])
    rows_b = gather_rows(normed.astype(BF16))
    enc_act = nt(rows_b, enc_f[0])
    enc_hidden = gelu(enc_act).astype(BF16)
    stream_end = stream_mid + sum_rows(nn(enc_hidden, enc_f[1]))
    normed, kept_m = norm_forward(stream_end, enc_g[2], enc_b[2])
    memory = gather_rows(normed.astype(BF16))

    branch, self_kept = self_attend(rows_c, self_w, self_allowed)
    target_mid = target_in + branch
    normed, kept_d = norm_forward(target_mid, dec_g[1], dec_b[1])
    rows_d = gather_rows(normed.astype(BF16))
    cross_q = nt(rows_d, cross_w[0]).astype(BF16)
    cross_kv = whole_keys(nt(memory, cross_w[1:3].reshape(2 * width, -1)).astype(BF16))
    cross_mixed, cross_kept = attend(
        cross_q, cross_kv[:, :width], cross_kv[:, width:], cross_allowed
    )
    target_late = target_mid + sum_rows(nn(cross_mixed, cross_w[3]))
    normed, kept_e = norm_forward(target_late, dec_g[2], dec_b[2])
    rows_e = gather_rows(normed.astype(BF16))
    dec_act = nt(rows_e, dec_f[0])
    dec_hidden = gelu(dec_act).astype(BF16)
    target_end = target_late + sum_rows(nn(dec_hidden, dec_f[1]))
    normed, kept_o = norm_forward(target_end, dec_g[3], dec_b[3])
    decoded = normed.astype(BF16)

    def feed_back(grad, act, hidden, rows, weights):
        grad_rows = gather_rows(grad.astype(BF16))
        grad_act = gelu_back(act, nt(grad_rows, weights[1])).astype(BF16)
        shares = jnp.stack([tn(grad_act, rows), tn(hidden, grad_rows)])
        return sum_rows(nn(grad_act, weights[0])), shares

    def attend_grads(grad, kept, allowed, query_rows, key_rows, weights):
        mixed, kept = kept
        grad_rows = gather_rows(grad.astype(BF16))
        grad_mixed = nt(grad_rows, weights[3]).astype(BF16)
        grad_q, grad_k, grad_v = attend_back(kept, grad_mixed, allowed)
        shares = jnp.stack(
            [tn(grad_q, query_rows), tn(grad_k, key_rows), tn(grad_v, key_rows), tn(mixed, grad_rows)]
        )
        return grad_q, jnp.concatenate([grad_k, grad_v], 1), shares

    grad_end, gain_3, shift_3 = norm_back(kept_o, dec_g[3], grad_out)
    grad_normed, dec_f_share = feed_back(grad_end, dec_act, dec_hidden, rows_e, dec_f)
    dec_f_grad = scatter_weights(by_z(dec_f_share))
    piece, gain_2, shift_2 = norm_back(kept_e, dec_g[2], grad_normed)
    grad_late = grad_end + piece
    grad_q, grad_kv, cross_share = attend_grads(
        grad_late, (cross_mixed, cross_kept), cross_allowed, rows_d, memory, cross_w
    )
    cross_grad = scatter_weights(by_z(cross_share))
    grad_memory = sum_rows(nn(grad_kv, cross_w[1:3].reshape(2 * width, -1)))
    piece, gain_1, shift_1 = norm_back(kept_d, dec_g[1], sum_rows(nn(grad_q, cross_w[0])))
    grad_mid = grad_late + piece

    grad_stream, enc_gain_2, enc_shift_2 = norm_back(kept_m, enc_g[2], grad_memory)
    grad_normed, enc_f_share = feed_back(grad_stream, enc_act, enc_hidden, rows_b, enc_f)
    enc_f_grad = scatter_weights(by_z(enc_f_share))

    grad_q, grad_kv, self_share = attend_grads(
        grad_mid, self_kept, self_allowed, rows_c, rows_c, self_w
    )
    self_grad = scatter_weights(by_z(self_share))
    piece, gain_0, shift_0 = norm_back(
        kept_c,
        dec_g[0],
        sum_rows(nn(jnp.concatenate([grad_q, grad_kv], 1), self_w[:3].reshape(3 * width, -1))),
    )
    target_grad = grad_mid + piece

    piece, enc_gain_1, enc_shift_1 = norm_back(kept_b, enc_g[1], grad_normed)
    grad_stream = grad_stream + piece
    grad_q, grad_kv, enc_share = attend_grads(
        grad_stream, enc_kept, enc_allowed, rows_a, rows_a, enc_w
    )
    piece, enc_gain_0, enc_shift_0 = norm_back(
        kept_a,
        enc_g[0],
        sum_rows(nn(jnp.concatenate([grad_q, grad_kv], 1), enc_w[:3].reshape(3 * width, -1))),
    )
    source_grad = grad_stream + piece

    norm_share = jnp.stack(
        [enc_gain_0, enc_gain_1, enc_gain_2, enc_shift_0, enc_shift_1, enc_shift_2]
        + [gain_0, gain_1, gain_2, gain_3, shift_0, shift_1, shift_2, shift_3]
    )
    norm_share = jnp.concatenate([norm_share, jnp.zeros_like(norm_share[:2])], 0)
    enc_grad = scatter_weights(by_z(enc_share))
    norm_grad = scatter_weights(jnp.broadcast_to(norm_share[None], (4, 16, norm_share.shape[1])))
    norm_grad = jnp.sum(norm_grad, 0)
    part = norm_grad.shape[1] // 4
    norm_grad = lax.dynamic_slice_in_dim(norm_grad, lax.axis_index("mp") * part, part, 1)

    def attend_shares(grads):
        grads = unpack(grads, 4)
        return jnp.swapaxes(grads[:3], 1, 2), grads[3]

    def feed_shares(grads):
        grads = unpack(grads, 2)
        return grads[0].T, grads[1]

    enc_a, enc_o = attend_shares(enc_grad)
    self_a, self_o = attend_shares(self_grad)
    cross_a, cross_o = attend_shares(cross_grad)
    enc_u, enc_d = feed_shares(enc_f_grad)
    dec_u, dec_d = feed_shares(dec_f_grad)
    return (
        from_slot(decoded),
        from_slot(source_grad),
        from_slot(target_grad),
        enc_a,
        enc_o,
        enc_u,
        enc_d,
        norm_grad[:3],
        norm_grad[3:6],
        self_a,
        self_o,
        cross_a,
        cross_o,
        dec_u,
        dec_d,
        norm_grad[6:10],
        norm_grad[10:14],
    )


def solution(mesh):
    dp, seq, mp = (mesh.shape[name] for name in ("dp", "seq", "mp"))
    assert dp % 2 == 0 and seq == 4 and mp == 4
    fine = Mesh(mesh.devices.reshape(2, dp // 2, 2, 2, 4), AXES)
    d, s = ("hi", "k"), ("y", "c")
    rows = P(d, s + ("mp",), None)
    three, flat = P(None, d + s, "mp"), P("mp", d + s)
    up, vector = P(d + s, "mp"), P(None, d + s + ("mp",))
    attention, feeding = (three, flat), (up, flat)
    return jax.shard_map(
        local,
        mesh=fine,
        in_specs=(rows,) * 3
        + (P(d), P(d), P(d, None), P(d, None))
        + attention
        + feeding
        + (vector, vector)
        + attention * 2
        + feeding
        + (vector, vector),
        out_specs=(rows,) * 3
        + attention
        + feeding
        + (vector, vector)
        + attention * 2
        + feeding
        + (vector, vector),
        check_vma=False,
    )
```

time: 2600 us -> 1290 us (0.50)
  waiting for transfers between devices: 1310 us -> 276 us
  blocking collectives: 750 us -> 95 us
  Pallas kernels: 0 us -> 363 us
  local copies, waits for them, and re-layouts: 49 us -> 172 us
  matrix products: 367 us -> 250 us
  starting transfers between devices: 3.69 us -> 41.3 us
    all_gather x41 -> x4, blocking collectives: 750 us -> 44.2 us  [local(): vectors = lax.all_gather(vectors, name, axis=1, tiled=True)]
    reduce_scatter x44 -> x12, waiting for transfers between devices: 805 us -> 176 us  [the longest x6 169 us: scatter_weights(): grads = lax.psum_scatter(grads, 'mp', scatter_dimension=0)]
    unnamed x59 -> x22, waiting for transfers between devices: 476 us -> 3.6 us
    pallas_call x0 -> x22, Pallas kernels: none -> 363 us  [the longest x11 183 us: gather_rows(): pl.pallas_call(gather_kernel, out_shape=jax.ShapeDtypeStruct((4, rows, wi...]
    dot_general x132 -> x56, matrix products: 367 us -> 250 us  [the longest x3 65.8 us: attend_back(): jnp.einsum('hqk,khd->qhd', grad_raw, heads(keys), preferred_element_type=...]
    all_to_all x0 -> x5, blocking collectives: none -> 50.8 us  [gather_weights(): packed = lax.all_to_all(packed, ('hi', 'y'), 0, 0, tiled=True)]
    all_gather x7 -> x10, waiting for transfers between devices: 31.3 us -> 70.4 us  [gather_weights(): packed = lax.all_gather(lax.all_gather(packed, 'mp'), 'c')]
    another operation x0 -> x9, local copies, waits for them, and re-layouts: none -> 33.7 us  [the longest x5 26.3 us: unpack(): unpacked = packed.reshape(parts, count, rows // count, width)]
  transfers between devices with their start and end apart: 55 -> 51, of which waited for: 35 -> 16; matrix products, arithmetic and copies ran while one was open for 16% -> 25% of each run, Pallas kernels for 0% -> 17%
where the time goes in v1:
time: 1290 us; the launch traced here: 1280 us
  Pallas kernels  363 us (28%)
  waiting for transfers between devices  276 us (21%)
  matrix products  250 us (19%)
  local copies, waits for them, and re-layouts  172 us (13%)
  blocking collectives  95 us (7%)
  other arithmetic  64 us (5%)
  starting transfers between devices  41.3 us (3%)
  between operations  17.8 us (1%)
    pallas_call x11, Pallas kernels, gather_rows(): pl.pallas_call(gather_kernel, out_shape=jax.ShapeDtypeStruct((4, rows, wi...  183 us
    pallas_call x11, Pallas kernels, sum_rows(): pl.pallas_call(scatter_kernel, out_shape=jax.ShapeDtypeStruct((rows, widt...  180 us
    reduce_scatter x6, waiting for transfers between devices, scatter_weights(): grads = lax.psum_scatter(grads, 'mp', scatter_dimension=0)  169 us
    all_gather x10, waiting for transfers between devices, gather_weights(): packed = lax.all_gather(lax.all_gather(packed, 'mp'), 'c')  70.4 us
    dot_general x3, matrix products, attend_back(): jnp.einsum('hqk,khd->qhd', grad_raw, heads(keys), preferred_element_type=...  65.8 us
    dot_general x3, matrix products, attend_back(): jnp.einsum('hqk,qhd->khd', grad_raw, heads(queries), preferred_element_ty...  55.4 us
    all_to_all x5, blocking collectives, gather_weights(): packed = lax.all_to_all(packed, ('hi', 'y'), 0, 0, tiled=True)  50.8 us
    dot_general x11, matrix products, nt(): lax.dot_general(left, right, (((1,), (1,)), ((), ())), preferred_element_...  48.2 us
  transfers between devices with their start and end apart: 51, of which 16 were waited for; matrix products, arithmetic and copies ran while one was open for 25% of the time, Pallas kernels for 17%

profile of v1, /device:TPU:0, one launch (start us, length us, event | category | flops | bytes accessed | tf_op | source)
XLA Modules:
  0.0 1279.3 jit_solution(6276687393398551669)
XLA Ops:
  49.9 27.1 %all-gather.22.cloned.1.call-done = bf16[16,256,128]{2,1,0:T(8,128)(2,1)} async-done(((bf16[4,256,128]{2,1,0:T(8,128)(2,1)}), bf16[16,256,128]{2,1,0:T(8,128)(2,1)}) %all-gather.22.cloned.1.call-update) | async-done | bytes 1048592 | tf_op jit(solution)/shard_map/all_gather | solution.py:222
  94.6 32.4 %all-gather.10 = f32[4,32,14]{1,2,0:T(8,128)S(1)} all-gather(f32[1,32,14]{1,2,0:T(8,128)S(1)} %maximum_bitcast_fusion.8), channel_id=1, replica_groups=mesh['hi'=2,'k'=1,'y'=2,'c'=2,'mp'=4] {'mp'}, dimensions={0}, use_global_device_ids=true | all-gather | bytes 8960 | tf_op jit(solution)/shard_map/all_gather | solution.py:331
  144.4 33.4 %all-gather.30.cloned.1.call-done = bf16[16,512,128]{2,1,0:T(8,128)(2,1)} async-done(((bf16[4,512,128]{2,1,0:T(8,128)(2,1)}), bf16[16,512,128]{2,1,0:T(8,128)(2,1)}) %all-gather.30.cloned.1.call-update) | async-done | bytes 2097168 | tf_op jit(solution)/shard_map/all_gather | solution.py:222
  183.0 16.6 %gather_rows.11 = bf16[4,128,1024]{2,1,0:T(8,128)(2,1)} custom-call(bf16[128,1024]{1,0:T(8,128)(2,1)} %fusion.206.h_ref), custom_call_target="tpu_custom_call" | custom-call | tf_op jit(solution)/shard_map/gather_rows/pallas_call | solution.py:54
  291.1 17.6 %sum_rows.12 = f32[128,1024]{1,0:T(8,128)} custom-call(bf16[4,128,1024]{2,1,0:T(8,128)(2,1)} %bitcast.708), custom_call_target="tpu_custom_call" | custom-call | tf_op jit(solution)/shard_map/sum_rows/pallas_call | solution.py:89
  311.1 16.7 %gather_rows.13 = bf16[4,128,1024]{2,1,0:T(8,128)(2,1)} custom-call(bf16[128,1024]{1,0:T(8,128)(2,1)} %add_convert_fusion.8.h_ref), custom_call_target="tpu_custom_call" | custom-call | tf_op jit(solution)/shard_map/gather_rows/pallas_call | solution.py:54
  355.2 16.7 %gather_rows.15 = bf16[4,128,1024]{2,1,0:T(8,128)(2,1)} custom-call(bf16[128,1024]{1,0:T(8,128)(2,1)} %add_convert_fusion.6.h_ref), custom_call_target="tpu_custom_call" | custom-call | tf_op jit(solution)/shard_map/gather_rows/pallas_call | solution.py:54
  424.4 16.8 %gather_rows.14 = bf16[4,128,1024]{2,1,0:T(8,128)(2,1)} custom-call(bf16[128,1024]{1,0:T(8,128)(2,1)} %add_convert_fusion.7.h_ref), custom_call_target="tpu_custom_call" | custom-call | tf_op jit(solution)/shard_map/gather_rows/pallas_call | solution.py:54
  478.8 16.6 %sum_rows.14 = f32[128,1024]{1,0:T(8,128)} custom-call(bf16[4,128,1024]{2,1,0:T(8,128)(2,1)} %bitcast.710), custom_call_target="tpu_custom_call" | custom-call | tf_op jit(solution)/shard_map/sum_rows/pallas_call | solution.py:89
  497.7 16.7 %gather_rows.16 = bf16[4,128,1024]{2,1,0:T(8,128)(2,1)} custom-call(bf16[128,1024]{1,0:T(8,128)(2,1)} %add_convert_fusion.5.h_ref), custom_call_target="tpu_custom_call" | custom-call | tf_op jit(solution)/shard_map/gather_rows/pallas_call | solution.py:54
  524.1 16.1 %sum_rows.15 = f32[128,1024]{1,0:T(8,128)} custom-call(bf16[4,128,1024]{2,1,0:T(8,128)(2,1)} %bitcast.792), custom_call_target="tpu_custom_call" | custom-call | tf_op jit(solution)/shard_map/sum_rows/pallas_call | solution.py:89
  542.8 16.7 %gather_rows.17 = bf16[4,128,1024]{2,1,0:T(8,128)(2,1)} custom-call(bf16[128,1024]{1,0:T(8,128)(2,1)} %fusion.252.h_ref), custom_call_target="tpu_custom_call" | custom-call | tf_op jit(solution)/shard_map/gather_rows/pallas_call | solution.py:54
  571.5 16.1 %sum_rows.16 = f32[128,1024]{1,0:T(8,128)} custom-call(bf16[4,128,1024]{2,1,0:T(8,128)(2,1)} %bitcast.786), custom_call_target="tpu_custom_call" | custom-call | tf_op jit(solution)/shard_map/sum_rows/pallas_call | solution.py:89
  591.3 16.7 %gather_rows.18 = bf16[4,128,1024]{2,1,0:T(8,128)(2,1)} custom-call(bf16[128,1024]{1,0:T(8,128)(2,1)} %get-tuple-element.109.h_ref), custom_call_target="tpu_custom_call" | custom-call | tf_op jit(solution)/shard_map/gather_rows/pallas_call | solution.py:54
  620.1 21.5 %fusion.158 = bf16[4,64,512]{2,1,0:T(8,128)(2,1)S(1)} fusion(bf16[1024,4,64]{0,2,1:T(8,128)(2,1)S(1)} %bitcast.726, f32[4,512,1024]{2,1,0:T(8,128)} %copy-done.2, f32[4,512]{1,0:T(4,128)S(1)} %log_add_fusion.2, f32[4,512,1024]{2,1,0:T(8,128)} %fusion.283), kind=kOutput, calls=%fused_computation.207 | convolution fusion | flops 285346816 | bytes 17571840 | tf_op jit(solution)/shard_map/hqk,khd->qhd/dot_general | solution.py:180
  641.6 18.7 %fusion.143 = bf16[1024,4,64]{0,2,1:T(8,128)(2,1)} fusion(bf16[512,4,64]{0,2,1:T(8,128)(2,1)S(1)} %bitcast.828, f32[4,512,1024]{2,1,0:T(8,128)} %copy-done.2, f32[4,512]{1,0:T(4,128)S(1)} %log_add_fusion.2, f32[4,512,1024]{2,1,0:T(8,128)} %fusion.283), kind=kOutput, calls=%fused_computation.198 | convolution fusion | flops 285477888 | bytes 17571840 | tf_op jit(solution)/shard_map/hqk,qhd->khd/dot_general | solution.py:181
  681.4 16.8 %gather_rows.21 = bf16[4,128,1024]{2,1,0:T(8,128)(2,1)} custom-call(bf16[128,1024]{1,0:T(8,128)(2,1)} %get-tuple-element.103.h_ref), custom_call_target="tpu_custom_call" | custom-call | tf_op jit(solution)/shard_map/gather_rows/pallas_call | solution.py:54
  709.5 22.2 %fusion.152 = bf16[4,64,512]{2,1,0:T(8,128)(2,1)} fusion(bf16[1024,4,64]{0,2,1:T(8,128)(2,1)S(1)} %bitcast.722, f32[4,512,1024]{2,1,0:T(8,128)} %copy-done.1, f32[4,512]{1,0:T(4,128)S(1)} %log_add_fusion, f32[4,512,1024]{2,1,0:T(8,128)} %fusion.285), kind=kOutput, calls=%fused_computation.205 | convolution fusion | flops 285346816 | bytes 17571840 | tf_op jit(solution)/shard_map/hqk,khd->qhd/dot_general | solution.py:180
  731.7 18.9 %fusion.149 = bf16[1024,4,64]{0,2,1:T(8,128)(2,1)} fusion(bf16[512,4,64]{0,2,1:T(8,128)(2,1)S(1)} %bitcast.782, f32[4,512,1024]{2,1,0:T(8,128)} %copy-done.1, f32[4,512]{1,0:T(4,128)S(1)} %log_add_fusion, f32[4,512,1024]{2,1,0:T(8,128)} %fusion.285), kind=kOutput, calls=%fused_computation.200 | convolution fusion | flops 285477888 | bytes 17571840 | tf_op jit(solution)/shard_map/hqk,qhd->khd/dot_general | solution.py:181
  757.7 16.4 %sum_rows.17 = f32[128,1024]{1,0:T(8,128)} custom-call(bf16[4,128,1024]{2,1,0:T(8,128)(2,1)} %bitcast.788), custom_call_target="tpu_custom_call" | custom-call | tf_op jit(solution)/shard_map/sum_rows/pallas_call | solution.py:89
  777.3 16.7 %gather_rows.19 = bf16[4,128,1024]{2,1,0:T(8,128)(2,1)} custom-call(bf16[128,1024]{1,0:T(8,128)(2,1)} %get-tuple-element.107.h_ref), custom_call_target="tpu_custom_call" | custom-call | tf_op jit(solution)/shard_map/gather_rows/pallas_call | solution.py:54
  825.7 16.8 %gather_rows.20 = bf16[4,128,1024]{2,1,0:T(8,128)(2,1)} custom-call(bf16[128,1024]{1,0:T(8,128)(2,1)} %get-tuple-element.105.h_ref), custom_call_target="tpu_custom_call" | custom-call | tf_op jit(solution)/shard_map/gather_rows/pallas_call | solution.py:54
  854.5 17.8 %fusion.146 = bf16[1024,4,64]{0,2,1:T(8,128)(2,1)S(1)} fusion(bf16[512,4,64]{0,2,1:T(8,128)(2,1)S(1)} %bitcast.780, f32[4,512,1024]{2,1,0:T(8,128)} %copy-done, f32[4,512]{1,0:T(4,128)S(1)} %copy-done.122, f32[4,512,1024]{2,1,0:T(8,128)} %fusion.284), kind=kOutput, calls=%fused_computation.199 | convolution fusion | flops 285477888 | bytes 17571840 | tf_op jit(solution)/shard_map/hqk,qhd->khd/dot_general | solution.py:181
  874.8 22.2 %fusion.155 = bf16[4,64,512]{2,1,0:T(8,128)(2,1)} fusion(bf16[1024,4,64]{0,2,1:T(8,128)(2,1)S(1)} %bitcast.716, f32[4,512,1024]{2,1,0:T(8,128)} %copy-done, f32[4,512]{1,0:T(4,128)S(1)} %copy-done.122, f32[4,512,1024]{2,1,0:T(8,128)} %fusion.284), kind=kOutput, calls=%fused_computation.206 | convolution fusion | flops 285346816 | bytes 17571840 | tf_op jit(solution)/shard_map/hqk,khd->qhd/dot_general | solution.py:180
  902.2 16.2 %sum_rows.21 = f32[128,1024]{1,0:T(8,128)} custom-call(bf16[4,128,1024]{2,1,0:T(8,128)(2,1)} %bitcast.789), custom_call_target="tpu_custom_call" | custom-call | tf_op jit(solution)/shard_map/sum_rows/pallas_call | solution.py:89
  924.4 17.0 %sum_rows.19 = f32[128,1024]{1,0:T(8,128)} custom-call(bf16[4,128,1024]{2,1,0:T(8,128)(2,1)} %bitcast.790), custom_call_target="tpu_custom_call" | custom-call | tf_op jit(solution)/shard_map/sum_rows/pallas_call | solution.py:89
  1048.5 29.6 %reduce-scatter.23.cloned.1.call-done = bf16[1,4,16,128]{3,2,1,0:T(8,128)(2,1)} async-done(((bf16[4,4,16,128]{3,2,1,0:T(8,128)(2,1)}), bf16[1,4,16,128]{3,2,1,0:T(8,128)(2,1)}) %reduce-scatter.23.cloned.1.call-update) | async-done | bytes 16400 | tf_op jit(solution)/shard_map/reduce_scatter | solution.py:235
  1088.6 22.4 %reduce-scatter.31.cloned.1.call-done = bf16[1,4,256,128]{3,2,1,0:T(8,128)(2,1)} async-done(((bf16[4,4,256,128]{3,2,1,0:T(8,128)(2,1)}), bf16[1,4,256,128]{3,2,1,0:T(8,128)(2,1)}) %reduce-scatter.31.cloned.1.call-update) | async-done | bytes 262160 | tf_op jit(solution)/shard_map/reduce_scatter | solution.py:235
  1115.2 25.1 %reduce-scatter.27.cloned.1.call-done = bf16[1,4,256,128]{3,2,1,0:T(8,128)(2,1)} async-done(((bf16[4,4,256,128]{3,2,1,0:T(8,128)(2,1)}), bf16[1,4,256,128]{3,2,1,0:T(8,128)(2,1)}) %reduce-scatter.27.cloned.1.call-update) | async-done | bytes 262160 | tf_op jit(solution)/shard_map/reduce_scatter | solution.py:235
  1149.3 19.0 %reduce-scatter.15.cloned.1.call-done = bf16[1,4,256,128]{3,2,1,0:T(8,128)(2,1)} async-done(((bf16[4,4,256,128]{3,2,1,0:T(8,128)(2,1)}), bf16[1,4,256,128]{3,2,1,0:T(8,128)(2,1)}) %reduce-scatter.15.cloned.1.call-update) | async-done | bytes 262160 | tf_op jit(solution)/shard_map/reduce_scatter | solution.py:235
  1177.3 35.9 %reduce-scatter.35.cloned.1.call-done = bf16[1,4,512,128]{3,2,1,0:T(8,128)(2,1)} async-done(((bf16[4,4,512,128]{3,2,1,0:T(8,128)(2,1)}), bf16[1,4,512,128]{3,2,1,0:T(8,128)(2,1)}) %reduce-scatter.35.cloned.1.call-update) | async-done | bytes 524304 | tf_op jit(solution)/shard_map/reduce_scatter | solution.py:235
  1221.2 37.5 %reduce-scatter.19.cloned.1.call-done = bf16[1,4,512,128]{3,2,1,0:T(8,128)(2,1)} async-done(((bf16[4,4,512,128]{3,2,1,0:T(8,128)(2,1)}), bf16[1,4,512,128]{3,2,1,0:T(8,128)(2,1)}) %reduce-scatter.19.cloned.1.call-update) | async-done | bytes 524304 | tf_op jit(solution)/shard_map/reduce_scatter | solution.py:235
  (719 shorter events, 594.8 us)
Async XLA Ops:
  20.2 56.8 %all-gather.22.cloned.1.call-start = ((), (), s32[]{:S(2)}) async-start(), calls=%async_computation.35 | async-start | bytes 1310720 | tf_op jit(solution)/shard_map/all_gather | solution.py:222
  29.4 110.8 %all-gather.34.cloned.1.call-start = ((), (), s32[]{:S(2)}) async-start(), calls=%async_computation.41 | async-start | bytes 1310720 | tf_op jit(solution)/shard_map/all_gather | solution.py:222
  38.5 139.2 %all-gather.30.cloned.1.call-start = ((), (), s32[]{:S(2)}) async-start(), calls=%async_computation.39 | async-start | bytes 2621440 | tf_op jit(solution)/shard_map/all_gather | solution.py:222
  49.3 167.6 %all-gather.28.cloned.1.call-start = ((), (), s32[]{:S(2)}) async-start(), calls=%async_computation.38 | async-start | bytes 3145728 | tf_op jit(solution)/shard_map/all_gather | solution.py:222
  49.9 175.3 %all-gather.24.cloned.1.call-start = ((), (), s32[]{:S(2)}) async-start(), calls=%async_computation.36 | async-start | bytes 3145728 | tf_op jit(solution)/shard_map/all_gather | solution.py:222
  77.1 173.2 %all-gather.38.cloned.1.call-start = ((), (), s32[]{:S(2)}) async-start(), calls=%async_computation.43 | async-start | bytes 2621440 | tf_op jit(solution)/shard_map/all_gather | solution.py:222
  89.4 171.8 %all-gather.36.cloned.1.call-start = ((), (), s32[]{:S(2)}) async-start(), calls=%async_computation.42 | async-start | bytes 3145728 | tf_op jit(solution)/shard_map/all_gather | solution.py:222
  89.5 50.8 %collective-permute-start.7 = (s32[2,1152]{1,0:T(2,128)S(1)}, s32[2,1152]{1,0:T(2,128)S(1)}, u32[]{:S(2)}, u32[]{:S(2)}) collective-permute-start(s32[2,1152]{1,0:T(2,128)S(1)} %pad_add_fusion.1), channel_id=1, source_target_pairs={{0,16},{16,0},{1,17},{17,1},{2,18},{18,2},{3,19},{19,3},{4,20},{20... | collective-permute-start | bytes 27656 | tf_op jit(solution)/shard_map/ppermute | solution.py:290
  90.5 51.7 %collective-permute-start.3 = (s32[2,1152]{1,0:T(2,128)S(1)}, s32[2,1152]{1,0:T(2,128)S(1)}, u32[]{:S(2)}, u32[]{:S(2)}) collective-permute-start(s32[2,1152]{1,0:T(2,128)S(1)} %pad_add_fusion), channel_id=1, source_target_pairs={{0,16},{16,0},{1,17},{17,1},{2,18},{18,2},{3,19},{19,3},{4,20},{20... | collective-permute-start | bytes 27656 | tf_op jit(solution)/shard_map/ppermute | solution.py:290
  91.7 107.9 %collective-permute-start.4 = (bf16[64,1024]{1,0:T(8,128)(2,1)S(1)}, bf16[64,1024]{1,0:T(8,128)(2,1)S(1)}, u32[]{:S(2)}, u32[]{:S(2)}) collective-permute-start(bf16[64,1024]{1,0:T(8,128)(2,1)S(1)} %get-tuple-element.168), channel_id=1, source_target_pairs={{0,0},{1,1},{2,16},{3,17},{4,4},{5,5},{6,20},{7,21},{8,8},{9,9},{1... | collective-permute-start | bytes 393224 | tf_op jit(solution)/shard_map/ppermute | solution.py:269
  92.4 107.2 %collective-permute-start.5 = (bf16[64,1024]{1,0:T(8,128)(2,1)S(1)}, bf16[64,1024]{1,0:T(8,128)(2,1)S(1)}, u32[]{:S(2)}, u32[]{:S(2)}) collective-permute-start(bf16[64,1024]{1,0:T(8,128)(2,1)S(1)} %get-tuple-element.169), channel_id=1, source_target_pairs={{0,1},{1,0},{2,17},{3,16},{4,5},{5,4},{6,21},{7,20},{8,9},{9,8},{1... | collective-permute-start | bytes 393224 | tf_op jit(solution)/shard_map/ppermute | solution.py:269
  93.8 87.8 %collective-permute-start = (bf16[64,1024]{1,0:T(8,128)(2,1)S(1)}, bf16[64,1024]{1,0:T(8,128)(2,1)S(1)}, u32[]{:S(2)}, u32[]{:S(2)}) collective-permute-start(bf16[64,1024]{1,0:T(8,128)(2,1)S(1)} %get-tuple-element.172), channel_id=1, source_target_pairs={{0,0},{1,1},{2,16},{3,17},{4,4},{5,5},{6,20},{7,21},{8,8},{9,9},{1... | collective-permute-start | bytes 393224 | tf_op jit(solution)/shard_map/ppermute | solution.py:269
  140.2 234.2 %all-gather.32.cloned.1.call-start = ((), (), s32[]{:S(2)}) async-start(), calls=%async_computation.40 | async-start | bytes 6291456 | tf_op jit(solution)/shard_map/all_gather | solution.py:222
  142.3 100.8 %collective-permute-start.11 = (bf16[64,1024]{1,0:T(8,128)(2,1)}, bf16[64,1024]{1,0:T(8,128)(2,1)S(1)}, u32[]{:S(2)}, u32[]{:S(2)}) collective-permute-start(bf16[64,1024]{1,0:T(8,128)(2,1)} %get-tuple-element.160), channel_id=1, source_target_pairs={{0,0},{1,1},{2,16},{3,17},{4,4},{5,5},{6,20},{7,21},{8,8},{9,9},{1... | collective-permute-start | bytes 393224 | tf_op jit(solution)/shard_map/ppermute | solution.py:269
  177.8 266.2 %all-gather.40.cloned.1.call-start = ((), (), s32[]{:S(2)}) async-start(), calls=%async_computation.44 | async-start | bytes 6291456 | tf_op jit(solution)/shard_map/all_gather | solution.py:222
  181.6 61.5 %collective-permute-start.12 = (bf16[64,1024]{1,0:T(8,128)(2,1)S(1)}, bf16[64,1024]{1,0:T(8,128)(2,1)}, u32[]{:S(2)}, u32[]{:S(2)}) collective-permute-start(bf16[64,1024]{1,0:T(8,128)(2,1)S(1)} %get-tuple-element.161), channel_id=1, source_target_pairs={{0,1},{1,0},{2,17},{3,16},{4,5},{5,4},{6,21},{7,20},{8,9},{9,8},{1... | collective-permute-start | bytes 393224 | tf_op jit(solution)/shard_map/ppermute | solution.py:269
  250.3 773.9 %reduce-scatter.21.cloned.1.call-start = ((), (), s32[]{:S(2)}) async-start(), calls=%async_computation.27 | async-start | bytes 196608 | tf_op jit(solution)/shard_map/reduce_scatter | solution.py:234
  754.5 119.2 %collective-permute-start.20 = (bf16[512,256]{0,1:T(8,128)(2,1)}, bf16[512,256]{0,1:T(8,128)(2,1)}, u32[]{:S(2)}, u32[]{:S(2)}) collective-permute-start(bf16[512,256]{0,1:T(8,128)(2,1)} %bitcast.153), channel_id=1, source_target_pairs={{0,4},{4,0},{1,5},{5,1},{2,6},{6,2},{3,7},{7,3},{8,12},{12,8},{9,1... | collective-permute-start | bytes 786440 | tf_op jit(solution)/shard_map/ppermute | solution.py:138
  755.5 141.4 %collective-permute-start.19 = (bf16[512,256]{0,1:T(8,128)(2,1)}, bf16[512,256]{0,1:T(8,128)(2,1)}, u32[]{:S(2)}, u32[]{:S(2)}) collective-permute-start(bf16[512,256]{0,1:T(8,128)(2,1)} %bitcast.150), channel_id=1, source_target_pairs={{0,4},{4,0},{1,5},{5,1},{2,6},{6,2},{3,7},{7,3},{8,12},{12,8},{9,1... | collective-permute-start | bytes 786440 | tf_op jit(solution)/shard_map/ppermute | solution.py:138
  854.5 65.6 %collective-permute-start.16 = (bf16[512,256]{0,1:T(8,128)(2,1)}, bf16[512,256]{0,1:T(8,128)(2,1)}, u32[]{:S(2)}, u32[]{:S(2)}) collective-permute-start(bf16[512,256]{0,1:T(8,128)(2,1)} %bitcast.137), channel_id=1, source_target_pairs={{0,4},{4,0},{1,5},{5,1},{2,6},{6,2},{3,7},{7,3},{8,12},{12,8},{9,1... | collective-permute-start | bytes 786440 | tf_op jit(solution)/shard_map/ppermute | solution.py:138
  873.2 48.0 %collective-permute-start.15 = (bf16[512,256]{0,1:T(8,128)(2,1)}, bf16[512,256]{0,1:T(8,128)(2,1)}, u32[]{:S(2)}, u32[]{:S(2)}) collective-permute-start(bf16[512,256]{0,1:T(8,128)(2,1)} %bitcast.134), channel_id=1, source_target_pairs={{0,4},{4,0},{1,5},{5,1},{2,6},{6,2},{3,7},{7,3},{8,12},{12,8},{9,1... | collective-permute-start | bytes 786440 | tf_op jit(solution)/shard_map/ppermute | solution.py:138
  943.7 81.1 %reduce-scatter.29.cloned.1.call-start = ((), (), s32[]{:S(2)}) async-start(), calls=%async_computation.31 | async-start | bytes 3145728 | tf_op jit(solution)/shard_map/reduce_scatter | solution.py:234
  951.5 73.9 %reduce-scatter.25.cloned.1.call-start = ((), (), s32[]{:S(2)}) async-start(), calls=%async_computation.29 | async-start | bytes 3145728 | tf_op jit(solution)/shard_map/reduce_scatter | solution.py:234
  962.1 64.0 %reduce-scatter.13.cloned.1.call-start = ((), (), s32[]{:S(2)}) async-start(), calls=%async_computation.23 | async-start | bytes 3145728 | tf_op jit(solution)/shard_map/reduce_scatter | solution.py:234
  972.8 53.9 %reduce-scatter.33.cloned.1.call-start = ((), (), s32[]{:S(2)}) async-start(), calls=%async_computation.33 | async-start | bytes 6291456 | tf_op jit(solution)/shard_map/reduce_scatter | solution.py:234
  1024.1 53.9 %reduce-scatter.23.cloned.1.call-start = ((), (), s32[]{:S(2)}) async-start(), calls=%async_computation.28 | async-start | bytes 81920 | tf_op jit(solution)/shard_map/reduce_scatter | solution.py:235
  1024.7 86.2 %reduce-scatter.31.cloned.1.call-start = ((), (), s32[]{:S(2)}) async-start(), calls=%async_computation.32 | async-start | bytes 1310720 | tf_op jit(solution)/shard_map/reduce_scatter | solution.py:235
  1025.3 115.0 %reduce-scatter.27.cloned.1.call-start = ((), (), s32[]{:S(2)}) async-start(), calls=%async_computation.30 | async-start | bytes 1310720 | tf_op jit(solution)/shard_map/reduce_scatter | solution.py:235
  1026.0 142.2 %reduce-scatter.15.cloned.1.call-start = ((), (), s32[]{:S(2)}) async-start(), calls=%async_computation.24 | async-start | bytes 1310720 | tf_op jit(solution)/shard_map/reduce_scatter | solution.py:235
  1026.6 186.6 %reduce-scatter.35.cloned.1.call-start = ((), (), s32[]{:S(2)}) async-start(), calls=%async_computation.34 | async-start | bytes 2621440 | tf_op jit(solution)/shard_map/reduce_scatter | solution.py:235
  1027.4 231.3 %reduce-scatter.19.cloned.1.call-start = ((), (), s32[]{:S(2)}) async-start(), calls=%async_computation.26 | async-start | bytes 2621440 | tf_op jit(solution)/shard_map/reduce_scatter | solution.py:235
  1213.2 45.5 %all-to-all-start.10 = ((bf16[4,512,128]{2,1,0:T(8,128)(2,1)}), bf16[4,512,128]{2,1,0:T(8,128)(2,1)S(1)}, u32[]{:S(2)}, u32[]{:S(2)}) async-start(bf16[4,512,128]{2,1,0:T(8,128)(2,1)} %bitcast.820), calls=%async_computation.22 | async-start | bytes 1048576 | tf_op jit(solution)/shard_map/all_to_all | solution.py:236
  (170 other events, 3008.5 us)
Sparse Core Ops, SparseCore 0:
  20.3 27.6 all-gather.25
  49.6 27.4 all-gather.21
  78.6 41.6 all-gather.33
  121.7 56.0 all-gather.29
  179.2 9.1 all-gather.27
  189.8 11.7 all-gather.23
  203.1 47.1 all-gather.37
  251.8 9.2 all-gather.35
  262.7 14.8 all-gather.31
  279.0 14.8 all-gather.39
  943.8 7.5 reduce-scatter.20
  953.5 10.7 reduce-scatter.28
  966.6 10.7 reduce-scatter.24
  979.5 10.7 reduce-scatter.12
  998.8 11.7 reduce-scatter.32
  1024.2 12.0 reduce-scatter.16
  1038.5 39.5 reduce-scatter.22
  1080.2 30.7 reduce-scatter.30
  1113.4 26.8 reduce-scatter.26
  1142.4 25.7 reduce-scatter.14
  1170.6 42.4 reduce-scatter.34
  1215.5 43.1 reduce-scatter.18

commit v2 on v1

v2 whole, which is shorter than its diff:
```python
import jax
import jax.numpy as jnp
from jax import lax
from jax.experimental import pallas as pl
from jax.experimental.pallas import tpu as pltpu
from jax.sharding import Mesh, PartitionSpec as P

HEAD_DIM = 64
EPSILON = 1e-05
MASKED = -1000000000.0
AXES = ("hi", "k", "y", "c", "mp")
MESH_ID = pl.DeviceIdType.MESH
F32 = jnp.float32
BF16 = jnp.bfloat16


class Call:
    def __init__(self):
        self.arrays, self.specs = [], []
        self.shapes, self.scratch = [], []

    def take(self, array, space=pltpu.VMEM):
        for i, known in enumerate(self.arrays):
            if known is array:
                return ("in", i)
        self.arrays.append(array)
        self.specs.append(pl.BlockSpec(memory_space=space))
        return ("in", len(self.arrays) - 1)

    def give(self, shape, dtype):
        self.shapes.append(jax.ShapeDtypeStruct(shape, dtype))
        return ("out", len(self.shapes) - 1)

    def hold(self, shape, dtype):
        self.scratch.append(pltpu.VMEM(shape, dtype))
        return ("tmp", len(self.scratch) - 1)

    def sems(self, count):
        self.scratch.append(pltpu.SemaphoreType.DMA((count,)))
        return ("tmp", len(self.scratch) - 1)

    def run(self, body, name, collective=None, flops=0):
        ins, outs = len(self.arrays), len(self.shapes)

        def kernel(*refs):
            parts = {"in": refs[:ins], "out": refs[ins : ins + outs], "tmp": refs[ins + outs :]}
            body(lambda handle: parts[handle[0]][handle[1]])

        return pl.pallas_call(
            kernel,
            out_shape=tuple(self.shapes),
            in_specs=self.specs,
            out_specs=tuple(pl.BlockSpec(memory_space=pltpu.VMEM) for _ in self.shapes),
            scratch_shapes=self.scratch,
            compiler_params=pltpu.CompilerParams(
                collective_id=collective,
                has_side_effects=collective is not None,
                vmem_limit_bytes=48 << 20,
            ),
            cost_estimate=pl.CostEstimate(flops=flops, bytes_accessed=0, transcendentals=0),
            name=name,
        )(*self.arrays)


MICROSECOND = 1_000_000_000


def nt(left, right):
    return lax.dot_general(left, right, (((1,), (1,)), ((), ())), preferred_element_type=F32)


def nn(left, right):
    return lax.dot_general(left, right, (((1,), (0,)), ((), ())), preferred_element_type=F32)


def tn(left, right):
    return lax.dot_general(left, right, (((0,), (0,)), ((), ())), preferred_element_type=F32)


def unit_of(stream):
    average = jnp.mean(stream, -1, keepdims=True)
    centred = stream - average
    scale = lax.rsqrt(jnp.mean(centred * centred, -1, keepdims=True) + EPSILON)
    return centred * scale, scale


def norm_back(stream, gain, upstream):
    unit, scale = unit_of(stream)
    inner = upstream * gain
    grad = scale * (
        inner - jnp.mean(inner, -1, keepdims=True) - unit * jnp.mean(inner * unit, -1, keepdims=True)
    )
    shares = jnp.concatenate(
        [jnp.sum(upstream * unit, 0, keepdims=True), jnp.sum(upstream, 0, keepdims=True)], 0
    )
    return grad, shares


def gelu_pair(act):
    bell = 0.5 + 0.5 * lax.erf(act * 0.7071067811865476)
    slope = bell + act * (jnp.exp(act * act * -0.5) * 0.3989422804014327)
    return act * bell, slope


def place():
    hi, k, y, c, z = (lax.axis_index(name) for name in AXES)
    return {
        "x": (1 - hi, k, y, c, z),
        "y": (hi, k, 1 - y, c, z),
        "d": (1 - hi, k, 1 - y, c, z),
        "core": (hi, k, y, 1 - c, z),
        "mesh": (hi, k, y, c, z),
        "own_row": y * 2 + hi,
        "x_row": y * 2 + 1 - hi,
        "y_row": (1 - y) * 2 + hi,
        "d_row": (1 - y) * 2 + 1 - hi,
    }


def greet(partners):
    barrier = pltpu.get_barrier_semaphore()
    for partner in partners:
        pl.semaphore_signal(barrier, inc=1, device_id=partner, device_id_type=MESH_ID)
    pl.semaphore_wait(barrier, len(partners))


class Weight:
    def __init__(self, call, packed, first, count):
        self.source = call.take(packed, pl.ANY)
        self.room = call.hold((4, count, 1024), BF16)
        self.sem = call.sems(1)
        self.first, self.count = first, count

    def start(self, get):
        source, room, sem = get(self.source), get(self.room), get(self.sem)
        for q in range(4):
            for c in range(2):
                pltpu.make_async_copy(
                    source.at[c, :, q, pl.ds(self.first, self.count), :],
                    room.at[:, :, pl.ds((q * 2 + c) * 128, 128)],
                    sem.at[0],
                ).start()

    def wait(self, get):
        room = get(self.room)
        pltpu.make_async_copy(room, room, get(self.sem).at[0]).wait()

    def matrix(self, get, first, count):
        return get(self.room)[:, first : first + count, :].reshape(4 * count, 1024)


class Job:
    def __init__(self, call, left, mid, right):
        self.left, self.mid, self.right = left, mid, right
        if left is not None:
            self.rows_in = call.take(left[0])
            self.out_first = call.hold((2, 128, 1024), BF16)
            self.out_edge = call.hold((2, 64, 1024), BF16)
            self.out_late = call.hold((2, 64, 1024), BF16)
            self.keep = call.hold((2, 64, 1024), F32)
            self.own = call.hold((128, 1024), F32)
            self.landed = call.hold((6, 64, 1024), BF16)
            self.sum_send, self.sum_recv = call.sems(6), call.sems(6)
        self.gathered = None
        if right is not None:
            self.gathered = call.give((4, 128, 1024), BF16)
            self.row_send, self.row_recv = call.sems(6), call.sems(6)

    def part(self, get, row, half=None):
        unused, weight, picks = self.left
        total, column = None, 0
        for first, count in picks:
            width = 4 * count
            left = get(self.rows_in)[row, :, column : column + width]
            term = nn(left, weight.matrix(get, first, count))
            total = term if total is None else total + term
            column += width
        return total

    def send(self, get, i, source, target, partner):
        copy = pltpu.make_async_remote_copy(
            src_ref=source,
            dst_ref=target,
            send_sem=get(self.sum_send).at[i],
            recv_sem=get(self.sum_recv).at[i],
            device_id=partner,
            device_id_type=MESH_ID,
        )
        copy.start()
        return copy

    def sum_start(self, get, at):
        first, edge, landed = get(self.out_first), get(self.out_edge), get(self.landed)
        keep = get(self.keep)
        self.copies = [None] * 6
        first[0] = self.part(get, at["d_row"]).astype(BF16)
        self.copies[0] = self.send(
            get, 0, first.at[0, pl.ds(0, 64)], landed.at[0], at["x"]
        )
        self.copies[1] = self.send(
            get, 1, first.at[0, pl.ds(64, 64)], landed.at[1], at["y"]
        )
        part = self.part(get, at["x_row"])
        edge[0] = part[:64].astype(BF16)
        keep[0] = part[64:]
        self.copies[2] = self.send(get, 2, edge.at[0], landed.at[2], at["x"])
        part = self.part(get, at["y_row"])
        edge[1] = part[64:].astype(BF16)
        keep[1] = part[:64]
        self.copies[3] = self.send(get, 3, edge.at[1], landed.at[3], at["y"])
        get(self.own)[...] = self.part(get, at["own_row"])

    def sum_forward(self, get, at):
        late, landed, keep = get(self.out_late), get(self.landed), get(self.keep)
        self.copies[0].wait_recv()
        late[1] = (keep[1] + landed[0].astype(F32)).astype(BF16)
        self.copies[4] = self.send(get, 4, late.at[1], landed.at[4], at["y"])
        self.copies[1].wait_recv()
        late[0] = (keep[0] + landed[1].astype(F32)).astype(BF16)
        self.copies[5] = self.send(get, 5, late.at[0], landed.at[5], at["x"])

    def sum_end(self, get):
        landed, own = get(self.landed), get(self.own)
        for i in (2, 3, 4, 5):
            self.copies[i].wait_recv()
        upper = own[:64] + landed[2].astype(F32) + landed[4].astype(F32)
        lower = own[64:] + landed[5].astype(F32) + landed[3].astype(F32)
        return jnp.concatenate([upper, lower], 0)

    def row_copy(self, get, i, row, half, partner):
        block = get(self.gathered).at[row, pl.ds(half * 64, 64)]
        copy = pltpu.make_async_remote_copy(
            src_ref=block,
            dst_ref=block,
            send_sem=get(self.row_send).at[i],
            recv_sem=get(self.row_recv).at[i],
            device_id=partner,
            device_id_type=MESH_ID,
        )
        copy.start()
        return copy

    def rows_start(self, get, at, normed):
        get(self.gathered)[at["own_row"]] = normed
        self.moves = [
            self.row_copy(get, 0, at["own_row"], 0, at["y"]),
            self.row_copy(get, 1, at["own_row"], 1, at["x"]),
            self.row_copy(get, 2, at["own_row"], 1, at["y"]),
            self.row_copy(get, 3, at["own_row"], 0, at["x"]),
        ]

    def rows_forward(self, get, at):
        self.moves[0].wait_recv()
        self.moves.append(self.row_copy(get, 4, at["y_row"], 0, at["x"]))
        self.moves[1].wait_recv()
        self.moves.append(self.row_copy(get, 5, at["x_row"], 1, at["y"]))

    def product(self, get, at, row):
        weight, picks, store = self.right
        rows = get(self.gathered)[row]
        column = 0
        for first, count in picks:
            store(get, at, row, column, nt(rows, weight.matrix(get, first, count)))
            column += 4 * count

    def drain(self):
        if self.left is not None:
            for copy in self.copies:
                copy.wait_send()
        if self.right is not None:
            for copy in self.moves:
                copy.wait_send()


def run_stage(call, jobs, weights, name, collective, finish=None, flops=0, core=False, more=None):
    def body(get):
        at = place()
        for weight in weights:
            weight.start(get)
        greet(
            [at["x"], at["y"]]
            + ([at["core"]] if core else [])
            + ([at["d"]] if more is not None else [])
        )
        lefts = [job for job in jobs if job.left is not None]
        rights = [job for job in jobs if job.right is not None and job.right[0] is not None]
        waited = []

        def ready(weight):
            if weight not in waited:
                weight.wait(get)
                waited.append(weight)

        for job in lefts:
            ready(job.left[1])
            job.sum_start(get, at)
        for job in lefts:
            job.sum_forward(get, at)
        for job in jobs:
            normed = job.mid(get, job.sum_end(get) if job.left is not None else None)
            if job.right is not None:
                job.rows_start(get, at, normed)
        if more is not None:
            more.start(get, at)
        for weight in weights:
            ready(weight)
        for job in rights:
            job.product(get, at, at["own_row"])
        for job in jobs:
            if job.right is not None:
                job.rows_forward(get, at)
        for job in jobs:
            if job.right is not None:
                job.moves[3].wait_recv()
                if job in rights:
                    job.product(get, at, at["x_row"])
                job.moves[2].wait_recv()
                if job in rights:
                    job.product(get, at, at["y_row"])
        for job in jobs:
            if job.right is not None:
                job.moves[4].wait_recv()
                job.moves[5].wait_recv()
                if job in rights:
                    job.product(get, at, at["d_row"])
        for job in jobs:
            job.drain()
        if finish is not None:
            finish(get)
        if more is not None:
            more.finish()

    return call.run(body, name, collective, flops)


class Plain:
    def __init__(self, call, width):
        self.out = call.give((4, 128, width), BF16)

    def store(self, get, at, row, column, value):
        get(self.out)[row, :, column : column + value.shape[1]] = value.astype(BF16)


class Shared:
    def __init__(self, call, width, skip=0):
        self.out = call.give((2, 4, 128, width), BF16)
        self.send_sem, self.recv_sem = call.sems(4), call.sems(4)
        self.width, self.skip, self.copies, self.blocks = width, skip, [], 0

    def store(self, get, at, row, column, value):
        out = get(self.out)
        column = column - self.skip
        out[0, row, :, column : column + value.shape[1]] = value.astype(BF16)
        if column + value.shape[1] == self.width:
            i = len(self.copies)
            copy = pltpu.make_async_remote_copy(
                src_ref=out.at[0, row],
                dst_ref=out.at[1, row],
                send_sem=get(self.send_sem).at[i],
                recv_sem=get(self.recv_sem).at[i],
                device_id=at["core"],
                device_id_type=MESH_ID,
            )
            copy.start()
            self.copies.append(copy)

    def finish(self, get):
        for copy in self.copies:
            copy.wait()


def query_and_shared(call, width):
    query, shared = Plain(call, width), Shared(call, 2 * width, skip=width)

    def store(get, at, row, column, value):
        if column < width:
            query.store(get, at, row, column, value)
        else:
            shared.store(get, at, row, column, value)

    return store, shared.finish


def lanes_of(head, rows):
    lane = lax.broadcasted_iota(jnp.int32, (rows, 128), 1)
    return lane // HEAD_DIM == head


def allowed_bias(facts_ref, keys_ref, causal):
    key = keys_ref[...]
    query = facts_ref[...]
    allowed = (key[:, 0:1] == query[0:1, :]) & (key[:, 2:3] > 0)
    if causal:
        allowed = allowed & (key[:, 1:2] <= query[1:2, :])
    return jnp.where(allowed, 0.0, MASKED)


def attend_kernel(causal, q_ref, kv_ref, facts_ref, keys_ref, mixed_ref, total_ref, bias):
    bias[...] = allowed_bias(facts_ref, keys_ref, causal)
    rows = q_ref.shape[0]
    half = rows // 2

    def pair_step(pair, carry):
        lanes = pl.ds(pl.multiple_of(pair * 128, 128), 128)
        value_lanes = pl.ds(pl.multiple_of(256 + pair * 128, 128), 128)
        keys, values = kv_ref[:, lanes], kv_ref[:, value_lanes]
        for block in range(2):
            queries = q_ref[pl.ds(block * half, half), lanes]
            mixed = []
            for head in range(2):
                picked = jnp.where(lanes_of(head, half), queries * 0.125, 0.0).astype(BF16)
                scores = nt(keys, picked) + bias[:, block * half : (block + 1) * half]
                top = jnp.max(scores, 0, keepdims=True)
                raised = jnp.exp(scores - top)
                total = jnp.sum(raised, 0, keepdims=True)
                probs = (raised * (1.0 / total)).astype(BF16)
                mixed.append(tn(values, probs)[head * HEAD_DIM : (head + 1) * HEAD_DIM])
                total_ref[pl.ds(pair * 2 + head, 1), block * half : (block + 1) * half] = (
                    top + jnp.log(total)
                )
            mixed = jnp.concatenate(mixed, 0).T
            mixed_ref[pl.ds(block * half, half), lanes] = mixed.astype(BF16)
        return carry

    lax.fori_loop(0, 2, pair_step, 0)


def attend(queries, key_value, facts, keys, causal):
    rows, width = 512, queries.shape[-1]

    def kernel(*refs):
        attend_kernel(causal, *refs)

    mixed, total = pl.pallas_call(
        kernel,
        out_shape=(
            jax.ShapeDtypeStruct((rows, width), BF16),
            jax.ShapeDtypeStruct((8, rows), F32),
        ),
        in_specs=[pl.BlockSpec(memory_space=pltpu.VMEM)] * 4,
        out_specs=(pl.BlockSpec(memory_space=pltpu.VMEM),) * 2,
        scratch_shapes=[pltpu.VMEM((1024, rows), F32)],
        compiler_params=pltpu.CompilerParams(vmem_limit_bytes=48 << 20),
        cost_estimate=pl.CostEstimate(flops=8 * MICROSECOND, bytes_accessed=0, transcendentals=0),
        name="attend",
    )(queries.reshape(rows, width), key_value.reshape(1024, 2 * width), facts, keys)
    return mixed.reshape(4, 128, width), total


def attend_back(
    queries, key_value, grad_mixed, total, facts, keys, causal, collective, done=()
):
    rows, width = 512, queries.shape[-1]
    half = rows // 2
    call = Call()
    q_in, kv_in = call.take(queries.reshape(rows, width)), call.take(key_value.reshape(1024, 2 * width))
    grad_in, total_in = call.take(grad_mixed.reshape(rows, width)), call.take(total)
    facts_in, keys_in = call.take(facts), call.take(keys)
    for array in done:
        call.take(array, pl.ANY)
    grad_out = call.give((rows, 3 * width), BF16)
    bias = call.hold((1024, rows), F32)
    gathered = call.hold((1024, 4 * 128), F32)
    outgoing, landed = call.hold((2, 512, 256), BF16), call.hold((2, 512, 256), BF16)
    send_sem, recv_sem = call.sems(2), call.sems(2)

    def body(get):
        at = place()
        q_ref, kv_ref, grad_ref, total_ref = get(q_in), get(kv_in), get(grad_in), get(total_in)
        out, mask, sums = get(grad_out), get(bias), get(gathered)
        away, here = get(outgoing), get(landed)
        mask[...] = allowed_bias(get(facts_in), get(keys_in), causal)
        greet([at["core"]])
        copies = []
        for pair in range(2):
            lanes = slice(pair * 128, pair * 128 + 128)
            keys_pair = kv_ref[:, lanes]
            values_pair = kv_ref[:, 256 + pair * 128 : 256 + pair * 128 + 128]
            key_sum = slice(pair * 256, pair * 256 + 128)
            value_sum = slice(pair * 256 + 128, pair * 256 + 256)
            for block in range(2):
                span = slice(block * half, (block + 1) * half)
                q_block, g_block = q_ref[span, lanes], grad_ref[span, lanes]
                grad_query = []
                for head in range(2):
                    inside = lanes_of(head, half)
                    picked = jnp.where(inside, q_block * 1.0, 0.0).astype(BF16)
                    grads = jnp.where(inside, g_block * 1.0, 0.0).astype(BF16)
                    scores = nt(keys_pair, picked) * 0.125 + mask[:, span]
                    probs = jnp.exp(scores - total_ref[pair * 2 + head : pair * 2 + head + 1, span])
                    weighted = probs * nt(values_pair, grads)
                    inner = jnp.sum(weighted, 0, keepdims=True)
                    grad_raw = ((weighted - probs * inner) * 0.125).astype(BF16)
                    value_term = nn(probs.astype(BF16), grads)
                    key_term = nn(grad_raw, picked)
                    if block == 0 and head == 0:
                        sums[:, key_sum] = key_term
                        sums[:, value_sum] = value_term
                    else:
                        sums[:, key_sum] += key_term
                        sums[:, value_sum] += value_term
                    grad_query.append(tn(keys_pair, grad_raw)[head * HEAD_DIM : (head + 1) * HEAD_DIM])
                out[span, lanes] = jnp.concatenate(grad_query, 0).T.astype(BF16)
            away[pair] = sums[512:, pair * 256 : pair * 256 + 256].astype(BF16)
            copy = pltpu.make_async_remote_copy(
                src_ref=away.at[pair],
                dst_ref=here.at[pair],
                send_sem=get(send_sem).at[pair],
                recv_sem=get(recv_sem).at[pair],
                device_id=at["core"],
                device_id_type=MESH_ID,
            )
            copy.start()
            copies.append(copy)
        for pair in range(2):
            copies[pair].wait()
            both = sums[:512, pair * 256 : pair * 256 + 256] + here[pair].astype(F32)
            out[:, width + pair * 128 : width + pair * 128 + 128] = both[:, :128].astype(BF16)
            out[:, 2 * width + pair * 128 : 2 * width + pair * 128 + 128] = both[:, 128:].astype(BF16)

    (grads,) = call.run(body, "attend_back", collective, 16 * MICROSECOND)
    return grads.reshape(4, 128, 3 * width)


def weight_shares(groups, collective):
    call = Call()
    plans = []
    for pairs in groups:
        count = 256 // len(pairs)
        handles = [
            (call.take(left.reshape(512, -1)), column, call.take(right.reshape(512, 1024)))
            for left, column, right in pairs
        ]
        made, landed = call.hold((2, 4, 4, 256, 128), BF16), call.hold((4, 4, 256, 128), BF16)
        send_sem, recv_sem = call.sems(4), call.sems(4)
        shares = call.give((4, 4, 256, 128), BF16)
        plans.append((count, handles, made, landed, send_sem, recv_sem, shares))

    def body(get):
        at = place()
        core = lax.axis_index("c")
        greet([at["core"]])
        copies = []

        def send(plan, i, part):
            made, landed, send_sem, recv_sem = (get(handle) for handle in plan[2:6])
            copy = pltpu.make_async_remote_copy(
                src_ref=made.at[(1 - core,) + part],
                dst_ref=landed.at[part],
                send_sem=send_sem.at[i],
                recv_sem=recv_sem.at[i],
                device_id=at["core"],
                device_id_type=MESH_ID,
            )
            copy.start()
            copies.append((plan, part, copy))

        for plan in plans:
            count, handles, made = plan[0], plan[1], get(plan[2])
            for m, (left, column, right) in enumerate(handles):
                left, right = get(left), get(right)
                for first in range(0, 4 * count, 256):
                    product = tn(left[:, column + first : column + first + 256], right[...])
                    for inner in range(0, 256, count):
                        z = (first + inner) // count
                        for d in range(8):
                            made[d % 2, z, d // 2, m * count : (m + 1) * count, :] = product[
                                inner : inner + count, d * 128 : d * 128 + 128
                            ].astype(BF16)
                    if count == 256:
                        send(plan, z, (z,))
                if count < 256:
                    every = slice(None)
                    send(plan, m, (every, every, pl.ds(m * count, count)))
        for plan, part, copy in copies:
            copy.wait()
            made, landed, shares = get(plan[2]), get(plan[3]), get(plan[6])
            own = made[(core,) + part].astype(F32)
            shares[part] = (own + landed[part].astype(F32)).astype(BF16)

    return call.run(body, "weight_shares", collective, 4 * len(groups) * MICROSECOND)


class Swap:
    def __init__(self, call, packs):
        self.packs = [call.take(pack) for pack in packs]
        self.outs = [call.give(pack.shape, pack.dtype) for pack in packs]
        self.send_sem, self.recv_sem = call.sems(3 * len(packs)), call.sems(3 * len(packs))

    def start(self, get, at):
        hi, k, y, c, z = at["mesh"]
        own = hi * 2 + y
        self.copies = []
        for pack, out in zip(self.packs, self.outs, strict=True):
            pack, out = get(pack), get(out)
            for name, q in (
                ("d", (1 - hi) * 2 + 1 - y),
                ("x", (1 - hi) * 2 + y),
                ("y", hi * 2 + 1 - y),
            ):
                i = len(self.copies)
                copy = pltpu.make_async_remote_copy(
                    src_ref=pack.at[q],
                    dst_ref=out.at[own],
                    send_sem=get(self.send_sem).at[i],
                    recv_sem=get(self.recv_sem).at[i],
                    device_id=at[name],
                    device_id_type=MESH_ID,
                )
                copy.start()
                self.copies.append(copy)
            out[own] = pack[own]

    def finish(self):
        for copy in self.copies:
            copy.wait()


class Slots:
    def __init__(self, call, arrays, inward):
        self.inward = inward
        self.arrays = [call.take(array) for array in arrays]
        shape = (128, 1024) if inward else (2, 64, 1024)
        self.outs = [call.give(shape, array.dtype) for array in arrays]
        self.send_sem, self.recv_sem = call.sems(2 * len(arrays)), call.sems(2 * len(arrays))

    def ends(self, get, at, j, step):
        z = at["mesh"][4]
        odd = lax.rem(z, 2)
        other = odd if step == 0 else 1 - odd
        array, out = get(self.arrays[j]), get(self.outs[j])
        if self.inward:
            return array.at[other], out.at[pl.ds(pl.multiple_of(odd * 64, 64), 64)]
        return array.at[pl.ds(pl.multiple_of(other * 64, 64), 64)], out.at[odd]

    def copy(self, get, at, j, step):
        hi, k, y, c, z = at["mesh"]
        odd = lax.rem(z, 2)
        source, target = self.ends(get, at, j, step)
        return pltpu.make_async_remote_copy(
            src_ref=source,
            dst_ref=target,
            send_sem=get(self.send_sem).at[2 * j + step],
            recv_sem=get(self.recv_sem).at[2 * j + step],
            device_id=(lax.div(z, 2), k, y, c, 2 * hi + (odd if step == 0 else 1 - odd)),
            device_id_type=MESH_ID,
        )

    def start(self, get, at):
        hi, z = at["mesh"][0], at["mesh"][4]
        stays = lax.div(z, 2) == hi
        for j in range(len(self.arrays)):
            self.copy(get, at, j, 1).start()

        @pl.when(jnp.logical_not(stays))
        def _():
            for j in range(len(self.arrays)):
                self.copy(get, at, j, 0).start()

        @pl.when(stays)
        def _():
            for j in range(len(self.arrays)):
                source, target = self.ends(get, at, j, 0)
                target[...] = source[...]

    def finish(self, get, at):
        hi, z = at["mesh"][0], at["mesh"][4]
        for j in range(len(self.arrays)):
            self.copy(get, at, j, 1).wait()

        @pl.when(lax.div(z, 2) != hi)
        def _():
            for j in range(len(self.arrays)):
                self.copy(get, at, j, 0).wait()


def all_partners(at):
    hi, k, y, c, z = at["mesh"]
    plane = [
        ((hi + i) % 2, k, (y + j) % 2, (c + n) % 2, z)
        for i in range(2)
        for j in range(2)
        for n in range(2)
        if i + j + n > 0
    ]
    ways = [((hi + i) % 2, k, y, c, (z + n) % 4) for i in range(2) for n in range(1, 4)]
    return plane, ways


def meet(at):
    plane, ways = all_partners(at)
    greet(plane + ways)
    return plane


def open_program(rows, vectors, facts, packs):
    call = Call()
    slots, swap = Slots(call, rows, True), Swap(call, packs)
    vec_in, fact_in = call.take(vectors), call.take(facts)
    vec_out, fact_out = call.give((16, 1024), F32), call.give((2,) + facts.shape, facts.dtype)
    landed, whole = call.hold((3, 16, 128), F32), call.hold((16, 128), F32)
    vec_send, vec_recv = call.sems(11), call.sems(11)

    def body(get):
        at = place()
        plane = meet(at)
        hi, k, y, c, z = at["mesh"]
        send, recv = get(vec_send), get(vec_recv)

        def push(i, source, target, partner):
            copy = pltpu.make_async_remote_copy(
                src_ref=source,
                dst_ref=target,
                send_sem=send.at[i],
                recv_sem=recv.at[i],
                device_id=partner,
                device_id_type=MESH_ID,
            )
            copy.start()
            return copy

        first = [
            push(n - 1, get(vec_in), get(landed).at[n - 1], (hi, k, y, c, (z + n) % 4))
            for n in range(1, 4)
        ]
        fact_copy = push(10, get(fact_in), get(fact_out).at[1], at["x"])
        slots.start(get, at)
        swap.start(get, at)
        get(fact_out)[0] = get(fact_in)[...]
        for copy in first:
            copy.wait()
        parts = get(landed)
        get(whole)[...] = get(vec_in)[...] + parts[0] + parts[1] + parts[2]
        block = pl.ds(pl.multiple_of(((hi * 2 + y) * 2 + c) * 128, 128), 128)
        second = [
            push(3 + i, get(whole), get(vec_out).at[:, block], partner)
            for i, partner in enumerate(plane)
        ]
        get(vec_out)[:, block] = get(whole)[...]
        for copy in second:
            copy.wait()
        fact_copy.wait()
        slots.finish(get, at)
        swap.finish()

    outs = call.run(body, "open_program", 13, 12 * MICROSECOND)
    n, m = len(rows), len(packs)
    return outs[:n], outs[n : n + m], outs[n + m], outs[n + m + 1]


def close_program(rows, vectors, packs):
    call = Call()
    slots, swap = Slots(call, rows, False), Swap(call, packs)
    vec_in = call.take(vectors)
    vec_out = call.give((16, 128), F32)
    landed, block_sum = call.hold((7, 16, 128), F32), call.hold((16, 128), F32)
    blocks, along = call.hold((8, 16, 128), F32), call.hold((3, 16, 128), F32)
    vec_send, vec_recv = call.sems(10), call.sems(10)

    def body(get):
        at = place()
        plane = meet(at)
        hi, k, y, c, z = at["mesh"]
        send, recv = get(vec_send), get(vec_recv)
        split = get(blocks)
        for d in range(8):
            split[d] = get(vec_in)[:, d * 128 : d * 128 + 128]

        def push(i, source, target, partner):
            copy = pltpu.make_async_remote_copy(
                src_ref=source,
                dst_ref=target,
                send_sem=send.at[i],
                recv_sem=recv.at[i],
                device_id=partner,
                device_id_type=MESH_ID,
            )
            copy.start()
            return copy

        first = [
            push(
                i,
                split.at[(partner[0] * 2 + partner[2]) * 2 + partner[3]],
                get(landed).at[i],
                partner,
            )
            for i, partner in enumerate(plane)
        ]
        slots.start(get, at)
        swap.start(get, at)
        for copy in first:
            copy.wait()
        total = split[(hi * 2 + y) * 2 + c]
        for i in range(7):
            total = total + get(landed)[i]
        get(block_sum)[...] = total
        second = [
            push(6 + n, get(block_sum), get(along).at[n - 1], (hi, k, y, c, (z + n) % 4))
            for n in range(1, 4)
        ]
        for copy in second:
            copy.wait()
        get(vec_out)[...] = get(block_sum)[...] + get(along)[0] + get(along)[1] + get(along)[2]
        slots.finish(get, at)
        swap.finish()

    outs = call.run(body, "close_program", 14, 16 * MICROSECOND)
    n, m = len(rows), len(packs)
    return outs[:n], outs[n : n + m], outs[n + m]


def swap_packs(packs, collective):
    call = Call()
    swap = Swap(call, packs)

    def body(get):
        at = place()
        greet([at["x"], at["y"], at["d"]])
        swap.start(get, at)
        swap.finish()

    return call.run(body, "swap_packs", collective, 5 * MICROSECOND)


def transposed(qkv):
    return [qkv[i].T for i in range(3)]


def pack_rows(matrices):
    stacked = jnp.stack(matrices)
    count, units, width = stacked.shape
    return jnp.swapaxes(stacked.reshape(count, 4, units // 4, width), 0, 1).reshape(4, -1, width)


def over_slots(shares):
    return lax.psum_scatter(shares, "mp", scatter_dimension=0)


def widen(packed):
    return packed if lax.axis_size("k") == 1 else lax.all_gather(packed, "k", axis=2, tiled=True)


def gather_weights(packed):
    copies = lax.axis_size("k")
    rows, width = packed.shape[1], 128 // copies
    packed = lax.all_gather(packed, ("c", "mp")).reshape(2, 4, 4, rows, 128)
    if copies > 1:
        packed = packed.reshape(2, 4, 2, 2, rows, copies, width)
        packed = packed.transpose(1, 4, 2, 5, 3, 0, 6).reshape(4, rows, 4, 2, 128)
        packed = packed.transpose(3, 0, 2, 1, 4)
    return packed


def by_owner(rights):
    copies = lax.axis_size("k")
    if copies == 1:
        return rights
    shape = rights.shape
    rights = rights.reshape(-1, 2, copies, 2, 2, 128 // copies).transpose(0, 1, 3, 4, 2, 5)
    return rights.reshape(shape)


def narrow(shares):
    shares = shares.astype(F32)
    if lax.axis_size("k") > 1:
        shares = lax.psum_scatter(shares, "k", scatter_dimension=2, tiled=True)
    return shares


def unpack(packed, count):
    parts, rows, width = packed.shape
    unpacked = packed.reshape(parts, count, rows // count, width)
    return jnp.swapaxes(unpacked, 0, 1).reshape(count, parts * rows // count, width)


def row_order(values):
    c = lax.axis_index("c")
    split = values.reshape(2, 2, values.shape[0] // 4)
    own = jnp.where(c == 0, split[:, 0], split[:, 1]).reshape(-1)
    other = jnp.where(c == 0, split[:, 1], split[:, 0]).reshape(-1)
    return own, jnp.concatenate([own, other])


def local(
    source,
    target,
    cotangent,
    source_len,
    target_len,
    source_seg,
    target_seg,
    enc_qkv,
    enc_proj,
    enc_up,
    enc_down,
    enc_gain,
    enc_shift,
    dec_qkv,
    dec_proj,
    cross_qkv,
    cross_proj,
    dec_up,
    dec_down,
    dec_gain,
    dec_shift,
):
    copies, z = lax.axis_size("k"), lax.axis_index("mp")
    vectors = jnp.concatenate([enc_gain, enc_shift, dec_gain, dec_shift, dec_shift[:2]], 0)
    if copies > 1:
        vectors = lax.all_gather(vectors, "k", axis=1, tiled=True)
    lane = jnp.arange(128)[None]
    vectors = jnp.where(lane // 32 == z, jnp.tile(vectors, (1, 4)), 0.0)
    facts = jnp.concatenate(
        [
            jnp.concatenate([segments, jnp.broadcast_to(lengths[:, None], (2, 128))], 1)
            for lengths, segments in ((source_len, source_seg), (target_len, target_seg))
        ],
        0,
    )
    facts = jnp.concatenate([facts.reshape(-1, 128), jnp.zeros((4, 128), jnp.int32)], 0)
    enc_p = widen(pack_rows([*transposed(enc_qkv), enc_proj]))
    self_p = widen(pack_rows([*transposed(dec_qkv), dec_proj]))
    cross_p = widen(pack_rows([*transposed(cross_qkv), cross_proj]))
    enc_up_p, enc_down_p = widen(pack_rows([enc_up.T])), widen(pack_rows([enc_down]))
    dec_up_p, dec_down_p = widen(pack_rows([dec_up.T])), widen(pack_rows([dec_down]))

    (stream_in, target_in, grad_out), (enc_p, self_p), vectors, facts = open_program(
        [source, target, cotangent], vectors, facts, [enc_p, self_p]
    )
    if copies > 1:
        vectors = vectors.reshape(16, 2, 2, 2, 4, copies, 32 // copies)
        vectors = vectors.transpose(0, 1, 5, 2, 3, 4, 6).reshape(16, 1024)
    enc_w, self_w = gather_weights(enc_p), gather_weights(self_p)
    near = jnp.where(lax.axis_index("hi") == z // 2, facts[0], facts[1])[:36].reshape(2, 2, 1152)
    near = jnp.where(z % 2 == 0, near[:, 0], near[:, 1])
    source_length, source_ids = near[0, 1024], near[0, :1024]
    target_length, target_ids = near[1, 1024], near[1, :1024]
    place_own, place_all = row_order(jnp.arange(source_ids.shape[0]))
    source_own, source_all = row_order(source_ids)
    target_own, target_all = row_order(target_ids)
    zero = jnp.zeros_like(place_own)
    source_facts = jnp.stack([source_own, place_own] + [zero] * 6)
    target_facts = jnp.stack([target_own, place_own] + [zero] * 6)

    def key_facts(ids, length):
        live = (place_all < length).astype(jnp.int32)
        blank = jnp.zeros_like(live)
        return jnp.stack([ids, place_all, live] + [blank] * 5, 1)

    source_keys = key_facts(source_all, source_length)
    target_keys = key_facts(target_all, target_length)

    ENC_G, ENC_B, DEC_G, DEC_B = 0, 3, 6, 10
    Q, K, V, O = (0, 64), (64, 64), (128, 64), (192, 64)
    ALL = (0, 256)

    def forward_mid(call, residual, gain, shift):
        vec, res = call.take(vectors), call.take(residual)
        kept = call.give((128, 1024), F32)

        def mid(get, total):
            stream = get(res)[...].astype(F32) + total
            get(kept)[...] = stream
            unit, scale = unit_of(stream)
            return (unit * get(vec)[gain : gain + 1] + get(vec)[shift : shift + 1]).astype(BF16)

        return mid

    def backward_mid(call, stream, gain, residual=None):
        vec, kept = call.take(vectors), call.take(stream)
        res = None if residual is None else call.take(residual)
        grad_out, share_out = call.give((128, 1024), F32), call.give((2, 1024), F32)

        def mid(get, total):
            grad, shares = norm_back(get(kept)[...].astype(F32), get(vec)[gain : gain + 1], total)
            if res is not None:
                grad = grad + get(res)[...]
            get(grad_out)[...] = grad
            get(share_out)[...] = shares
            return grad.astype(BF16)

        return mid

    def activated(call):
        hidden = call.give((4, 128, 1024), BF16)
        slope = call.give((4, 128, 1024), F32)

        def store(get, at, row, column, value):
            made, slopes = gelu_pair(value)
            get(hidden)[row, :, column : column + value.shape[1]] = made.astype(BF16)
            get(slope)[row, :, column : column + value.shape[1]] = slopes

        return store

    def deactivated(call, slope):
        kept, out = call.take(slope), call.give((4, 128, 1024), BF16)

        def store(get, at, row, column, value):
            span = slice(column, column + value.shape[1])
            get(out)[row, :, span] = (value * get(kept)[row, :, span]).astype(BF16)

        return store

    call = Call()

    def first_mid(stream, gain, shift):
        vec, res = call.take(vectors), call.take(stream)

        def mid(get, total):
            unit, scale = unit_of(get(res)[...].astype(F32))
            return (unit * get(vec)[gain : gain + 1] + get(vec)[shift : shift + 1]).astype(BF16)

        return mid

    jobs = []
    for stream, gain, shift in ((stream_in, ENC_G, ENC_B), (target_in, DEC_G, DEC_B)):
        jobs.append(Job(call, None, first_mid(stream, gain, shift), (None, None, None)))
    swap = Swap(call, [enc_up_p, cross_p, enc_down_p, dec_up_p, dec_down_p])
    outs = run_stage(call, jobs, [], "first_rows", 0, flops=30 * MICROSECOND, more=swap)
    rows_a, rows_c = outs[:2]
    enc_up_w, cross_w, enc_down_w, dec_up_w, dec_down_w = (
        gather_weights(packed) for packed in outs[2:]
    )

    call = Call()
    made, finishes, plans = [], [], []
    for rows, packed in ((rows_a, enc_w), (rows_c, self_w)):
        weight = Weight(call, packed, 0, 192)
        store, finish = query_and_shared(call, 256)
        plans.append((call.take(rows), weight, store))
        finishes.append(finish)

    def project(get):
        at = place()
        for unused, weight, unused2 in plans:
            weight.start(get)
        greet([at["core"]])
        for rows, weight, store in plans:
            weight.wait(get)
            for row in range(4):
                for m in range(3):
                    store(
                        get, at, row, m * 256, nt(get(rows)[row], weight.matrix(get, m * 64, 64))
                    )
        for finish in finishes:
            finish(get)

    enc_q, enc_kv, self_q, self_kv = call.run(project, "project", 1, 6 * MICROSECOND)

    enc_mixed, enc_total = attend(enc_q, enc_kv, source_facts, source_keys, False)
    self_mixed, self_total = attend(self_q, self_kv, target_facts, target_keys, True)

    call = Call()
    enc_o, enc_u = Weight(call, enc_w, *O), Weight(call, enc_up_w, *ALL)
    self_o, cross_a = Weight(call, self_w, *O), Weight(call, cross_w, *Q)
    mid_b = forward_mid(call, stream_in, ENC_G + 1, ENC_B + 1)
    job_b = Job(call, (enc_mixed, enc_o, [(0, 64)]), mid_b, (enc_u, [(0, 256)], activated(call)))
    mid_d = forward_mid(call, target_in, DEC_G + 1, DEC_B + 1)
    job_d = Job(call, (self_mixed, self_o, [(0, 64)]), mid_d, (cross_a, [(0, 64)], None))
    query = Plain(call, 256)
    job_d.right = (cross_a, [(0, 64)], query.store)
    (
        stream_mid,
        enc_hidden,
        enc_slope,
        rows_b,
        target_mid,
        rows_d,
        cross_q,
    ) = run_stage(
        call,
        [job_b, job_d],
        [enc_o, self_o, enc_u, cross_a],
        "after_self",
        2,
        flops=32 * MICROSECOND,
    )

    call = Call()
    enc_d, cross_b = Weight(call, enc_down_w, *ALL), Weight(call, cross_w, 64, 128)
    mid_m = forward_mid(call, stream_mid, ENC_G + 2, ENC_B + 2)
    shared = Shared(call, 512)
    job = Job(
        call, (enc_hidden, enc_d, [(0, 256)]), mid_m, (cross_b, [(0, 64), (64, 64)], shared.store)
    )
    stream_end, cross_kv, memory = run_stage(
        call, [job], [enc_d, cross_b], "memory", 3, shared.finish, 20 * MICROSECOND, core=True
    )

    cross_mixed, cross_total = attend(cross_q, cross_kv, target_facts, source_keys, False)

    call = Call()
    cross_o, dec_u = Weight(call, cross_w, *O), Weight(call, dec_up_w, *ALL)
    mid_e = forward_mid(call, target_mid, DEC_G + 2, DEC_B + 2)
    job = Job(call, (cross_mixed, cross_o, [(0, 64)]), mid_e, (dec_u, [(0, 256)], activated(call)))
    target_late, dec_hidden, dec_slope, rows_e = run_stage(
        call, [job], [cross_o, dec_u], "after_cross", 4, flops=20 * MICROSECOND
    )

    call = Call()
    dec_d = Weight(call, dec_down_w, *ALL)
    vec, res, cot = call.take(vectors), call.take(target_late), call.take(grad_out)
    decoded_out, grad_end_out = call.give((128, 1024), BF16), call.give((128, 1024), F32)
    share_out = call.give((2, 1024), F32)

    def last_mid(get, total):
        stream = get(res)[...] + total
        gain, shift = get(vec)[DEC_G + 3 : DEC_G + 4], get(vec)[DEC_B + 3 : DEC_B + 4]
        unit, unused = unit_of(stream)
        get(decoded_out)[...] = (unit * gain + shift).astype(BF16)
        grad, shares = norm_back(stream, gain, get(cot)[...].astype(F32))
        get(grad_end_out)[...] = grad
        get(share_out)[...] = shares
        return grad.astype(BF16)

    job = Job(
        call,
        (dec_hidden, dec_d, [(0, 256)]),
        last_mid,
        (dec_d, [(0, 256)], deactivated(call, dec_slope)),
    )
    decoded, grad_end, norm_3, dec_grad_act, grad_rows_e = run_stage(
        call, [job], [dec_d], "turn", 5, flops=20 * MICROSECOND
    )
    dec_up_s, dec_down_s = weight_shares(
        [[(dec_grad_act, 0, by_owner(rows_e))], [(dec_hidden, 0, by_owner(grad_rows_e))]], 15
    )
    dec_up_g, dec_down_g = over_slots(dec_up_s), over_slots(dec_down_s)

    call = Call()
    call.take(dec_up_s, pl.ANY)
    call.take(dec_down_s, pl.ANY)
    dec_u, cross_o = Weight(call, dec_up_w, *ALL), Weight(call, cross_w, *O)
    mid = backward_mid(call, target_late, DEC_G + 2, grad_end)
    query = Plain(call, 256)
    job = Job(call, (dec_grad_act, dec_u, [(0, 256)]), mid, (cross_o, [(0, 64)], query.store))
    grad_late, norm_2, cross_grad_mixed, grad_rows_d = run_stage(
        call, [job], [dec_u, cross_o], "back_cross", 6, flops=20 * MICROSECOND
    )

    cross_grads = attend_back(
        cross_q, cross_kv, cross_grad_mixed, cross_total, target_facts, source_keys, False, 7
    )
    memory_o, rows_o = by_owner(memory), by_owner(rows_d)
    (cross_s,) = weight_shares(
        [
            [
                (cross_grads, 0, rows_o),
                (cross_grads, 256, memory_o),
                (cross_grads, 512, memory_o),
                (cross_mixed, 0, by_owner(grad_rows_d)),
            ]
        ],
        16,
    )
    cross_g = over_slots(cross_s)

    call = Call()
    call.take(cross_s, pl.ANY)
    cross_a, cross_b = Weight(call, cross_w, *Q), Weight(call, cross_w, 64, 128)
    self_o, enc_d = Weight(call, self_w, *O), Weight(call, enc_down_w, *ALL)
    mid = backward_mid(call, target_mid, DEC_G + 1, grad_late)
    query = Plain(call, 256)
    job_t = Job(
        call, (cross_grads[:, :, :256], cross_a, [(0, 64)]), mid, (self_o, [(0, 64)], query.store)
    )
    mid = backward_mid(call, stream_end, ENC_G + 2)
    job_s = Job(
        call,
        (cross_grads[:, :, 256:], cross_b, [(0, 64), (64, 64)]),
        mid,
        (enc_d, [(0, 256)], deactivated(call, enc_slope)),
    )
    (
        grad_mid,
        norm_1,
        self_grad_mixed,
        grad_rows_c,
        grad_stream,
        enc_norm_2,
        enc_grad_act,
        grad_rows_b,
    ) = run_stage(
        call,
        [job_t, job_s],
        [cross_a, cross_b, self_o, enc_d],
        "back_both",
        8,
        flops=32 * MICROSECOND,
    )
    enc_up_s, enc_down_s = weight_shares(
        [[(enc_grad_act, 0, by_owner(rows_b))], [(enc_hidden, 0, by_owner(grad_rows_b))]], 17
    )
    enc_up_g, enc_down_g = over_slots(enc_up_s), over_slots(enc_down_s)

    self_grads = attend_back(
        self_q, self_kv, self_grad_mixed, self_total, target_facts, target_keys, True, 9, [enc_up_s, enc_down_s]
    )
    rows_o = by_owner(rows_c)
    (self_s,) = weight_shares(
        [
            [
                (self_grads, 0, rows_o),
                (self_grads, 256, rows_o),
                (self_grads, 512, rows_o),
                (self_mixed, 0, by_owner(grad_rows_c)),
            ]
        ],
        18,
    )
    self_g = over_slots(self_s)

    call = Call()
    for done in (self_s, dec_up_g, dec_down_g):
        call.take(done, pl.ANY)
    enc_u, enc_o, self_a = Weight(call, enc_up_w, *ALL), Weight(call, enc_w, *O), Weight(call, self_w, 0, 192)
    mid = backward_mid(call, stream_mid, ENC_G + 1, grad_stream)
    query = Plain(call, 256)
    job_s = Job(call, (enc_grad_act, enc_u, [(0, 256)]), mid, (enc_o, [(0, 64)], query.store))
    mid = backward_mid(call, target_in, DEC_G, grad_mid)
    job_t = Job(call, (self_grads, self_a, [(0, 64), (64, 64), (128, 64)]), mid, None)
    (
        grad_stream,
        enc_norm_1,
        enc_grad_mixed,
        grad_rows_a,
        target_grad,
        norm_0,
    ) = run_stage(
        call, [job_s, job_t], [enc_u, self_a, enc_o], "back_self", 10, flops=28 * MICROSECOND
    )

    enc_grads = attend_back(
        enc_q, enc_kv, enc_grad_mixed, enc_total, source_facts, source_keys, False, 11, [cross_g]
    )
    rows_o = by_owner(rows_a)
    (enc_s,) = weight_shares(
        [
            [
                (enc_grads, 0, rows_o),
                (enc_grads, 256, rows_o),
                (enc_grads, 512, rows_o),
                (enc_mixed, 0, by_owner(grad_rows_a)),
            ]
        ],
        19,
    )
    enc_g = over_slots(enc_s)

    call = Call()
    for done in (enc_s, enc_up_g, enc_down_g):
        call.take(done, pl.ANY)
    enc_a = Weight(call, enc_w, 0, 192)
    mid = backward_mid(call, stream_in, ENC_G, grad_stream)
    job = Job(call, (enc_grads, enc_a, [(0, 64), (64, 64), (128, 64)]), mid, None)
    source_grad, enc_norm_0 = run_stage(
        call, [job], [enc_a], "back_first", 12, flops=12 * MICROSECOND
    )

    norm_share = jnp.stack(
        [enc_norm_0, enc_norm_1, enc_norm_2], 1
    ).reshape(6, 1024)
    norm_share = jnp.concatenate(
        [
            norm_share,
            jnp.stack([norm_0, norm_1, norm_2, norm_3], 1).reshape(8, 1024),
            jnp.zeros((2, 1024), F32),
        ],
        0,
    )
    (decoded, source_grad, target_grad), swapped, norm_grad = close_program(
        [decoded, source_grad.astype(BF16), target_grad.astype(BF16)],
        by_owner(norm_share),
        [dec_up_g, dec_down_g, cross_g, enc_up_g, enc_down_g, self_g],
    )
    norm_grad = norm_grad.reshape(16, copies, 4, 32 // copies)
    if copies > 1:
        norm_grad = lax.psum_scatter(norm_grad, "k", scatter_dimension=1)
    norm_grad = norm_grad.reshape(16, 4, -1)
    norm_grad = lax.dynamic_index_in_dim(norm_grad, z, 1, False)
    (enc_g,) = swap_packs([enc_g], 20)

    def attend_shares(packed):
        grads = unpack(narrow(packed), 4)
        return jnp.swapaxes(grads[:3], 1, 2), grads[3]

    def feed_share(packed):
        return unpack(narrow(packed), 1)[0]

    dec_u, dec_d, enc_u, enc_d = (feed_share(swapped[i]) for i in (0, 1, 3, 4))
    dec_u, enc_u = dec_u.T, enc_u.T
    enc_a, enc_o = attend_shares(enc_g)
    cross_a, cross_o = attend_shares(swapped[2])
    self_a, self_o = attend_shares(swapped[5])
    return (
        decoded,
        source_grad.astype(F32),
        target_grad.astype(F32),
        enc_a,
        enc_o,
        enc_u,
        enc_d,
        norm_grad[:3],
        norm_grad[3:6],
        self_a,
        self_o,
        cross_a,
        cross_o,
        dec_u,
        dec_d,
        norm_grad[6:10],
        norm_grad[10:14],
    )


def solution(mesh):
    dp, seq, mp = (mesh.shape[name] for name in ("dp", "seq", "mp"))
    assert dp % 2 == 0 and seq == 4 and mp == 4
    fine = Mesh(mesh.devices.reshape(2, dp // 2, 2, 2, 4), AXES)
    d, s = ("hi", "k"), ("y", "c")
    rows = P(d, s + ("mp",), None)
    three, flat = P(None, d + s, "mp"), P("mp", d + s)
    up, vector = P(d + s, "mp"), P(None, d + s + ("mp",))
    attention, feeding = (three, flat), (up, flat)
    return jax.shard_map(
        local,
        mesh=fine,
        in_specs=(rows,) * 3
        + (P(d), P(d), P(d, None), P(d, None))
        + attention
        + feeding
        + (vector, vector)
        + attention * 2
        + feeding
        + (vector, vector),
        out_specs=(rows,) * 3
        + attention
        + feeding
        + (vector, vector)
        + attention * 2
        + feeding
        + (vector, vector),
        check_vma=False,
    )
```

time: 1290 us -> 597 us (0.46)
  matrix products: 250 us -> 0 us
  waiting for transfers between devices: 276 us -> 52.5 us
  local copies, waits for them, and re-layouts: 172 us -> 64.1 us
  blocking collectives: 95 us -> 0 us
  Pallas kernels: 363 us -> 452 us
  other arithmetic: 64 us -> 6.2 us
  starting transfers between devices: 41.3 us -> 2.12 us
    dot_general x56 -> x0, matrix products: 250 us -> none  [the longest x3 65.8 us: attend_back(): jnp.einsum('hqk,khd->qhd', grad_raw, heads(keys), preferred_element_type=...]
    reduce_scatter x12 -> x7, waiting for transfers between devices: 176 us -> 0.04 us  [over_slots(): return lax.psum_scatter(shares, 'mp', scatter_dimension=0)]
    pallas_call x22 -> x24, Pallas kernels: 363 us -> 452 us  [the longest x21 428 us: run(): pl.pallas_call(kernel, out_shape=tuple(self.shapes), in_specs=self.specs,...]
    all_to_all x5 -> x0, blocking collectives: 50.8 us -> none  [gather_weights(): packed = lax.all_to_all(packed, ('hi', 'y'), 0, 0, tiled=True)]
    all_gather x4 -> x0, blocking collectives: 44.2 us -> none  [local(): vectors = lax.all_gather(vectors, name, axis=1, tiled=True)]
    unnamed x309 -> x218, local copies, waits for them, and re-layouts: 15 us -> 51.9 us
    another operation x9 -> x17, local copies, waits for them, and re-layouts: 33.7 us -> 0.87 us  [the longest x4 0.48 us: key_facts(): return jnp.stack([ids, place_all, live] + [blank] * 5, 1)]
    transpose x10 -> x7, local copies, waits for them, and re-layouts: 32.8 us -> 2.39 us  [the longest x2 1.99 us: local(): dec_u, enc_u = (dec_u.T, enc_u.T)]
  transfers between devices with their start and end apart: 51 -> 14, of which waited for: 16 -> 3; matrix products, arithmetic and copies ran while one was open for 25% -> 3% of each run, Pallas kernels for 17% -> 65%
where the time goes in v2:
time: 597 us; the launch traced here: 592 us
  Pallas kernels  452 us (76%)
  local copies, waits for them, and re-layouts  64.1 us (11%)
  waiting for transfers between devices  52.5 us (9%)
  between operations  15.9 us (3%)
  other arithmetic  6.2 us (1%)
    pallas_call x21, Pallas kernels, run(): pl.pallas_call(kernel, out_shape=tuple(self.shapes), in_specs=self.specs,...  428 us
    unnamed x218, local copies, waits for them, and re-layouts  51.9 us
    all_gather x7, waiting for transfers between devices, gather_weights(): packed = lax.all_gather(packed, ('c', 'mp')).reshape(2, 4, 4, rows, 128)  48.2 us
    pallas_call x3, Pallas kernels, attend(): pl.pallas_call(kernel, out_shape=(jax.ShapeDtypeStruct((rows, width), BF1...  23.2 us
  transfers between devices with their start and end apart: 14, of which 3 were waited for; matrix products, arithmetic and copies ran while one was open for 3% of the time, Pallas kernels for 65%

profile of v2, /device:TPU:0, one launch (start us, length us, event | category | flops | bytes accessed | tf_op | source)
XLA Modules:
  0.0 592.3 jit_solution(515145051155252198)
XLA Ops:
  8.1 2.2 concatenate.50
  14.2 29.6 %open_program.1 = (bf16[128,1024]{1,0:T(8,128)(2,1)S(1)}, bf16[128,1024]{1,0:T(8,128)(2,1)S(1)}, bf16[128,1024]{1,0:T(8,128)(2,1)S(1)}, bf16[4,256,128]{2,1,0:T(...) custom-call(bf16[2,64,1024]{2,1,0:T(8,128)(2,1)S(1)} %copy-done.3, ...), custom_call_target="tpu_custom_call" | custom-call | flops 12000000000 | tf_op jit(solution)/shard_map/open_program/pallas_call | solution.py:49
  46.2 49.6 %first_rows.1 = (bf16[4,128,1024]{2,1,0:T(8,128)(2,1)S(1)}, bf16[4,128,1024]{2,1,0:T(8,128)(2,1)S(1)}, bf16[4,256,128]{2,1,0:T(8,128)(2,1)}, bf16[4,256,128]{2,1...) custom-call(f32[16,1024]{1,0:T(8,128)S(1)} %get-tuple-element.94.refs_0_., ...), custom_call_target="tpu_custom_call" | custom-call | flops 30000001024 | tf_op jit(solution)/shard_map/first_rows/pallas_call | solution.py:49
  100.6 1.3 compare_convert_fusion
  102.8 13.6 %all-gather.25.cloned.1.call-done = bf16[32,256,128]{2,1,0:T(8,128)(2,1)} async-done(((bf16[4,256,128]{2,1,0:T(8,128)(2,1)}), bf16[32,256,128]{2,1,0:T(8,128)(2,1)}) %all-gather.25.cloned.1.call-update) | async-done | bytes 2097168 | tf_op jit(solution)/shard_map/all_gather | solution.py:847
  117.6 8.9 %project.1 = (bf16[4,128,256]{2,1,0:T(8,128)(2,1)S(1)}, bf16[2,4,128,512]{3,2,1,0:T(8,128)(2,1)S(1)}, bf16[4,128,256]{2,1,0:T(8,128)(2,1)S(1)}, bf16[2,4,128,512]{3,2,1,0:T(8,128)(2,1)S(1)}) custom-call(bf16[2,4,4,256,128]{4,3,2,1,0:T(8,128)(2,1)} %bitcast.201, bf16[4,128,1024]{2,1,0:T(8,128)(2,1)S(1)} %get-tuple-element.103.refs_1_, ...), custom_call_target="tpu_custom_call" | custom-call | flops 6000000000 | tf_op jit(solution)/shard_map/project/pallas_call | solution.py:49
  126.5 7.7 %attend.4 = (bf16[512,256]{1,0:T(8,128)(2,1)S(1)}, f32[8,512]{1,0:T(8,128)S(1)}) custom-call(bf16[512,256]{1,0:T(8,128)(2,1)S(1)} %bitcast.249, bf16[1024,512]{1,0:T(8,128)(2,1)S(1)} %bitcast.227, s32[8,512]{1,0:T(8,128)S(1)} %get-tuple-element.232.refs_2_.refs_4_, s32[1024,8]{1,0:T(8,128)S(1)} %copy.106.refs_3_.refs_5_), custom_call_target="tpu_custom_call" | custom-call | flops 8000000000 | tf_op jit(solution)/shard_map/attend/pallas_call | solution.py:434
  134.3 7.7 %attend.3 = (bf16[512,256]{1,0:T(8,128)(2,1)S(1)}, f32[8,512]{1,0:T(8,128)S(1)}) custom-call(bf16[512,256]{1,0:T(8,128)(2,1)S(1)} %bitcast.246, bf16[1024,512]{1,0:T(8,128)(2,1)S(1)} %bitcast.225, s32[8,512]{1,0:T(8,128)S(1)} %get-tuple-element.233.refs_2_.refs_4_, s32[1024,8]{1,0:T(8,128)S(1)} %copy.105.refs_3_.refs_5_), custom_call_target="tpu_custom_call" | custom-call | flops 8000000000 | tf_op jit(solution)/shard_map/attend/pallas_call | solution.py:434
  142.1 4.5 all-gather.17.cloned.1.call-done
  146.6 30.1 %all-gather.23.cloned.1.call-done = bf16[32,256,128]{2,1,0:T(8,128)(2,1)} async-done(((bf16[4,256,128]{2,1,0:T(8,128)(2,1)}), bf16[32,256,128]{2,1,0:T(8,128)(2,1)}) %all-gather.23.cloned.1.call-update) | async-done | bytes 2097168 | tf_op jit(solution)/shard_map/all_gather | solution.py:847
  177.6 40.0 %after_self.1 = (f32[128,1024]{1,0:T(8,128)S(1)}, bf16[4,128,1024]{2,1,0:T(8,128)(2,1)S(1)}, f32[4,128,1024]{2,1,0:T(8,128)}, bf16[4,128,1024]{2,1,0:T(8,128)(2,...) custom-call(bf16[2,4,4,256,128]{4,3,2,1,0:T(8,128)(2,1)} %bitcast.202, ...), custom_call_target="tpu_custom_call" | custom-call | flops 32000000000 | tf_op jit(solution)/shard_map/after_self/pallas_call | solution.py:49
  222.3 23.5 %memory.1 = (f32[128,1024]{1,0:T(8,128)S(1)}, bf16[2,4,128,512]{3,2,1,0:T(8,128)(2,1)S(1)}, bf16[4,128,1024]{2,1,0:T(8,128)(2,1)S(1)}) custom-call(bf16[2,4,4,256,128]{4,3,2,1,0:T(8,128)(2,1)} %bitcast.312, bf16[2,4,4,256,128]{4,3,2,1,0:T(8,128)(2,1)} %bitcast.308, f32[16,1024]{1,0:T(8,128)S(1)} %get-tuple-element.94.refs_0_.refs_4_.refs_2_.refs_1_.refs_6_, ...), custom_call_target="tpu_custom_call" | custom-call | flops 20000000000 | tf_op jit(solution)/shard_map/memory/pallas_call | solution.py:49
  247.6 7.8 %attend.5 = (bf16[512,256]{1,0:T(8,128)(2,1)S(1)}, f32[8,512]{1,0:T(8,128)S(1)}) custom-call(bf16[512,256]{1,0:T(8,128)(2,1)S(1)} %bitcast.252, bf16[1024,512]{1,0:T(8,128)(2,1)S(1)} %bitcast.236, s32[8,512]{1,0:T(8,128)S(1)} %get-tuple-element.232.refs_2_.refs_4_, s32[1024,8]{1,0:T(8,128)S(1)} %copy.105.refs_3_.refs_5_), custom_call_target="tpu_custom_call" | custom-call | flops 8000000000 | tf_op jit(solution)/shard_map/attend/pallas_call | solution.py:434
  257.4 23.6 %after_cross.1 = (f32[128,1024]{1,0:T(8,128)S(1)}, bf16[4,128,1024]{2,1,0:T(8,128)(2,1)S(1)}, f32[4,128,1024]{2,1,0:T(8,128)S(1)}, bf16[4,128,1024]{2,1,0:T(8,128)(2,1)S(1)}) custom-call(bf16[2,4,4,256,128]{4,3,2,1,0:T(8,128)(2,1)} %bitcast.309, bf16[2,4,4,256,128]{4,3,2,1,0:T(8,128)(2,1)} %bitcast.314, ...), custom_call_target="tpu_custom_call" | custom-call | flops 20000000000 | tf_op jit(solution)/shard_map/after_cross/pallas_call | solution.py:49
  283.0 1.3 copy-done.62
  285.2 1.2 copy-done.45
  287.4 24.2 %turn.1 = (bf16[128,1024]{1,0:T(8,128)(2,1)S(1)}, f32[128,1024]{1,0:T(8,128)S(1)}, f32[2,1024]{1,0:T(2,128)S(1)}, bf16[4,128,1024]{2,1,0:T(8,128)(2,1)S(1)}, bf16[4,128,1024]{2,1,0:T(8,128)(2,1)S(1)}) custom-call(bf16[2,4,4,256,128]{4,3,2,1,0:T(8,128)(2,1)} %bitcast.316, f32[16,1024]{1,0:T(8,128)S(1)} %get-tuple-element.94.refs_0_.refs_4_.refs_2_.refs_1_.refs_6_, ...), custom_call_target="tpu_custom_call" | custom-call | flops 20000000000 | tf_op jit(solution)/shard_map/turn/pallas_call | solution.py:49
  312.6 8.6 %weight_shares.5 = (bf16[4,4,256,128]{3,2,1,0:T(8,128)(2,1)}, bf16[4,4,256,128]{3,2,1,0:T(8,128)(2,1)}) custom-call(bf16[512,1024]{1,0:T(8,128)(2,1)S(1)} %bitcast.238, bf16[512,1024]{1,0:T(8,128)(2,1)S(1)} %bitcast.241, bf16[512,1024]{1,0:T(8,128)(2,1)S(1)} %bitcast.240, bf16[512,1024]{1,0:T(8,128)(2,1)} %bitcast.243), custom_call_target="tpu_custom_call" | custom-call | flops 8000000000 | tf_op jit(solution)/shard_map/weight_shares/pallas_call | solution.py:49
  324.8 23.8 %back_cross.1 = (f32[128,1024]{1,0:T(8,128)S(1)}, f32[2,1024]{1,0:T(2,128)S(1)}, bf16[4,128,256]{2,1,0:T(8,128)(2,1)S(1)}, bf16[4,128,1024]{2,1,0:T(8,128)(2,1)S(1)}) custom-call(bf16[4,4,256,128]{3,2,1,0:T(8,128)(2,1)} %get-tuple-element.127.refs_0_, bf16[4,4,256,128]{3,2,1,0:T(8,128)(2,1)} %get-tuple-element.128.refs_1_, ...), custom_call_target="tpu_custom_call" | custom-call | flops 20000000000 | tf_op jit(solution)/shard_map/back_cross/pallas_call | solution.py:49
  348.6 9.0 %attend_back.3.refs_0_.refs_2_.refs_4_ = bf16[512,768]{1,0:T(8,128)(2,1)S(1)} custom-call(bf16[512,256]{1,0:T(8,128)(2,1)S(1)} %bitcast.253, bf16[1024,512]{1,0:T(8,128)(2,1)S(1)} %bitcast.237, bf16[512,256]{1,0:T(8,128)(2,1)S(1)} %bitcast.257, f32[8,512]{1,0:T(8,128)S(1)} %get-tuple-element.131.refs_3_, s32[8,512]{1,0:T(8,128)S(1)} %get-tuple-element.232.refs_2_.refs_4_, ...), custom_call_target="tpu_custom_call" | custom-call | flops 16000000000 | tf_op jit(solution)/shard_map/attend_back/pallas_call | solution.py:49
  357.7 4.6 weight_shares.6.refs_0_
  365.7 40.8 %back_both.1 = (f32[128,1024]{1,0:T(8,128)S(1)}, f32[2,1024]{1,0:T(2,128)S(1)}, bf16[4,128,256]{2,1,0:T(8,128)(2,1)S(1)}, bf16[4,128,1024]{2,1,0:T(8,128)(2,1)S(...) custom-call(bf16[4,4,256,128]{3,2,1,0:T(8,128)(2,1)} %weight_shares., ...), custom_call_target="tpu_custom_call" | custom-call | flops 32000000000 | tf_op jit(solution)/shard_map/back_both/pallas_call | solution.py:49
  408.3 8.5 %weight_shares.7 = (bf16[4,4,256,128]{3,2,1,0:T(8,128)(2,1)}, bf16[4,4,256,128]{3,2,1,0:T(8,128)(2,1)}) custom-call(bf16[512,1024]{1,0:T(8,128)(2,1)S(1)} %bitcast.231, bf16[512,1024]{1,0:T(8,128)(2,1)S(1)} %bitcast.230, bf16[512,1024]{1,0:T(8,128)(2,1)S(1)} %bitcast.229, bf16[512,1024]{1,0:T(8,128)(2,1)} %bitcast.317), custom_call_target="tpu_custom_call" | custom-call | flops 8000000000 | tf_op jit(solution)/shard_map/weight_shares/pallas_call | solution.py:49
  418.3 9.2 %attend_back.4.refs_0_.refs_2_.refs_4_ = bf16[512,768]{1,0:T(8,128)(2,1)S(1)} custom-call(bf16[512,256]{1,0:T(8,128)(2,1)S(1)} %bitcast.250, bf16[1024,512]{1,0:T(8,128)(2,1)S(1)} %bitcast.228, bf16[512,256]{1,0:T(8,128)(2,1)S(1)} %bitcast.255, f32[8,512]{1,0:T(8,128)S(1)} %get-tuple-element.139.refs_3_, s32[8,512]{1,0:T(8,128)S(1)} %get-tuple-element.232.refs_2_.refs_4_, ...), custom_call_target="tpu_custom_call" | custom-call | flops 16000000000 | tf_op jit(solution)/shard_map/attend_back/pallas_call | solution.py:49
  427.6 4.5 weight_shares.8.refs_0_
  439.6 31.6 %back_self.1 = (f32[128,1024]{1,0:T(8,128)S(1)}, f32[2,1024]{1,0:T(2,128)S(1)}, bf16[4,128,256]{2,1,0:T(8,128)(2,1)S(1)}, bf16[4,128,1024]{2,1,0:T(8,128)(2,1)S(...) custom-call(bf16[4,4,256,128]{3,2,1,0:T(8,128)(2,1)} %weight_shares.8.refs_0_, bf16[4,256,128]{2,1,0:T(8,128)(2,1)S(1)} %bitcast.207, ...), custom_call_target="tpu_custom_call" | custom-call | flops 28000000000 | tf_op jit(solution)/shard_map/back_self/pallas_call | solution.py:49
  473.1 9.0 %attend_back.5.refs_0_.refs_2_.refs_4_ = bf16[512,768]{1,0:T(8,128)(2,1)S(1)} custom-call(bf16[512,256]{1,0:T(8,128)(2,1)S(1)} %bitcast.247, bf16[1024,512]{1,0:T(8,128)(2,1)S(1)} %bitcast.226, bf16[512,256]{1,0:T(8,128)(2,1)S(1)} %bitcast.256, f32[8,512]{1,0:T(8,128)S(1)} %get-tuple-element.149.refs_3_, s32[8,512]{1,0:T(8,128)S(1)} %copy-done.1, ...), custom_call_target="tpu_custom_call" | custom-call | flops 16000000000 | tf_op jit(solution)/shard_map/attend_back/pallas_call | solution.py:49
  482.2 4.8 weight_shares.9.refs_0_
  487.9 1.6 copy-done.2
  492.6 12.6 %back_first.1 = (f32[128,1024]{1,0:T(8,128)S(1)}, f32[2,1024]{1,0:T(2,128)S(1)}) custom-call(bf16[4,4,256,128]{3,2,1,0:T(8,128)(2,1)} %weight_shares.9.refs_0_, bf16[4,256,128]{2,1,0:T(8,128)(2,1)S(1)} %bitcast.213, bf16[4,256,128]{2,1,0:T(8,128)(2,1)S(1)} %bitcast.215, bf16[2,4,4,256,128]{4,3,2,1,0:T(8,128)(2,1)S(1)} %bitcast.204, ...), custom_call_target="tpu_custom_call" | custom-call | flops 12000000000 | tf_op jit(solution)/shard_map/back_first/pallas_call | solution.py:49
  509.3 55.5 %close_program.1 = (bf16[2,64,1024]{2,1,0:T(8,128)(2,1)S(1)}, bf16[2,64,1024]{2,1,0:T(8,128)(2,1)S(1)}, bf16[2,64,1024]{2,1,0:T(8,128)(2,1)S(1)}, bf16[4,256,128...) custom-call(bf16[128,1024]{1,0:T(8,128)(2,1)S(1)} %copy-done.86, ...), custom_call_target="tpu_custom_call" | custom-call | flops 16000000000 | tf_op jit(solution)/shard_map/close_program/pallas_call | solution.py:49
  576.4 6.5 %swap_packs.1 = bf16[4,256,128]{2,1,0:T(8,128)(2,1)S(1)} custom-call(bf16[4,256,128]{2,1,0:T(8,128)(2,1)S(1)} %bitcast.218), custom_call_target="tpu_custom_call" | custom-call | flops 5000000000 | tf_op jit(solution)/shard_map/swap_packs/pallas_call | solution.py:49
  (333 shorter events, 69.1 us)
Async XLA Ops:
  7.3 95.5 %all-gather.21.cloned.1.call-start = ((), (), s32[]{:S(2)}) async-start(), calls=%async_computation.17 | async-start | bytes 2359296 | tf_op jit(solution)/shard_map/all_gather | solution.py:847
  14.2 31.2 %copy-start.93 = (bf16[3,128,256]{2,1,0:T(8,128)(2,1)S(1)}, bf16[3,128,256]{2,1,0:T(8,128)(2,1)}, u32[]{:S(2)}) copy-start(bf16[3,128,256]{2,1,0:T(8,128)(2,1)} %param.36) | copy-start | bytes 589828
  14.2 31.5 %copy-start.95 = (bf16[256,128]{1,0:T(8,128)(2,1)S(1)}, bf16[256,128]{1,0:T(8,128)(2,1)}, u32[]{:S(2)}) copy-start(bf16[256,128]{1,0:T(8,128)(2,1)} %param.37) | copy-start | bytes 196612
  44.5 51.3 %copy-start.65 = (bf16[128,1024]{1,0:T(8,128)(2,1)}, bf16[128,1024]{1,0:T(8,128)(2,1)S(1)}, u32[]{:S(2)}) copy-start(bf16[128,1024]{1,0:T(8,128)(2,1)S(1)} %get-tuple-element.96.refs_2_.refs_7_.refs_10_) | copy-start | bytes 786436
  44.5 132.2 %copy-start.63 = (bf16[128,1024]{1,0:T(8,128)(2,1)}, bf16[128,1024]{1,0:T(8,128)(2,1)S(1)}, u32[]{:S(2)}) copy-start(bf16[128,1024]{1,0:T(8,128)(2,1)S(1)} %get-tuple-element.95.refs_1_.refs_5_) | copy-start | bytes 786436
  44.6 71.8 %all-gather.25.cloned.1.call-start = ((), (), s32[]{:S(2)}) async-start(), calls=%async_computation.19 | async-start | bytes 2359296 | tf_op jit(solution)/shard_map/all_gather | solution.py:847
  45.3 101.3 %all-gather.17.cloned.1.call-start = ((), (), s32[]{:S(2)}) async-start(), calls=%async_computation.15 | async-start | bytes 2359296 | tf_op jit(solution)/shard_map/all_gather | solution.py:847
  96.8 29.7 %copy-start.20 = (bf16[4,128,1024]{2,1,0:T(8,128)(2,1)}, bf16[4,128,1024]{2,1,0:T(8,128)(2,1)S(1)}, u32[]{:S(2)}) copy-start(bf16[4,128,1024]{2,1,0:T(8,128)(2,1)S(1)} %get-tuple-element.103.refs_1_) | copy-start | bytes 3145732
  96.8 79.8 %all-gather.23.cloned.1.call-start = ((), (), s32[]{:S(2)}) async-start(), calls=%async_computation.18 | async-start | bytes 2359296 | tf_op jit(solution)/shard_map/all_gather | solution.py:847
  97.4 123.9 %all-gather.27.cloned.1.call-start = ((), (), s32[]{:S(2)}) async-start(), calls=%async_computation.20 | async-start | bytes 2359296 | tf_op jit(solution)/shard_map/all_gather | solution.py:847
  98.0 158.4 %all-gather.19.cloned.1.call-start = ((), (), s32[]{:S(2)}) async-start(), calls=%async_computation.16 | async-start | bytes 2359296 | tf_op jit(solution)/shard_map/all_gather | solution.py:847
  98.6 186.6 %all-gather.15.cloned.1.call-start = ((), (), s32[]{:S(2)}) async-start(), calls=%async_computation.14 | async-start | bytes 2359296 | tf_op jit(solution)/shard_map/all_gather | solution.py:847
  99.3 333.1 %reduce-scatter.8.cloned.1.call-start = ((), (), s32[]{:S(2)}) async-start(), calls=%async_computation.7 | async-start | bytes 1310720 | tf_op jit(solution)/shard_map/reduce_scatter | solution.py:837
  102.8 31.5 %copy-start = (s32[8,512]{1,0:T(8,128)}, s32[8,512]{1,0:T(8,128)S(1)}, u32[]{:S(2)}) copy-start(s32[8,512]{1,0:T(8,128)S(1)} %get-tuple-element.233.refs_2_.refs_4_) | copy-start | bytes 49156
  134.3 42.4 %copy-start.60 = (bf16[512,256]{1,0:T(8,128)(2,1)}, bf16[512,256]{1,0:T(8,128)(2,1)S(1)}, u32[]{:S(2)}) copy-start(bf16[512,256]{1,0:T(8,128)(2,1)S(1)} %get-tuple-element.111.refs_6_) | copy-start | bytes 786436
  142.1 75.6 %copy-start.56 = (bf16[512,256]{1,0:T(8,128)(2,1)}, bf16[512,256]{1,0:T(8,128)(2,1)S(1)}, u32[]{:S(2)}) copy-start(bf16[512,256]{1,0:T(8,128)(2,1)S(1)} %get-tuple-element.108.refs_6_) | copy-start | bytes 786436
  257.4 27.8 %copy-start.69 = (bf16[128,1024]{1,0:T(8,128)(2,1)S(1)}, bf16[128,1024]{1,0:T(8,128)(2,1)}, u32[]{:S(2)}) copy-start(bf16[128,1024]{1,0:T(8,128)(2,1)} %copy-done.68) | copy-start | bytes 786436
  287.4 25.2 %copy-start.46 = (bf16[4,128,1024]{2,1,0:T(8,128)(2,1)S(1)}, bf16[4,128,1024]{2,1,0:T(8,128)(2,1)}, u32[]{:S(2)}) copy-start(bf16[4,128,1024]{2,1,0:T(8,128)(2,1)} %copy-done.44) | copy-start | bytes 3145732
  287.4 25.2 %copy-start.48 = (bf16[4,128,1024]{2,1,0:T(8,128)(2,1)S(1)}, bf16[4,128,1024]{2,1,0:T(8,128)(2,1)}, u32[]{:S(2)}) copy-start(bf16[4,128,1024]{2,1,0:T(8,128)(2,1)} %copy-done.47) | copy-start | bytes 3145732
  321.4 111.1 %reduce-scatter.10.cloned.1.call-start = ((), (), s32[]{:S(2)}) async-start(), calls=%async_computation.8 | async-start | bytes 1310720 | tf_op jit(solution)/shard_map/reduce_scatter | solution.py:837
  322.1 150.1 %reduce-scatter.12.cloned.1.call-start = ((), (), s32[]{:S(2)}) async-start(), calls=%async_computation.9 | async-start | bytes 1310720 | tf_op jit(solution)/shard_map/reduce_scatter | solution.py:837
  324.8 23.8 %copy-start.39 = (bf16[2,4,128,512]{3,2,1,0:T(8,128)(2,1)S(1)}, bf16[2,4,128,512]{3,2,1,0:T(8,128)(2,1)}, u32[]{:S(2)}) copy-start(bf16[2,4,128,512]{3,2,1,0:T(8,128)(2,1)} %copy-done.38) | copy-start | bytes 3145732
  362.3 125.6 %reduce-scatter.14.cloned.1.call-start = ((), (), s32[]{:S(2)}) async-start(), calls=%async_computation.10 | async-start | bytes 1310720 | tf_op jit(solution)/shard_map/reduce_scatter | solution.py:837
  365.7 42.6 %copy-start.30 = (bf16[4,128,1024]{2,1,0:T(8,128)(2,1)S(1)}, bf16[4,128,1024]{2,1,0:T(8,128)(2,1)}, u32[]{:S(2)}) copy-start(bf16[4,128,1024]{2,1,0:T(8,128)(2,1)} %copy-done.29) | copy-start | bytes 3145732
  416.9 71.0 %reduce-scatter.16.cloned.1.call-start = ((), (), s32[]{:S(2)}) async-start(), calls=%async_computation.11 | async-start | bytes 1310720 | tf_op jit(solution)/shard_map/reduce_scatter | solution.py:837
  417.5 88.5 %reduce-scatter.18.cloned.1.call-start = ((), (), s32[]{:S(2)}) async-start(), calls=%async_computation.12 | async-start | bytes 1310720 | tf_op jit(solution)/shard_map/reduce_scatter | solution.py:837
  418.3 9.2 %copy-start.37 = (bf16[4,128,1024]{2,1,0:T(8,128)(2,1)S(1)}, bf16[4,128,1024]{2,1,0:T(8,128)(2,1)}, u32[]{:S(2)}) copy-start(bf16[4,128,1024]{2,1,0:T(8,128)(2,1)} %copy-done.36) | copy-start | bytes 3145732
  418.3 9.2 %copy-start.61 = (bf16[512,256]{1,0:T(8,128)(2,1)S(1)}, bf16[512,256]{1,0:T(8,128)(2,1)}, u32[]{:S(2)}) copy-start(bf16[512,256]{1,0:T(8,128)(2,1)} %copy-done.60) | copy-start | bytes 786436
  432.1 143.3 %reduce-scatter.20.cloned.1.call-start = ((), (), s32[]{:S(2)}) async-start(), calls=%async_computation.13 | async-start | bytes 1310720 | tf_op jit(solution)/shard_map/reduce_scatter | solution.py:837
  439.6 32.6 %copy-start.1 = (s32[8,512]{1,0:T(8,128)S(1)}, s32[8,512]{1,0:T(8,128)}, u32[]{:S(2)}) copy-start(s32[8,512]{1,0:T(8,128)} %copy-done) | copy-start | bytes 49156
  439.6 32.6 %copy-start.26 = (bf16[2,4,128,512]{3,2,1,0:T(8,128)(2,1)S(1)}, bf16[2,4,128,512]{3,2,1,0:T(8,128)(2,1)}, u32[]{:S(2)}) copy-start(bf16[2,4,128,512]{3,2,1,0:T(8,128)(2,1)} %copy-done.25) | copy-start | bytes 3145732
  439.6 32.6 %copy-start.55 = (bf16[4,128,256]{2,1,0:T(8,128)(2,1)S(1)}, bf16[4,128,256]{2,1,0:T(8,128)(2,1)}, u32[]{:S(2)}) copy-start(bf16[4,128,256]{2,1,0:T(8,128)(2,1)} %copy-done.54) | copy-start | bytes 786436
  (83 other events, 263.6 us)
Sparse Core Ops, SparseCore 0:
  44.7 41.4 all-gather.20
  87.7 28.5 all-gather.24
  118.0 28.5 all-gather.16
  148.0 28.5 all-gather.22
  178.1 28.5 all-gather.26
  208.2 28.5 all-gather.18
  238.4 28.5 all-gather.14
  321.5 25.6 reduce-scatter.7
  349.6 25.8 reduce-scatter.9
  377.6 25.7 reduce-scatter.11
  417.0 25.9 reduce-scatter.13
  445.1 25.7 reduce-scatter.15
  473.3 25.8 reduce-scatter.17
  505.6 47.9 reduce-scatter.19

commit v3 on v2

--- a/solution.py
+++ b/solution.py
@@ -1,3 +1,5 @@
+import math
+
 import jax
 import jax.numpy as jnp
 from jax import lax
@@ -16,20 +18,41 @@
 
 class Call:
     def __init__(self):
-        self.arrays, self.specs = [], []
-        self.shapes, self.scratch = [], []
+        self.known, self.arrays, self.specs = [], [], []
+        self.shapes, self.places, self.scratch = [], [], []
+        self.fetched, self.kept = [], []
 
     def take(self, array, space=pltpu.VMEM):
-        for i, known in enumerate(self.arrays):
-            if known is array:
+        for i, known in enumerate(self.known):
+            if known is array and self.specs[i].memory_space == space:
                 return ("in", i)
+        self.known.append(array)
+        if space == pltpu.HBM:
+            array = pltpu.with_memory_space_constraint(array, pltpu.HBM)
         self.arrays.append(array)
         self.specs.append(pl.BlockSpec(memory_space=space))
         return ("in", len(self.arrays) - 1)
 
-    def give(self, shape, dtype):
-        self.shapes.append(jax.ShapeDtypeStruct(shape, dtype))
+    def fetch(self, array):
+        source = self.take(array, pltpu.HBM)
+        for i, (known, room, sem) in enumerate(self.fetched):
+            if known == source:
+                return ("fetch", i)
+        self.fetched.append((source, self.hold(array.shape, array.dtype), self.sems(1)))
+        return ("fetch", len(self.fetched) - 1)
+
+    def give(self, shape, dtype, space=pltpu.VMEM):
+        if space == pltpu.HBM:
+            self.shapes.append(pltpu.HBM(shape, dtype))
+        else:
+            self.shapes.append(jax.ShapeDtypeStruct(shape, dtype))
+        self.places.append(pl.BlockSpec(memory_space=space))
         return ("out", len(self.shapes) - 1)
+
+    def keep(self, shape, dtype, parts=1):
+        target = self.give(shape, dtype, pltpu.HBM)
+        self.kept.append((target, self.hold(shape, dtype), self.sems(parts)))
+        return ("keep", len(self.kept) - 1)
 
     def hold(self, shape, dtype):
         self.scratch.append(pltpu.VMEM(shape, dtype))
@@ -39,23 +62,56 @@
         self.scratch.append(pltpu.SemaphoreType.DMA((count,)))
         return ("tmp", len(self.scratch) - 1)
 
+    def save(self, get, handle, row=None):
+        target, room, sems = (get(part) for part in self.kept[handle[1]])
+        if row is not None:
+            target, room = target.at[row], room.at[row]
+        count = sum(1 for known, unused in self.saves if known == handle)
+        copy = pltpu.make_async_copy(room, target, sems.at[count])
+        copy.start()
+        self.saves.append((handle, copy))
+
     def run(self, body, name, collective=None, flops=0):
         ins, outs = len(self.arrays), len(self.shapes)
 
         def kernel(*refs):
             parts = {"in": refs[:ins], "out": refs[ins : ins + outs], "tmp": refs[ins + outs :]}
-            body(lambda handle: parts[handle[0]][handle[1]])
-
+            here, self.saves = set(), []
+
+            def get(handle):
+                kind, i = handle
+                if kind == "keep":
+                    return get(self.kept[i][1])
+                if kind != "fetch":
+                    return parts[kind][i]
+                source, room, sem = (get(part) for part in self.fetched[i])
+                if i not in here:
+                    here.add(i)
+                    pltpu.make_async_copy(source, room, sem.at[0]).wait()
+                return room
+
+            for source, room, sem in self.fetched:
+                pltpu.make_async_copy(get(source), get(room), get(sem).at[0]).start()
+            body(get)
+            for i in range(len(self.fetched)):
+                get(("fetch", i))
+            for handle, copy in self.saves:
+                copy.wait()
+
+        held = [a for a, spec in zip(self.arrays, self.specs) if spec.memory_space == pltpu.VMEM]
+        held += [a for a, spec in zip(self.shapes, self.places) if spec.memory_space == pltpu.VMEM]
+        held += [x for x in self.scratch if x.dtype in (BF16, F32)]
+        room = sum(math.prod(x.shape) * jnp.dtype(x.dtype).itemsize for x in held)
         return pl.pallas_call(
             kernel,
             out_shape=tuple(self.shapes),
             in_specs=self.specs,
-            out_specs=tuple(pl.BlockSpec(memory_space=pltpu.VMEM) for _ in self.shapes),
+            out_specs=tuple(self.places),
             scratch_shapes=self.scratch,
             compiler_params=pltpu.CompilerParams(
                 collective_id=collective,
                 has_side_effects=collective is not None,
-                vmem_limit_bytes=48 << 20,
+                vmem_limit_bytes=room + (8 << 20),
             ),
             cost_estimate=pl.CostEstimate(flops=flops, bytes_accessed=0, transcendentals=0),
             name=name,
@@ -126,7 +182,7 @@
 
 class Weight:
     def __init__(self, call, packed, first, count):
-        self.source = call.take(packed, pl.ANY)
+        self.source = call.take(packed, pltpu.HBM)
         self.room = call.hold((4, count, 1024), BF16)
         self.sem = call.sems(1)
         self.first, self.count = first, count
@@ -149,11 +205,28 @@
         return get(self.room)[:, first : first + count, :].reshape(4 * count, 1024)
 
 
+class Feed:
+    def __init__(self, call, rows, up, down):
+        self.call, self.rows, self.weights = call, call.fetch(rows), [up, down]
+        self.hidden = call.keep((4, 128, 1024), BF16, 4)
+        self.slope = call.keep((4, 128, 1024), F32, 4)
+
+    def part(self, get, row):
+        up, down = self.weights
+        made, slope = gelu_pair(nt(get(self.rows)[row], up.matrix(get, 0, 256)))
+        made = made.astype(BF16)
+        get(self.hidden)[row] = made
+        get(self.slope)[row] = slope
+        self.call.save(get, self.hidden, row)
+        self.call.save(get, self.slope, row)
+        return nn(made, down.matrix(get, 0, 256))
+
+
 class Job:
     def __init__(self, call, left, mid, right):
-        self.left, self.mid, self.right = left, mid, right
+        self.call, self.left, self.mid, self.right = call, left, mid, right
         if left is not None:
-            self.rows_in = call.take(left[0])
+            self.rows_in = None if isinstance(left, Feed) else call.fetch(left[0])
             self.out_first = call.hold((2, 128, 1024), BF16)
             self.out_edge = call.hold((2, 64, 1024), BF16)
             self.out_late = call.hold((2, 64, 1024), BF16)
@@ -163,12 +236,17 @@
             self.sum_send, self.sum_recv = call.sems(6), call.sems(6)
         self.gathered = None
         if right is not None:
-            self.gathered = call.give((4, 128, 1024), BF16)
+            self.gathered = call.keep((4, 128, 1024), BF16, 4)
             self.row_send, self.row_recv = call.sems(6), call.sems(6)
 
-    def part(self, get, row, half=None):
-        unused, weight, picks = self.left
-        total, column = None, 0
+    def lefts(self):
+        return self.left.weights if isinstance(self.left, Feed) else [self.left[1]]
+
+    def part(self, get, row):
+        if isinstance(self.left, Feed):
+            return self.left.part(get, row)
+        unused, weight, picks, column = self.left
+        total = None
         for first, count in picks:
             width = 4 * count
             left = get(self.rows_in)[row, :, column : column + width]
@@ -242,6 +320,7 @@
 
     def rows_start(self, get, at, normed):
         get(self.gathered)[at["own_row"]] = normed
+        self.call.save(get, self.gathered, at["own_row"])
         self.moves = [
             self.row_copy(get, 0, at["own_row"], 0, at["y"]),
             self.row_copy(get, 1, at["own_row"], 1, at["x"]),
@@ -272,18 +351,35 @@
                 copy.wait_send()
 
 
-def run_stage(call, jobs, weights, name, collective, finish=None, flops=0, core=False, more=None):
+class Extra:
+    def partners(self, at):
+        return []
+
+    def start(self, get, at):
+        return None
+
+    def middle(self, get, at):
+        return None
+
+    def late(self, get, at):
+        return None
+
+    def finish(self, get, at):
+        return None
+
+
+def run_stage(call, jobs, weights, name, collective, finish=None, flops=0, core=False, more=()):
     def body(get):
         at = place()
         for weight in weights:
             weight.start(get)
-        greet(
-            [at["x"], at["y"]]
-            + ([at["core"]] if core else [])
-            + ([at["d"]] if more is not None else [])
-        )
+        partners = [at["x"], at["y"]] + ([at["core"]] if core else [])
+        for extra in more:
+            partners += [p for p in extra.partners(at) if all(p is not q for q in partners)]
+        greet(partners)
         lefts = [job for job in jobs if job.left is not None]
-        rights = [job for job in jobs if job.right is not None and job.right[0] is not None]
+        movers = [job for job in jobs if job.right is not None]
+        rights = [job for job in movers if job.right[0] is not None]
         waited = []
 
         def ready(weight):
@@ -291,59 +387,66 @@
                 weight.wait(get)
                 waited.append(weight)
 
+        def arrived(job, row):
+            call.save(get, job.gathered, row)
+            if job in rights:
+                job.product(get, at, row)
+
         for job in lefts:
-            ready(job.left[1])
+            for weight in job.lefts():
+                ready(weight)
             job.sum_start(get, at)
         for job in lefts:
             job.sum_forward(get, at)
+        for extra in more:
+            extra.middle(get, at)
         for job in jobs:
             normed = job.mid(get, job.sum_end(get) if job.left is not None else None)
             if job.right is not None:
                 job.rows_start(get, at, normed)
-        if more is not None:
-            more.start(get, at)
+        for extra in more:
+            extra.start(get, at)
         for weight in weights:
             ready(weight)
+        for extra in more:
+            extra.late(get, at)
         for job in rights:
             job.product(get, at, at["own_row"])
-        for job in jobs:
-            if job.right is not None:
-                job.rows_forward(get, at)
-        for job in jobs:
-            if job.right is not None:
-                job.moves[3].wait_recv()
-                if job in rights:
-                    job.product(get, at, at["x_row"])
-                job.moves[2].wait_recv()
-                if job in rights:
-                    job.product(get, at, at["y_row"])
-        for job in jobs:
-            if job.right is not None:
-                job.moves[4].wait_recv()
-                job.moves[5].wait_recv()
-                if job in rights:
-                    job.product(get, at, at["d_row"])
+        for job in movers:
+            job.rows_forward(get, at)
+        for job in movers:
+            job.moves[3].wait_recv()
+            arrived(job, at["x_row"])
+            job.moves[2].wait_recv()
+            arrived(job, at["y_row"])
+        for job in movers:
+            job.moves[4].wait_recv()
+            job.moves[5].wait_recv()
+            arrived(job, at["d_row"])
         for job in jobs:
             job.drain()
         if finish is not None:
             finish(get)
-        if more is not None:
-            more.finish()
+        for extra in more:
+            extra.finish(get, at)
 
     return call.run(body, name, collective, flops)
 
 
 class Plain:
     def __init__(self, call, width):
-        self.out = call.give((4, 128, width), BF16)
+        self.call, self.width = call, width
+        self.out = call.keep((4, 128, width), BF16, 4)
 
     def store(self, get, at, row, column, value):
         get(self.out)[row, :, column : column + value.shape[1]] = value.astype(BF16)
+        if column + value.shape[1] == self.width:
+            self.call.save(get, self.out, row)
 
 
 class Shared:
     def __init__(self, call, width, skip=0):
-        self.out = call.give((2, 4, 128, width), BF16)
+        self.call, self.out = call, call.keep((2, 4, 128, width), BF16, 2)
         self.send_sem, self.recv_sem = call.sems(4), call.sems(4)
         self.width, self.skip, self.copies, self.blocks = width, skip, [], 0
 
@@ -365,8 +468,10 @@
             self.copies.append(copy)
 
     def finish(self, get):
+        self.call.save(get, self.out, 0)
         for copy in self.copies:
             copy.wait()
+        self.call.save(get, self.out, 1)
 
 
 def query_and_shared(call, width):
@@ -395,55 +500,45 @@
     return jnp.where(allowed, 0.0, MASKED)
 
 
-def attend_kernel(causal, q_ref, kv_ref, facts_ref, keys_ref, mixed_ref, total_ref, bias):
-    bias[...] = allowed_bias(facts_ref, keys_ref, causal)
-    rows = q_ref.shape[0]
-    half = rows // 2
-
-    def pair_step(pair, carry):
-        lanes = pl.ds(pl.multiple_of(pair * 128, 128), 128)
-        value_lanes = pl.ds(pl.multiple_of(256 + pair * 128, 128), 128)
-        keys, values = kv_ref[:, lanes], kv_ref[:, value_lanes]
-        for block in range(2):
-            queries = q_ref[pl.ds(block * half, half), lanes]
-            mixed = []
-            for head in range(2):
-                picked = jnp.where(lanes_of(head, half), queries * 0.125, 0.0).astype(BF16)
-                scores = nt(keys, picked) + bias[:, block * half : (block + 1) * half]
-                top = jnp.max(scores, 0, keepdims=True)
-                raised = jnp.exp(scores - top)
-                total = jnp.sum(raised, 0, keepdims=True)
-                probs = (raised * (1.0 / total)).astype(BF16)
-                mixed.append(tn(values, probs)[head * HEAD_DIM : (head + 1) * HEAD_DIM])
-                total_ref[pl.ds(pair * 2 + head, 1), block * half : (block + 1) * half] = (
-                    top + jnp.log(total)
-                )
-            mixed = jnp.concatenate(mixed, 0).T
-            mixed_ref[pl.ds(block * half, half), lanes] = mixed.astype(BF16)
-        return carry
-
-    lax.fori_loop(0, 2, pair_step, 0)
-
-
 def attend(queries, key_value, facts, keys, causal):
     rows, width = 512, queries.shape[-1]
-
-    def kernel(*refs):
-        attend_kernel(causal, *refs)
-
-    mixed, total = pl.pallas_call(
-        kernel,
-        out_shape=(
-            jax.ShapeDtypeStruct((rows, width), BF16),
-            jax.ShapeDtypeStruct((8, rows), F32),
-        ),
-        in_specs=[pl.BlockSpec(memory_space=pltpu.VMEM)] * 4,
-        out_specs=(pl.BlockSpec(memory_space=pltpu.VMEM),) * 2,
-        scratch_shapes=[pltpu.VMEM((1024, rows), F32)],
-        compiler_params=pltpu.CompilerParams(vmem_limit_bytes=48 << 20),
-        cost_estimate=pl.CostEstimate(flops=8 * MICROSECOND, bytes_accessed=0, transcendentals=0),
-        name="attend",
-    )(queries.reshape(rows, width), key_value.reshape(1024, 2 * width), facts, keys)
+    half = rows // 2
+    call = Call()
+    q_in = call.fetch(queries.reshape(rows, width))
+    kv_in = call.fetch(key_value.reshape(1024, 2 * width))
+    facts_in, keys_in = call.take(facts), call.take(keys)
+    mixed_out, total_out = call.keep((rows, width), BF16, 2), call.give((8, rows), F32)
+    bias = call.hold((1024, rows), F32)
+
+    def body(get):
+        mask = get(bias)
+        mask[...] = allowed_bias(get(facts_in), get(keys_in), causal)
+        q_ref, kv_ref, mixed_ref, total_ref = get(q_in), get(kv_in), get(mixed_out), get(total_out)
+
+        def pair_step(pair, carry):
+            lanes = pl.ds(pl.multiple_of(pair * 128, 128), 128)
+            value_lanes = pl.ds(pl.multiple_of(256 + pair * 128, 128), 128)
+            keys, values = kv_ref[:, lanes], kv_ref[:, value_lanes]
+            for block in range(2):
+                span = slice(block * half, (block + 1) * half)
+                queries = q_ref[span, lanes]
+                mixed = []
+                for head in range(2):
+                    picked = jnp.where(lanes_of(head, half), queries * 0.125, 0.0).astype(BF16)
+                    scores = nt(keys, picked) + mask[:, span]
+                    top = jnp.max(scores, 0, keepdims=True)
+                    raised = jnp.exp(scores - top)
+                    total = jnp.sum(raised, 0, keepdims=True)
+                    probs = (raised * (1.0 / total)).astype(BF16)
+                    mixed.append(tn(values, probs)[head * HEAD_DIM : (head + 1) * HEAD_DIM])
+                    total_ref[pl.ds(pair * 2 + head, 1), span] = top + jnp.log(total)
+                mixed_ref[span, lanes] = jnp.concatenate(mixed, 0).T.astype(BF16)
+            return carry
+
+        lax.fori_loop(0, 2, pair_step, 0)
+        call.save(get, mixed_out)
+
+    mixed, total = call.run(body, "attend", None, 8 * MICROSECOND)
     return mixed.reshape(4, 128, width), total
 
 
@@ -453,12 +548,13 @@
     rows, width = 512, queries.shape[-1]
     half = rows // 2
     call = Call()
-    q_in, kv_in = call.take(queries.reshape(rows, width)), call.take(key_value.reshape(1024, 2 * width))
-    grad_in, total_in = call.take(grad_mixed.reshape(rows, width)), call.take(total)
+    q_in = call.fetch(queries.reshape(rows, width))
+    kv_in = call.fetch(key_value.reshape(1024, 2 * width))
+    grad_in, total_in = call.fetch(grad_mixed.reshape(rows, width)), call.take(total)
     facts_in, keys_in = call.take(facts), call.take(keys)
     for array in done:
-        call.take(array, pl.ANY)
-    grad_out = call.give((rows, 3 * width), BF16)
+        call.take(array, pltpu.HBM)
+    grad_out = call.keep((rows, 3 * width), BF16)
     bias = call.hold((1024, rows), F32)
     gathered = call.hold((1024, 4 * 128), F32)
     outgoing, landed = call.hold((2, 512, 256), BF16), call.hold((2, 512, 256), BF16)
@@ -466,11 +562,11 @@
 
     def body(get):
         at = place()
-        q_ref, kv_ref, grad_ref, total_ref = get(q_in), get(kv_in), get(grad_in), get(total_in)
         out, mask, sums = get(grad_out), get(bias), get(gathered)
         away, here = get(outgoing), get(landed)
         mask[...] = allowed_bias(get(facts_in), get(keys_in), causal)
         greet([at["core"]])
+        q_ref, kv_ref, grad_ref, total_ref = get(q_in), get(kv_in), get(grad_in), get(total_in)
         copies = []
         for pair in range(2):
             lanes = slice(pair * 128, pair * 128 + 128)
@@ -517,71 +613,84 @@
             both = sums[:512, pair * 256 : pair * 256 + 256] + here[pair].astype(F32)
             out[:, width + pair * 128 : width + pair * 128 + 128] = both[:, :128].astype(BF16)
             out[:, 2 * width + pair * 128 : 2 * width + pair * 128 + 128] = both[:, 128:].astype(BF16)
+        call.save(get, grad_out)
 
     (grads,) = call.run(body, "attend_back", collective, 16 * MICROSECOND)
     return grads.reshape(4, 128, 3 * width)
 
 
-def weight_shares(groups, collective):
-    call = Call()
-    plans = []
-    for pairs in groups:
-        count = 256 // len(pairs)
-        handles = [
-            (call.take(left.reshape(512, -1)), column, call.take(right.reshape(512, 1024)))
+class Shares(Extra):
+    def __init__(self, call, pairs, count):
+        self.call, self.count = call, count
+        self.handles = [
+            (call.fetch(left.reshape(512, -1)), column, call.fetch(by_owner(right).reshape(512, 1024)))
             for left, column, right in pairs
         ]
-        made, landed = call.hold((2, 4, 4, 256, 128), BF16), call.hold((4, 4, 256, 128), BF16)
-        send_sem, recv_sem = call.sems(4), call.sems(4)
-        shares = call.give((4, 4, 256, 128), BF16)
-        plans.append((count, handles, made, landed, send_sem, recv_sem, shares))
+        shape = (4, 4, len(pairs) * count, 128)
+        sends = len(pairs) * max(1, count // 64)
+        self.made, self.landed = call.hold((2,) + shape, BF16), call.hold(shape, BF16)
+        self.send_sem, self.recv_sem = call.sems(sends), call.sems(sends)
+        self.out = call.keep(shape, BF16)
+
+    def partners(self, at):
+        return [at["core"]]
+
+    def send(self, get, at, part):
+        i = len(self.copies)
+        copy = pltpu.make_async_remote_copy(
+            src_ref=get(self.made).at[(1 - lax.axis_index("c"),) + part],
+            dst_ref=get(self.landed).at[part],
+            send_sem=get(self.send_sem).at[i],
+            recv_sem=get(self.recv_sem).at[i],
+            device_id=at["core"],
+            device_id_type=MESH_ID,
+        )
+        copy.start()
+        self.copies.append((part, copy))
+
+    def middle(self, get, at):
+        self.copies, every, count = [], slice(None), self.count
+        made = get(self.made)
+        for m, (left, column, right) in enumerate(self.handles):
+            left, right = get(left), get(right)
+            span = slice(m * count, (m + 1) * count)
+            for first in range(0, 4 * count, 256):
+                product = tn(left[:, column + first : column + first + 256], right[...])
+                for inner in range(0, 256, count):
+                    z = (first + inner) // count
+                    for d in range(8):
+                        made[d % 2, z, d // 2, span, :] = product[
+                            inner : inner + count, d * 128 : d * 128 + 128
+                        ].astype(BF16)
+                if count == 256:
+                    self.send(get, at, (first // 256, every, pl.ds(m * count, count)))
+            if count < 256:
+                self.send(get, at, (every, every, pl.ds(m * count, count)))
+
+    def finish(self, get, at):
+        core = lax.axis_index("c")
+        for part, copy in self.copies:
+            copy.wait()
+            own = get(self.made)[(core,) + part].astype(F32)
+            get(self.out)[part] = (own + get(self.landed)[part].astype(F32)).astype(BF16)
+        self.call.save(get, self.out)
+
+
+def weight_shares(pairs, count, collective):
+    call = Call()
+    shares = Shares(call, pairs, count)
 
     def body(get):
         at = place()
-        core = lax.axis_index("c")
         greet([at["core"]])
-        copies = []
-
-        def send(plan, i, part):
-            made, landed, send_sem, recv_sem = (get(handle) for handle in plan[2:6])
-            copy = pltpu.make_async_remote_copy(
-                src_ref=made.at[(1 - core,) + part],
-                dst_ref=landed.at[part],
-                send_sem=send_sem.at[i],
-                recv_sem=recv_sem.at[i],
-                device_id=at["core"],
-                device_id_type=MESH_ID,
-            )
-            copy.start()
-            copies.append((plan, part, copy))
-
-        for plan in plans:
-            count, handles, made = plan[0], plan[1], get(plan[2])
-            for m, (left, column, right) in enumerate(handles):
-                left, right = get(left), get(right)
-                for first in range(0, 4 * count, 256):
-                    product = tn(left[:, column + first : column + first + 256], right[...])
-                    for inner in range(0, 256, count):
-                        z = (first + inner) // count
-                        for d in range(8):
-                            made[d % 2, z, d // 2, m * count : (m + 1) * count, :] = product[
-                                inner : inner + count, d * 128 : d * 128 + 128
-                            ].astype(BF16)
-                    if count == 256:
-                        send(plan, z, (z,))
-                if count < 256:
-                    every = slice(None)
-                    send(plan, m, (every, every, pl.ds(m * count, count)))
-        for plan, part, copy in copies:
-            copy.wait()
-            made, landed, shares = get(plan[2]), get(plan[3]), get(plan[6])
-            own = made[(core,) + part].astype(F32)
-            shares[part] = (own + landed[part].astype(F32)).astype(BF16)
-
-    return call.run(body, "weight_shares", collective, 4 * len(groups) * MICROSECOND)
-
-
-class Swap:
+        shares.middle(get, at)
+        shares.finish(get, at)
+
+    (made,) = call.run(body, "weight_shares", collective, len(pairs) * count // 64 * MICROSECOND)
+    return made
+
+
+class Swap(Extra):
     def __init__(self, call, packs):
         self.packs = [call.take(pack) for pack in packs]
         self.outs = [call.give(pack.shape, pack.dtype) for pack in packs]
@@ -611,12 +720,20 @@
                 self.copies.append(copy)
             out[own] = pack[own]
 
-    def finish(self):
+    def partners(self, at):
+        return [at["x"], at["y"], at["d"]]
+
+    def finish(self, get, at):
         for copy in self.copies:
             copy.wait()
 
 
-class Slots:
+class Local(Extra):
+    def __init__(self, work):
+        self.late = work
+
+
+class Slots(Extra):
     def __init__(self, call, arrays, inward):
         self.inward = inward
         self.arrays = [call.take(array) for array in arrays]
@@ -626,29 +743,36 @@
 
     def ends(self, get, at, j, step):
         z = at["mesh"][4]
-        odd = lax.rem(z, 2)
-        other = odd if step == 0 else 1 - odd
+        low = lax.div(z, 2)
+        other = low if step == 0 else 1 - low
         array, out = get(self.arrays[j]), get(self.outs[j])
         if self.inward:
-            return array.at[other], out.at[pl.ds(pl.multiple_of(odd * 64, 64), 64)]
-        return array.at[pl.ds(pl.multiple_of(other * 64, 64), 64)], out.at[odd]
+            return array.at[other], out.at[pl.ds(pl.multiple_of(low * 64, 64), 64)]
+        return array.at[pl.ds(pl.multiple_of(other * 64, 64), 64)], out.at[low]
+
+    def partners(self, at):
+        return all_partners(at)[1]
+
+    def stays(self, at):
+        hi, z = at["mesh"][0], at["mesh"][4]
+        return lax.rem(z, 2) == hi
 
     def copy(self, get, at, j, step):
         hi, k, y, c, z = at["mesh"]
-        odd = lax.rem(z, 2)
+        low = lax.div(z, 2)
+        partner = (lax.rem(z, 2), k, y, c, 2 * (low if step == 0 else 1 - low) + hi)
         source, target = self.ends(get, at, j, step)
         return pltpu.make_async_remote_copy(
             src_ref=source,
             dst_ref=target,
             send_sem=get(self.send_sem).at[2 * j + step],
             recv_sem=get(self.recv_sem).at[2 * j + step],
-            device_id=(lax.div(z, 2), k, y, c, 2 * hi + (odd if step == 0 else 1 - odd)),
+            device_id=partner,
             device_id_type=MESH_ID,
         )
 
     def start(self, get, at):
-        hi, z = at["mesh"][0], at["mesh"][4]
-        stays = lax.div(z, 2) == hi
+        stays = self.stays(at)
         for j in range(len(self.arrays)):
             self.copy(get, at, j, 1).start()
 
@@ -664,11 +788,10 @@
                 target[...] = source[...]
 
     def finish(self, get, at):
-        hi, z = at["mesh"][0], at["mesh"][4]
         for j in range(len(self.arrays)):
             self.copy(get, at, j, 1).wait()
 
-        @pl.when(lax.div(z, 2) != hi)
+        @pl.when(jnp.logical_not(self.stays(at)))
         def _():
             for j in range(len(self.arrays)):
                 self.copy(get, at, j, 0).wait()
@@ -741,7 +864,7 @@
             copy.wait()
         fact_copy.wait()
         slots.finish(get, at)
-        swap.finish()
+        swap.finish(get, at)
 
     outs = call.run(body, "open_program", 13, 12 * MICROSECOND)
     n, m = len(rows), len(packs)
@@ -803,7 +926,7 @@
             copy.wait()
         get(vec_out)[...] = get(block_sum)[...] + get(along)[0] + get(along)[1] + get(along)[2]
         slots.finish(get, at)
-        swap.finish()
+        swap.finish(get, at)
 
     outs = call.run(body, "close_program", 14, 16 * MICROSECOND)
     n, m = len(rows), len(packs)
@@ -818,7 +941,7 @@
         at = place()
         greet([at["x"], at["y"], at["d"]])
         swap.start(get, at)
-        swap.finish()
+        swap.finish(get, at)
 
     return call.run(body, "swap_packs", collective, 5 * MICROSECOND)
 
@@ -876,7 +999,7 @@
 
 def row_order(values):
     c = lax.axis_index("c")
-    split = values.reshape(2, 2, values.shape[0] // 4)
+    split = values.reshape(2, 2, 2, 2, values.shape[0] // 16).swapaxes(2, 3)
     own = jnp.where(c == 0, split[:, 0], split[:, 1]).reshape(-1)
     other = jnp.where(c == 0, split[:, 1], split[:, 0]).reshape(-1)
     return own, jnp.concatenate([own, other])
@@ -919,21 +1042,23 @@
         0,
     )
     facts = jnp.concatenate([facts.reshape(-1, 128), jnp.zeros((4, 128), jnp.int32)], 0)
-    enc_p = widen(pack_rows([*transposed(enc_qkv), enc_proj]))
-    self_p = widen(pack_rows([*transposed(dec_qkv), dec_proj]))
-    cross_p = widen(pack_rows([*transposed(cross_qkv), cross_proj]))
-    enc_up_p, enc_down_p = widen(pack_rows([enc_up.T])), widen(pack_rows([enc_down]))
-    dec_up_p, dec_down_p = widen(pack_rows([dec_up.T])), widen(pack_rows([dec_down]))
-
-    (stream_in, target_in, grad_out), (enc_p, self_p), vectors, facts = open_program(
-        [source, target, cotangent], vectors, facts, [enc_p, self_p]
+    first_p = widen(
+        pack_rows([*transposed(enc_qkv), enc_proj, *transposed(dec_qkv), dec_proj])
+    )
+    second_p = jnp.concatenate(
+        [pack_rows([*transposed(cross_qkv), cross_proj]), pack_rows([enc_up.T, enc_down])], 1
+    )
+    second_p, third_p = widen(second_p), widen(pack_rows([dec_up.T, dec_down]))
+
+    (stream_in, target_in), (first_p,), vectors, facts = open_program(
+        [source, target], vectors, facts, [first_p]
     )
     if copies > 1:
         vectors = vectors.reshape(16, 2, 2, 2, 4, copies, 32 // copies)
         vectors = vectors.transpose(0, 1, 5, 2, 3, 4, 6).reshape(16, 1024)
-    enc_w, self_w = gather_weights(enc_p), gather_weights(self_p)
-    near = jnp.where(lax.axis_index("hi") == z // 2, facts[0], facts[1])[:36].reshape(2, 2, 1152)
-    near = jnp.where(z % 2 == 0, near[:, 0], near[:, 1])
+    first_w = gather_weights(first_p)
+    near = jnp.where(lax.axis_index("hi") == z % 2, facts[0], facts[1])[:36].reshape(2, 2, 1152)
+    near = jnp.where(z < 2, near[:, 0], near[:, 1])
     source_length, source_ids = near[0, 1024], near[0, :1024]
     target_length, target_ids = near[1, 1024], near[1, :1024]
     place_own, place_all = row_order(jnp.arange(source_ids.shape[0]))
@@ -952,60 +1077,55 @@
     target_keys = key_facts(target_all, target_length)
 
     ENC_G, ENC_B, DEC_G, DEC_B = 0, 3, 6, 10
-    Q, K, V, O = (0, 64), (64, 64), (128, 64), (192, 64)
-    ALL = (0, 256)
+    SELF, CROSS = 256, 0
+    Q, QKV, KV, O = (0, 64), (0, 192), (64, 128), (192, 64)
+    ENC_UP, ENC_DOWN, DEC_UP, DEC_DOWN = (256, 256), (512, 256), (0, 256), (256, 256)
+
+    def pick(call, packed, span, base=0):
+        return Weight(call, packed, base + span[0], span[1])
 
     def forward_mid(call, residual, gain, shift):
-        vec, res = call.take(vectors), call.take(residual)
-        kept = call.give((128, 1024), F32)
+        vec, res = call.take(vectors), call.fetch(residual)
+        kept = call.keep((128, 1024), F32)
 
         def mid(get, total):
             stream = get(res)[...].astype(F32) + total
             get(kept)[...] = stream
+            call.save(get, kept)
             unit, scale = unit_of(stream)
             return (unit * get(vec)[gain : gain + 1] + get(vec)[shift : shift + 1]).astype(BF16)
 
         return mid
 
     def backward_mid(call, stream, gain, residual=None):
-        vec, kept = call.take(vectors), call.take(stream)
-        res = None if residual is None else call.take(residual)
-        grad_out, share_out = call.give((128, 1024), F32), call.give((2, 1024), F32)
+        vec, kept = call.take(vectors), call.fetch(stream)
+        res = None if residual is None else call.fetch(residual)
+        grad_out, share_out = call.keep((128, 1024), F32), call.give((2, 1024), F32)
 
         def mid(get, total):
             grad, shares = norm_back(get(kept)[...].astype(F32), get(vec)[gain : gain + 1], total)
             if res is not None:
                 grad = grad + get(res)[...]
             get(grad_out)[...] = grad
+            call.save(get, grad_out)
             get(share_out)[...] = shares
             return grad.astype(BF16)
 
         return mid
 
-    def activated(call):
-        hidden = call.give((4, 128, 1024), BF16)
-        slope = call.give((4, 128, 1024), F32)
+    def deactivated(call, slope):
+        out = call.keep((4, 128, 1024), BF16, 4)
 
         def store(get, at, row, column, value):
-            made, slopes = gelu_pair(value)
-            get(hidden)[row, :, column : column + value.shape[1]] = made.astype(BF16)
-            get(slope)[row, :, column : column + value.shape[1]] = slopes
+            get(out)[row] = (value * get(slope)[row]).astype(BF16)
+            call.save(get, out, row)
 
         return store
 
-    def deactivated(call, slope):
-        kept, out = call.take(slope), call.give((4, 128, 1024), BF16)
-
-        def store(get, at, row, column, value):
-            span = slice(column, column + value.shape[1])
-            get(out)[row, :, span] = (value * get(kept)[row, :, span]).astype(BF16)
-
-        return store
-
     call = Call()
 
     def first_mid(stream, gain, shift):
-        vec, res = call.take(vectors), call.take(stream)
+        vec, res = call.take(vectors), call.fetch(stream)
 
         def mid(get, total):
             unit, scale = unit_of(get(res)[...].astype(F32))
@@ -1016,26 +1136,27 @@
     jobs = []
     for stream, gain, shift in ((stream_in, ENC_G, ENC_B), (target_in, DEC_G, DEC_B)):
         jobs.append(Job(call, None, first_mid(stream, gain, shift), (None, None, None)))
-    swap = Swap(call, [enc_up_p, cross_p, enc_down_p, dec_up_p, dec_down_p])
-    outs = run_stage(call, jobs, [], "first_rows", 0, flops=30 * MICROSECOND, more=swap)
-    rows_a, rows_c = outs[:2]
-    enc_up_w, cross_w, enc_down_w, dec_up_w, dec_down_w = (
-        gather_weights(packed) for packed in outs[2:]
-    )
+    swap = Swap(call, [second_p])
+    rows_a, rows_c, second_p = run_stage(
+        call, jobs, [], "first_rows", 0, flops=24 * MICROSECOND, more=[swap]
+    )
+    second_w = gather_weights(second_p)
 
     call = Call()
     made, finishes, plans = [], [], []
-    for rows, packed in ((rows_a, enc_w), (rows_c, self_w)):
-        weight = Weight(call, packed, 0, 192)
+    swap = Swap(call, [third_p])
+    for rows, base in ((rows_a, 0), (rows_c, SELF)):
+        weight = pick(call, first_w, QKV, base)
         store, finish = query_and_shared(call, 256)
-        plans.append((call.take(rows), weight, store))
+        plans.append((call.fetch(rows), weight, store))
         finishes.append(finish)
 
     def project(get):
         at = place()
         for unused, weight, unused2 in plans:
             weight.start(get)
-        greet([at["core"]])
+        greet([at["core"]] + swap.partners(at))
+        swap.start(get, at)
         for rows, weight, store in plans:
             weight.wait(get)
             for row in range(4):
@@ -1045,63 +1166,64 @@
                     )
         for finish in finishes:
             finish(get)
-
-    enc_q, enc_kv, self_q, self_kv = call.run(project, "project", 1, 6 * MICROSECOND)
+        swap.finish(get, at)
+
+    third_p, enc_q, enc_kv, self_q, self_kv = call.run(project, "project", 1, 8 * MICROSECOND)
+    third_w = gather_weights(third_p)
 
     enc_mixed, enc_total = attend(enc_q, enc_kv, source_facts, source_keys, False)
     self_mixed, self_total = attend(self_q, self_kv, target_facts, target_keys, True)
 
     call = Call()
-    enc_o, enc_u = Weight(call, enc_w, *O), Weight(call, enc_up_w, *ALL)
-    self_o, cross_a = Weight(call, self_w, *O), Weight(call, cross_w, *Q)
-    mid_b = forward_mid(call, stream_in, ENC_G + 1, ENC_B + 1)
-    job_b = Job(call, (enc_mixed, enc_o, [(0, 64)]), mid_b, (enc_u, [(0, 256)], activated(call)))
-    mid_d = forward_mid(call, target_in, DEC_G + 1, DEC_B + 1)
-    job_d = Job(call, (self_mixed, self_o, [(0, 64)]), mid_d, (cross_a, [(0, 64)], None))
-    query = Plain(call, 256)
-    job_d.right = (cross_a, [(0, 64)], query.store)
-    (
-        stream_mid,
-        enc_hidden,
-        enc_slope,
-        rows_b,
-        target_mid,
-        rows_d,
-        cross_q,
-    ) = run_stage(
+    enc_o, self_o = pick(call, first_w, O), pick(call, first_w, O, SELF)
+    mid = forward_mid(call, stream_in, ENC_G + 1, ENC_B + 1)
+    job_b = Job(call, (enc_mixed, enc_o, [(0, 64)], 0), mid, (None, None, None))
+    mid = forward_mid(call, target_in, DEC_G + 1, DEC_B + 1)
+    job_d = Job(call, (self_mixed, self_o, [(0, 64)], 0), mid, (None, None, None))
+    stream_mid, rows_b, target_mid, rows_d = run_stage(
+        call, [job_b, job_d], [enc_o, self_o], "after_self", 2, flops=34 * MICROSECOND
+    )
+
+    call = Call()
+    enc_u, enc_d = pick(call, second_w, ENC_UP), pick(call, second_w, ENC_DOWN)
+    cross_a, cross_b = pick(call, second_w, Q), pick(call, second_w, KV)
+    feed = Feed(call, rows_b, enc_u, enc_d)
+    mid = forward_mid(call, stream_mid, ENC_G + 2, ENC_B + 2)
+    shared, query, rows_in = Shared(call, 512), Plain(call, 256), call.fetch(rows_d)
+    job = Job(call, feed, mid, (cross_b, [(0, 64), (64, 64)], shared.store))
+
+    def queries(get, at):
+        for row in range(4):
+            query.store(get, at, row, 0, nt(get(rows_in)[row], cross_a.matrix(get, 0, 64)))
+
+    enc_hidden, enc_slope, stream_end, cross_kv, cross_q, memory = run_stage(
         call,
-        [job_b, job_d],
-        [enc_o, self_o, enc_u, cross_a],
-        "after_self",
-        2,
-        flops=32 * MICROSECOND,
-    )
-
-    call = Call()
-    enc_d, cross_b = Weight(call, enc_down_w, *ALL), Weight(call, cross_w, 64, 128)
-    mid_m = forward_mid(call, stream_mid, ENC_G + 2, ENC_B + 2)
-    shared = Shared(call, 512)
-    job = Job(
-        call, (enc_hidden, enc_d, [(0, 256)]), mid_m, (cross_b, [(0, 64), (64, 64)], shared.store)
-    )
-    stream_end, cross_kv, memory = run_stage(
-        call, [job], [enc_d, cross_b], "memory", 3, shared.finish, 20 * MICROSECOND, core=True
+        [job],
+        [enc_u, enc_d, cross_a, cross_b],
+        "memory",
+        3,
+        shared.finish,
+        24 * MICROSECOND,
+        core=True,
+        more=[Local(queries)],
     )
 
     cross_mixed, cross_total = attend(cross_q, cross_kv, target_facts, source_keys, False)
 
     call = Call()
-    cross_o, dec_u = Weight(call, cross_w, *O), Weight(call, dec_up_w, *ALL)
-    mid_e = forward_mid(call, target_mid, DEC_G + 2, DEC_B + 2)
-    job = Job(call, (cross_mixed, cross_o, [(0, 64)]), mid_e, (dec_u, [(0, 256)], activated(call)))
-    target_late, dec_hidden, dec_slope, rows_e = run_stage(
-        call, [job], [cross_o, dec_u], "after_cross", 4, flops=20 * MICROSECOND
-    )
-
-    call = Call()
-    dec_d = Weight(call, dec_down_w, *ALL)
-    vec, res, cot = call.take(vectors), call.take(target_late), call.take(grad_out)
-    decoded_out, grad_end_out = call.give((128, 1024), BF16), call.give((128, 1024), F32)
+    cross_o = pick(call, second_w, O)
+    mid = forward_mid(call, target_mid, DEC_G + 2, DEC_B + 2)
+    slots = Slots(call, [cotangent], True)
+    job = Job(call, (cross_mixed, cross_o, [(0, 64)], 0), mid, (None, None, None))
+    target_late, grad_out, rows_e = run_stage(
+        call, [job], [cross_o], "after_cross", 4, flops=20 * MICROSECOND, more=[slots]
+    )
+
+    call = Call()
+    dec_u, dec_d = pick(call, third_w, DEC_UP), pick(call, third_w, DEC_DOWN)
+    feed = Feed(call, rows_e, dec_u, dec_d)
+    vec, res, cot = call.take(vectors), call.fetch(target_late), call.fetch(grad_out)
+    decoded_out, grad_end_out = call.keep((128, 1024), BF16), call.keep((128, 1024), F32)
     share_out = call.give((2, 1024), F32)
 
     def last_mid(get, total):
@@ -1112,29 +1234,25 @@
         grad, shares = norm_back(stream, gain, get(cot)[...].astype(F32))
         get(grad_end_out)[...] = grad
         get(share_out)[...] = shares
+        call.save(get, decoded_out)
+        call.save(get, grad_end_out)
         return grad.astype(BF16)
 
-    job = Job(
-        call,
-        (dec_hidden, dec_d, [(0, 256)]),
-        last_mid,
-        (dec_d, [(0, 256)], deactivated(call, dec_slope)),
-    )
-    decoded, grad_end, norm_3, dec_grad_act, grad_rows_e = run_stage(
-        call, [job], [dec_d], "turn", 5, flops=20 * MICROSECOND
-    )
-    dec_up_s, dec_down_s = weight_shares(
-        [[(dec_grad_act, 0, by_owner(rows_e))], [(dec_hidden, 0, by_owner(grad_rows_e))]], 15
-    )
-    dec_up_g, dec_down_g = over_slots(dec_up_s), over_slots(dec_down_s)
-
-    call = Call()
-    call.take(dec_up_s, pl.ANY)
-    call.take(dec_down_s, pl.ANY)
-    dec_u, cross_o = Weight(call, dec_up_w, *ALL), Weight(call, cross_w, *O)
+    job = Job(call, feed, last_mid, (dec_d, [(0, 256)], deactivated(call, feed.slope)))
+    dec_hidden, dec_slope, decoded, grad_end, norm_3, dec_grad_act, grad_rows_e = run_stage(
+        call, [job], [dec_u, dec_d], "turn", 5, flops=24 * MICROSECOND
+    )
+    dec_s = weight_shares(
+        [(dec_grad_act, 0, rows_e), (dec_hidden, 0, grad_rows_e)], 256, 15
+    )
+    dec_g = over_slots(dec_s)
+
+    call = Call()
+    call.take(dec_s, pltpu.HBM)
+    dec_u, cross_o = pick(call, third_w, DEC_UP), pick(call, second_w, O)
     mid = backward_mid(call, target_late, DEC_G + 2, grad_end)
     query = Plain(call, 256)
-    job = Job(call, (dec_grad_act, dec_u, [(0, 256)]), mid, (cross_o, [(0, 64)], query.store))
+    job = Job(call, (dec_grad_act, dec_u, [(0, 256)], 0), mid, (cross_o, [(0, 64)], query.store))
     grad_late, norm_2, cross_grad_mixed, grad_rows_d = run_stage(
         call, [job], [dec_u, cross_o], "back_cross", 6, flops=20 * MICROSECOND
     )
@@ -1142,37 +1260,37 @@
     cross_grads = attend_back(
         cross_q, cross_kv, cross_grad_mixed, cross_total, target_facts, source_keys, False, 7
     )
-    memory_o, rows_o = by_owner(memory), by_owner(rows_d)
-    (cross_s,) = weight_shares(
+    cross_s = weight_shares(
         [
-            [
-                (cross_grads, 0, rows_o),
-                (cross_grads, 256, memory_o),
-                (cross_grads, 512, memory_o),
-                (cross_mixed, 0, by_owner(grad_rows_d)),
-            ]
+            (cross_grads, 0, rows_d),
+            (cross_grads, 256, memory),
+            (cross_grads, 512, memory),
+            (cross_mixed, 0, grad_rows_d),
         ],
+        64,
         16,
     )
     cross_g = over_slots(cross_s)
 
     call = Call()
-    call.take(cross_s, pl.ANY)
-    cross_a, cross_b = Weight(call, cross_w, *Q), Weight(call, cross_w, 64, 128)
-    self_o, enc_d = Weight(call, self_w, *O), Weight(call, enc_down_w, *ALL)
+    call.take(cross_s, pltpu.HBM)
+    cross_a, cross_b = pick(call, second_w, Q), pick(call, second_w, KV)
+    self_o, enc_d = pick(call, first_w, O, SELF), pick(call, second_w, ENC_DOWN)
+    slots = Slots(call, [decoded], False)
     mid = backward_mid(call, target_mid, DEC_G + 1, grad_late)
     query = Plain(call, 256)
     job_t = Job(
-        call, (cross_grads[:, :, :256], cross_a, [(0, 64)]), mid, (self_o, [(0, 64)], query.store)
+        call, (cross_grads, cross_a, [(0, 64)], 0), mid, (self_o, [(0, 64)], query.store)
     )
     mid = backward_mid(call, stream_end, ENC_G + 2)
     job_s = Job(
         call,
-        (cross_grads[:, :, 256:], cross_b, [(0, 64), (64, 64)]),
+        (cross_grads, cross_b, [(0, 64), (64, 64)], 256),
         mid,
-        (enc_d, [(0, 256)], deactivated(call, enc_slope)),
+        (enc_d, [(0, 256)], deactivated(call, call.fetch(enc_slope))),
     )
     (
+        decoded,
         grad_mid,
         norm_1,
         self_grad_mixed,
@@ -1187,40 +1305,38 @@
         [cross_a, cross_b, self_o, enc_d],
         "back_both",
         8,
-        flops=32 * MICROSECOND,
-    )
-    enc_up_s, enc_down_s = weight_shares(
-        [[(enc_grad_act, 0, by_owner(rows_b))], [(enc_hidden, 0, by_owner(grad_rows_b))]], 17
-    )
-    enc_up_g, enc_down_g = over_slots(enc_up_s), over_slots(enc_down_s)
+        flops=38 * MICROSECOND,
+        more=[slots],
+    )
+    feed_s = weight_shares(
+        [(enc_grad_act, 0, rows_b), (enc_hidden, 0, grad_rows_b)], 256, 17
+    )
+    feed_g = over_slots(feed_s)
 
     self_grads = attend_back(
-        self_q, self_kv, self_grad_mixed, self_total, target_facts, target_keys, True, 9, [enc_up_s, enc_down_s]
-    )
-    rows_o = by_owner(rows_c)
-    (self_s,) = weight_shares(
+        self_q, self_kv, self_grad_mixed, self_total, target_facts, target_keys, True, 9, [feed_s]
+    )
+    call = Call()
+    call.take(dec_g, pltpu.HBM)
+    shares = Shares(
+        call,
         [
-            [
-                (self_grads, 0, rows_o),
-                (self_grads, 256, rows_o),
-                (self_grads, 512, rows_o),
-                (self_mixed, 0, by_owner(grad_rows_c)),
-            ]
+            (self_grads, 0, rows_c),
+            (self_grads, 256, rows_c),
+            (self_grads, 512, rows_c),
+            (self_mixed, 0, grad_rows_c),
         ],
-        18,
-    )
-    self_g = over_slots(self_s)
-
-    call = Call()
-    for done in (self_s, dec_up_g, dec_down_g):
-        call.take(done, pl.ANY)
-    enc_u, enc_o, self_a = Weight(call, enc_up_w, *ALL), Weight(call, enc_w, *O), Weight(call, self_w, 0, 192)
+        64,
+    )
+    enc_u, enc_o = pick(call, second_w, ENC_UP), pick(call, first_w, O)
+    self_a = pick(call, first_w, QKV, SELF)
     mid = backward_mid(call, stream_mid, ENC_G + 1, grad_stream)
     query = Plain(call, 256)
-    job_s = Job(call, (enc_grad_act, enc_u, [(0, 256)]), mid, (enc_o, [(0, 64)], query.store))
+    job_s = Job(call, (enc_grad_act, enc_u, [(0, 256)], 0), mid, (enc_o, [(0, 64)], query.store))
     mid = backward_mid(call, target_in, DEC_G, grad_mid)
-    job_t = Job(call, (self_grads, self_a, [(0, 64), (64, 64), (128, 64)]), mid, None)
+    job_t = Job(call, (self_grads, self_a, [(0, 64), (64, 64), (128, 64)], 0), mid, None)
     (
+        self_s,
         grad_stream,
         enc_norm_1,
         enc_grad_mixed,
@@ -1228,32 +1344,37 @@
         target_grad,
         norm_0,
     ) = run_stage(
-        call, [job_s, job_t], [enc_u, self_a, enc_o], "back_self", 10, flops=28 * MICROSECOND
-    )
+        call,
+        [job_s, job_t],
+        [enc_u, self_a, enc_o],
+        "back_self",
+        10,
+        flops=28 * MICROSECOND,
+        more=[shares],
+    )
+    self_g = over_slots(self_s)
 
     enc_grads = attend_back(
         enc_q, enc_kv, enc_grad_mixed, enc_total, source_facts, source_keys, False, 11, [cross_g]
     )
-    rows_o = by_owner(rows_a)
-    (enc_s,) = weight_shares(
+    enc_s = weight_shares(
         [
-            [
-                (enc_grads, 0, rows_o),
-                (enc_grads, 256, rows_o),
-                (enc_grads, 512, rows_o),
-                (enc_mixed, 0, by_owner(grad_rows_a)),
-            ]
+            (enc_grads, 0, rows_a),
+            (enc_grads, 256, rows_a),
+            (enc_grads, 512, rows_a),
+            (enc_mixed, 0, grad_rows_a),
         ],
+        64,
         19,
     )
     enc_g = over_slots(enc_s)
 
     call = Call()
-    for done in (enc_s, enc_up_g, enc_down_g):
-        call.take(done, pl.ANY)
-    enc_a = Weight(call, enc_w, 0, 192)
+    for done in (enc_s, feed_g):
+        call.take(done, pltpu.HBM)
+    enc_a = pick(call, first_w, QKV)
     mid = backward_mid(call, stream_in, ENC_G, grad_stream)
-    job = Job(call, (enc_grads, enc_a, [(0, 64), (64, 64), (128, 64)]), mid, None)
+    job = Job(call, (enc_grads, enc_a, [(0, 64), (64, 64), (128, 64)], 0), mid, None)
     source_grad, enc_norm_0 = run_stage(
         call, [job], [enc_a], "back_first", 12, flops=12 * MICROSECOND
     )
@@ -1269,10 +1390,10 @@
         ],
         0,
     )
-    (decoded, source_grad, target_grad), swapped, norm_grad = close_program(
-        [decoded, source_grad.astype(BF16), target_grad.astype(BF16)],
+    (source_grad, target_grad), swapped, norm_grad = close_program(
+        [source_grad.astype(BF16), target_grad.astype(BF16)],
         by_owner(norm_share),
-        [dec_up_g, dec_down_g, cross_g, enc_up_g, enc_down_g, self_g],
+        [dec_g, cross_g, feed_g, self_g],
     )
     norm_grad = norm_grad.reshape(16, copies, 4, 32 // copies)
     if copies > 1:
@@ -1285,14 +1406,15 @@
         grads = unpack(narrow(packed), 4)
         return jnp.swapaxes(grads[:3], 1, 2), grads[3]
 
-    def feed_share(packed):
-        return unpack(narrow(packed), 1)[0]
-
-    dec_u, dec_d, enc_u, enc_d = (feed_share(swapped[i]) for i in (0, 1, 3, 4))
-    dec_u, enc_u = dec_u.T, enc_u.T
+    def feed_shares(packed):
+        grads = unpack(narrow(packed), 2)
+        return grads[0].T, grads[1]
+
+    dec_u, dec_d = feed_shares(swapped[0])
+    enc_u, enc_d = feed_shares(swapped[2])
     enc_a, enc_o = attend_shares(enc_g)
-    cross_a, cross_o = attend_shares(swapped[2])
-    self_a, self_o = attend_shares(swapped[5])
+    cross_a, cross_o = attend_shares(swapped[1])
+    self_a, self_o = attend_shares(swapped[3])
     return (
         decoded,
         source_grad.astype(F32),

time: 597 us -> 506 us (0.85)
  waiting for transfers between devices: 52.5 us -> 10.1 us
  local copies, waits for them, and re-layouts: 64.1 us -> 23.8 us
  Pallas kernels: 452 us -> 445 us
    unnamed x218 -> x86, local copies, waits for them, and re-layouts: 51.9 us -> 12 us
    all_gather x7 -> x3, waiting for transfers between devices: 48.2 us -> 8.4 us  [gather_weights(): packed = lax.all_gather(packed, ('c', 'mp')).reshape(2, 4, 4, rows, 128)]
    pallas_call x3 -> x0, Pallas kernels: 23.2 us -> none  [attend(): pl.pallas_call(kernel, out_shape=(jax.ShapeDtypeStruct((rows, width), BF1...]
    pallas_call x21 -> x23, Pallas kernels: 428 us -> 445 us  [run(): pl.pallas_call(kernel, out_shape=tuple(self.shapes), in_specs=self.specs,...]
  transfers between devices with their start and end apart: 14 -> 8, of which waited for: 3 -> 2; matrix products, arithmetic and copies ran while one was open for 3% -> 2% of each run, Pallas kernels for 65% -> 75%
where the time goes in v3:
time: 506 us; the launch traced here: 501 us
  Pallas kernels  445 us (88%)
  local copies, waits for them, and re-layouts  23.8 us (5%)
  between operations  15.4 us (3%)
  waiting for transfers between devices  10.1 us (2%)
    pallas_call x23, Pallas kernels, run(): pl.pallas_call(kernel, out_shape=tuple(self.shapes), in_specs=self.specs,...  445 us
    unnamed x86, local copies, waits for them, and re-layouts  12 us
  transfers between devices with their start and end apart: 8, of which 2 were waited for; matrix products, arithmetic and copies ran while one was open for 2% of the time, Pallas kernels for 75%

profile of v3, /device:TPU:0, one launch (start us, length us, event | category | flops | bytes accessed | tf_op | source)
XLA Modules:
  0.0 500.6 jit_solution(4492735239521265333)
XLA Ops:
  7.4 1.0 fusion.9
  11.6 25.2 %open_program.1 = (bf16[128,1024]{1,0:T(8,128)(2,1)S(1)}, bf16[128,1024]{1,0:T(8,128)(2,1)S(1)}, bf16[4,512,128]{2,1,0:T(8,128)(2,1)}, f32[16,1024]{1,0:T(8,128)S(1)}, s32[2,40,128]{2,1,0:T(8,128)S(1)}) custom-call(bf16[2,64,1024]{2,1,0:T(8,128)(2,1)S(1)} %copy-done.2, bf16[2,64,1024]{2,1,0:T(8,128)(2,1)S(1)} %copy-done.3, ...), custom_call_target="tpu_custom_call" | custom-call | flops 12000000000 | tf_op jit(solution)/shard_map/open_program/pallas_call | solution.py:105
  39.5 33.1 %first_rows.1 = (bf16[4,128,1024]{2,1,0:T(8,128)(2,1)}, bf16[4,128,1024]{2,1,0:T(8,128)(2,1)}, bf16[4,768,128]{2,1,0:T(8,128)(2,1)}) custom-call(f32[16,1024]{1,0:T(8,128)S(1)} %get-tuple-element.84.refs_0_.refs_1_.refs_2_.refs_3_.refs_4_.refs_11_, bf16[128,1024]{1,0:T(8,128)(2,1)} %copy-done.8, bf16[128,1024]{1,0:T(8,128)(2,1)} %copy-done.9, ...), custom_call_target="tpu_custom_call" | custom-call | flops 24000000000 | tf_op jit(solution)/shard_map/first_rows/pallas_call | solution.py:105
  74.4 1.3 compare_convert_fusion
  76.8 8.4 %all-gather.9.cloned.1.call-done = bf16[32,512,128]{2,1,0:T(8,128)(2,1)} async-done(((bf16[4,512,128]{2,1,0:T(8,128)(2,1)}), bf16[32,512,128]{2,1,0:T(8,128)(2,1)}) %all-gather.9.cloned.1.call-update) | async-done | bytes 4194320 | tf_op jit(solution)/shard_map/all_gather | solution.py:970
  85.2 11.5 %project.1 = (bf16[4,512,128]{2,1,0:T(8,128)(2,1)}, bf16[4,128,256]{2,1,0:T(8,128)(2,1)}, bf16[2,4,128,512]{3,2,1,0:T(8,128)(2,1)}, bf16[4,128,256]{2,1,0:T(8,128)(2,1)}, bf16[2,4,128,512]{3,2,1,0:T(8,128)(2,1)}) custom-call(bf16[4,512,128]{2,1,0:T(8,128)(2,1)S(1)} %bitcast.200, bf16[2,4,4,512,128]{4,3,2,1,0:T(8,128)(2,1)} %bitcast.269, ...), custom_call_target="tpu_custom_call" | custom-call | flops 8000000000 | tf_op jit(solution)/shard_map/project/pallas_call | solution.py:105
  97.1 9.4 %attend.4 = (bf16[512,256]{1,0:T(8,128)(2,1)}, f32[8,512]{1,0:T(8,128)S(1)}) custom-call(bf16[512,256]{1,0:T(8,128)(2,1)} %bitcast.309, bf16[1024,512]{1,0:T(8,128)(2,1)} %bitcast.284, s32[8,512]{1,0:T(8,128)S(1)} %get-tuple-element.233.refs_2_.refs_4_, s32[1024,8]{1,0:T(8,128)S(1)} %copy.169.refs_3_.refs_5_), custom_call_target="tpu_custom_call" | custom-call | flops 8000000000 | tf_op jit(solution)/shard_map/attend/pallas_call | solution.py:105
  106.5 9.5 %attend.3 = (bf16[512,256]{1,0:T(8,128)(2,1)}, f32[8,512]{1,0:T(8,128)S(1)}) custom-call(bf16[512,256]{1,0:T(8,128)(2,1)} %bitcast.305, bf16[1024,512]{1,0:T(8,128)(2,1)} %bitcast.282, s32[8,512]{1,0:T(8,128)S(1)} %get-tuple-element.234.refs_2_.refs_4_, s32[1024,8]{1,0:T(8,128)S(1)} %copy.165.refs_3_.refs_5_), custom_call_target="tpu_custom_call" | custom-call | flops 8000000000 | tf_op jit(solution)/shard_map/attend/pallas_call | solution.py:105
  116.0 38.7 %after_self.1 = (f32[128,1024]{1,0:T(8,128)}, bf16[4,128,1024]{2,1,0:T(8,128)(2,1)}, f32[128,1024]{1,0:T(8,128)}, bf16[4,128,1024]{2,1,0:T(8,128)(2,1)}) custom-call(bf16[2,4,4,512,128]{4,3,2,1,0:T(8,128)(2,1)} %bitcast.270, f32[16,1024]{1,0:T(8,128)S(1)} %get-tuple-element.84.refs_0_.refs_1_.refs_2_.refs_3_.refs_4_.refs_11_, bf16[128,1024]{1,0:T(8,128)(2,1)} %copy-done.8, ...), custom_call_target="tpu_custom_call" | custom-call | flops 33999998976 | tf_op jit(solution)/shard_map/after_self/pallas_call | solution.py:105
  154.7 27.2 %memory.1 = (bf16[4,128,1024]{2,1,0:T(8,128)(2,1)}, f32[4,128,1024]{2,1,0:T(8,128)}, f32[128,1024]{1,0:T(8,128)}, bf16[2,4,128,512]{3,2,1,0:T(8,128)(2,1)}, bf16...) custom-call(bf16[2,4,4,768,128]{4,3,2,1,0:T(8,128)(2,1)} %bitcast.264, ...), custom_call_target="tpu_custom_call" | custom-call | flops 24000000000 | tf_op jit(solution)/shard_map/memory/pallas_call | solution.py:105
  182.0 9.7 %attend.5 = (bf16[512,256]{1,0:T(8,128)(2,1)}, f32[8,512]{1,0:T(8,128)S(1)}) custom-call(bf16[512,256]{1,0:T(8,128)(2,1)} %bitcast.311, bf16[1024,512]{1,0:T(8,128)(2,1)} %bitcast.293, s32[8,512]{1,0:T(8,128)S(1)} %get-tuple-element.233.refs_2_.refs_4_, s32[1024,8]{1,0:T(8,128)S(1)} %copy.165.refs_3_.refs_5_), custom_call_target="tpu_custom_call" | custom-call | flops 8000000000 | tf_op jit(solution)/shard_map/attend/pallas_call | solution.py:105
  191.7 27.2 %after_cross.1 = (f32[128,1024]{1,0:T(8,128)}, bf16[128,1024]{1,0:T(8,128)(2,1)S(1)}, bf16[4,128,1024]{2,1,0:T(8,128)(2,1)}) custom-call(bf16[2,4,4,768,128]{4,3,2,1,0:T(8,128)(2,1)} %bitcast.265, f32[16,1024]{1,0:T(8,128)S(1)} %get-tuple-element.84.refs_0_.refs_1_.refs_2_.refs_3_.refs_4_.refs_11_, f32[128,1024]{1,0:T(8,128)} %get-tuple-element.104.refs_2_.refs_5_, ...), custom_call_target="tpu_custom_call" | custom-call | flops 20000000000 | tf_op jit(solution)/shard_map/after_cross/pallas_call | solution.py:105
  219.7 29.1 %turn.1 = (bf16[4,128,1024]{2,1,0:T(8,128)(2,1)}, f32[4,128,1024]{2,1,0:T(8,128)}, bf16[128,1024]{1,0:T(8,128)(2,1)}, f32[128,1024]{1,0:T(8,128)}, f32[2,1024]{1...) custom-call(bf16[2,4,4,512,128]{4,3,2,1,0:T(8,128)(2,1)} %bitcast.274, ...), custom_call_target="tpu_custom_call" | custom-call | flops 24000000000 | tf_op jit(solution)/shard_map/turn/pallas_call | solution.py:105
  248.8 8.0 %weight_shares.4.refs_0_ = bf16[4,4,512,128]{3,2,1,0:T(8,128)(2,1)} custom-call(bf16[512,1024]{1,0:T(8,128)(2,1)} %bitcast.296, bf16[512,1024]{1,0:T(8,128)(2,1)} %bitcast.298, bf16[512,1024]{1,0:T(8,128)(2,1)} %bitcast.300, bf16[512,1024]{1,0:T(8,128)(2,1)} %bitcast.301), custom_call_target="tpu_custom_call" | custom-call | flops 8000000000 | tf_op jit(solution)/shard_map/weight_shares/pallas_call | solution.py:105
  257.1 25.4 %back_cross.1 = (f32[128,1024]{1,0:T(8,128)}, f32[2,1024]{1,0:T(2,128)S(1)}, bf16[4,128,256]{2,1,0:T(8,128)(2,1)}, bf16[4,128,1024]{2,1,0:T(8,128)(2,1)}) custom-call(bf16[4,4,512,128]{3,2,1,0:T(8,128)(2,1)} %weight_shares.4.refs_0_, bf16[2,4,4,512,128]{4,3,2,1,0:T(8,128)(2,1)} %bitcast.275, bf16[2,4,4,768,128]{4,3,2,1,0:T(8,128)(2,1)} %bitcast.266, ...), custom_call_target="tpu_custom_call" | custom-call | flops 20000000000 | tf_op jit(solution)/shard_map/back_cross/pallas_call | solution.py:105
  282.5 10.5 %attend_back.3.refs_0_.refs_2_.refs_4_ = bf16[512,768]{1,0:T(8,128)(2,1)} custom-call(bf16[512,256]{1,0:T(8,128)(2,1)} %bitcast.312, bf16[1024,512]{1,0:T(8,128)(2,1)} %bitcast.294, bf16[512,256]{1,0:T(8,128)(2,1)} %bitcast.316, f32[8,512]{1,0:T(8,128)S(1)} %get-tuple-element.114.refs_3_, s32[8,512]{1,0:T(8,128)S(1)} %get-tuple-element.233.refs_2_.refs_4_, ...), custom_call_target="tpu_custom_call" | custom-call | flops 16000000000 | tf_op jit(solution)/shard_map/attend_back/pallas_call | solution.py:105
  293.1 6.5 %weight_shares.5.refs_0_ = bf16[4,4,256,128]{3,2,1,0:T(8,128)(2,1)} custom-call(bf16[512,768]{1,0:T(8,128)(2,1)} %attend_back.3.refs_0_.refs_2_.refs_4_, bf16[512,1024]{1,0:T(8,128)(2,1)} %bitcast.290, bf16[512,768]{1,0:T(8,128)(2,1)} %attend_back.3.refs_0_.refs_2_.refs_4_, bf16[512,1024]{1,0:T(8,128)(2,1)} %bitcast.291, ...), custom_call_target="tpu_custom_call" | custom-call | flops 4000000000 | tf_op jit(solution)/shard_map/weight_shares/pallas_call | solution.py:105
  299.9 43.2 %back_both.1 = (bf16[2,64,1024]{2,1,0:T(8,128)(2,1)S(1)}, f32[128,1024]{1,0:T(8,128)}, f32[2,1024]{1,0:T(2,128)S(1)}, bf16[4,128,256]{2,1,0:T(8,128)(2,1)}, bf16...) custom-call(bf16[4,4,256,128]{3,2,1,0:T(8,128)(2,1)} %weight_shares., ...), custom_call_target="tpu_custom_call" | custom-call | flops 38000001024 | tf_op jit(solution)/shard_map/back_both/pallas_call | solution.py:105
  343.1 8.1 %weight_shares.6.refs_6_ = bf16[4,4,512,128]{3,2,1,0:T(8,128)(2,1)} custom-call(bf16[512,1024]{1,0:T(8,128)(2,1)} %bitcast.289, bf16[512,1024]{1,0:T(8,128)(2,1)} %bitcast.286, bf16[512,1024]{1,0:T(8,128)(2,1)} %bitcast.287, bf16[512,1024]{1,0:T(8,128)(2,1)} %bitcast.297), custom_call_target="tpu_custom_call" | custom-call | flops 8000000000 | tf_op jit(solution)/shard_map/weight_shares/pallas_call | solution.py:105
  351.8 10.8 %attend_back.4.refs_1_.refs_3_.refs_5_ = bf16[512,768]{1,0:T(8,128)(2,1)} custom-call(bf16[512,256]{1,0:T(8,128)(2,1)} %bitcast.310, bf16[1024,512]{1,0:T(8,128)(2,1)} %bitcast.285, bf16[512,256]{1,0:T(8,128)(2,1)} %bitcast.313, f32[8,512]{1,0:T(8,128)S(1)} %get-tuple-element.123.refs_3_, s32[8,512]{1,0:T(8,128)S(1)} %get-tuple-element.233.refs_2_.refs_4_, ...), custom_call_target="tpu_custom_call" | custom-call | flops 16000000000 | tf_op jit(solution)/shard_map/attend_back/pallas_call | solution.py:105
  362.6 37.9 %back_self.1 = (bf16[4,4,256,128]{3,2,1,0:T(8,128)(2,1)}, f32[128,1024]{1,0:T(8,128)}, f32[2,1024]{1,0:T(2,128)S(1)}, bf16[4,128,256]{2,1,0:T(8,128)(2,1)}, bf16...) custom-call(bf16[4,512,128]{2,1,0:T(8,128)(2,1)} %bitcast.211, ...), custom_call_target="tpu_custom_call" | custom-call | flops 28000000000 | tf_op jit(solution)/shard_map/back_self/pallas_call | solution.py:105
  400.7 10.5 %attend_back.5.refs_0_.refs_2_.refs_4_ = bf16[512,768]{1,0:T(8,128)(2,1)} custom-call(bf16[512,256]{1,0:T(8,128)(2,1)} %bitcast.306, bf16[1024,512]{1,0:T(8,128)(2,1)} %bitcast.283, bf16[512,256]{1,0:T(8,128)(2,1)} %bitcast.315, f32[8,512]{1,0:T(8,128)S(1)} %get-tuple-element.131.refs_3_, s32[8,512]{1,0:T(8,128)S(1)} %get-tuple-element.234.refs_2_.refs_4_, ...), custom_call_target="tpu_custom_call" | custom-call | flops 16000000000 | tf_op jit(solution)/shard_map/attend_back/pallas_call | solution.py:105
  411.2 6.6 %weight_shares.7.refs_0_ = bf16[4,4,256,128]{3,2,1,0:T(8,128)(2,1)} custom-call(bf16[512,768]{1,0:T(8,128)(2,1)} %attend_back.5.refs_0_.refs_2_.refs_4_, bf16[512,1024]{1,0:T(8,128)(2,1)} %bitcast.276, bf16[512,768]{1,0:T(8,128)(2,1)} %attend_back.5.refs_0_.refs_2_.refs_4_, bf16[512,1024]{1,0:T(8,128)(2,1)} %bitcast.277, ...), custom_call_target="tpu_custom_call" | custom-call | flops 4000000000 | tf_op jit(solution)/shard_map/weight_shares/pallas_call | solution.py:105
  417.8 14.0 %back_first.1 = (f32[128,1024]{1,0:T(8,128)}, f32[2,1024]{1,0:T(2,128)S(1)}) custom-call(bf16[4,4,256,128]{3,2,1,0:T(8,128)(2,1)} %weight_shares.7.refs_0_, bf16[4,512,128]{2,1,0:T(8,128)(2,1)} %bitcast.213, bf16[2,4,4,512,128]{4,3,2,1,0:T(8,128)(2,1)} %bitcast.273, f32[16,1024]{1,0:T(8,128)S(1)} %get-tuple-element.84.refs_0_.refs_1_.refs_2_.refs_3_.refs_4_.refs_11_, ...), custom_call_target="tpu_custom_call" | custom-call | flops 12000000000 | tf_op jit(solution)/shard_map/back_first/pallas_call | solution.py:105
  432.1 1.2 convert_element_type.39.refs_0_
  434.3 0.9 copy-done.6
  435.3 35.3 %close_program.1 = (bf16[2,64,1024]{2,1,0:T(8,128)(2,1)S(1)}, bf16[2,64,1024]{2,1,0:T(8,128)(2,1)S(1)}, bf16[4,512,128]{2,1,0:T(8,128)(2,1)S(1)}, bf16[4,256,128...) custom-call(bf16[128,1024]{1,0:T(8,128)(2,1)S(1)} %convert_element_t, ...), custom_call_target="tpu_custom_call" | custom-call | flops 16000000000 | tf_op jit(solution)/shard_map/close_program/pallas_call | solution.py:105
  472.1 1.5 reduce-scatter.14.cloned.1.call-done
  473.6 0.9 copy-done.7
  474.6 7.3 %swap_packs.1 = bf16[4,256,128]{2,1,0:T(8,128)(2,1)S(1)} custom-call(bf16[4,256,128]{2,1,0:T(8,128)(2,1)S(1)} %bitcast.218), custom_call_target="tpu_custom_call" | custom-call | flops 5000000000 | tf_op jit(solution)/shard_map/swap_packs/pallas_call | solution.py:105
  483.6 1.0 copy.187
  485.5 1.0 copy.188
  (203 shorter events, 22.9 us)
Async XLA Ops:
  7.2 3.8 copy-start.21
  7.2 3.9 copy-start.25
  7.2 3.9 slice-start.3
  7.2 3.9 copy-start.26
  7.2 3.9 copy-start.27
  7.2 3.9 copy-start.28
  7.3 4.1 copy-start.29
  7.3 4.2 copy-start.30
  7.3 4.2 copy-start.24
  7.3 4.2 copy-start.23
  7.3 4.3 copy-start.2
  7.3 4.3 copy-start.3
  7.3 77.9 %all-gather.9.cloned.1.call-start = ((), (), s32[]{:S(2)}) async-start(), calls=%async_computation.11 | async-start | bytes 4718592 | tf_op jit(solution)/shard_map/all_gather | solution.py:970
  11.6 26.8 %copy-start.20 = (bf16[3,128,256]{2,1,0:T(8,128)(2,1)S(1)}, bf16[3,128,256]{2,1,0:T(8,128)(2,1)}, u32[]{:S(2)}) copy-start(bf16[3,128,256]{2,1,0:T(8,128)(2,1)} %param.36) | copy-start | bytes 589828
  11.6 27.1 %copy-start.22 = (bf16[256,128]{1,0:T(8,128)(2,1)S(1)}, bf16[256,128]{1,0:T(8,128)(2,1)}, u32[]{:S(2)}) copy-start(bf16[256,128]{1,0:T(8,128)(2,1)} %param.37) | copy-start | bytes 196612
  38.3 116.4 %all-gather.7.cloned.1.call-start = ((), (), s32[]{:S(2)}) async-start(), calls=%async_computation.10 | async-start | bytes 7077888 | tf_op jit(solution)/shard_map/all_gather | solution.py:970
  72.6 3.6 copy-start.17
  72.6 4.1 copy-start.19
  72.6 147.0 %all-gather.11.cloned.1.call-start = ((), (), s32[]{:S(2)}) async-start(), calls=%async_computation.12 | async-start | bytes 4718592 | tf_op jit(solution)/shard_map/all_gather | solution.py:970
  96.8 265.8 %reduce-scatter.6.cloned.1.call-start = ((), (), s32[]{:S(2)}) async-start(), calls=%async_computation.5 | async-start | bytes 2621440 | tf_op jit(solution)/shard_map/reduce_scatter | solution.py:960
  181.9 9.8 %copy-start.4 = (bf16[2,64,1024]{2,1,0:T(8,128)(2,1)S(1)}, bf16[2,64,1024]{2,1,0:T(8,128)(2,1)}, u32[]{:S(2)}) copy-start(bf16[2,64,1024]{2,1,0:T(8,128)(2,1)} %refs_3_.1) | copy-start | bytes 786436
  256.8 143.8 %reduce-scatter.8.cloned.1.call-start = ((), (), s32[]{:S(2)}) async-start(), calls=%async_computation.6 | async-start | bytes 1310720 | tf_op jit(solution)/shard_map/reduce_scatter | solution.py:960
  293.0 6.9 %copy-start.11 = (bf16[128,1024]{1,0:T(8,128)(2,1)S(1)}, bf16[128,1024]{1,0:T(8,128)(2,1)}, u32[]{:S(2)}) copy-start(bf16[128,1024]{1,0:T(8,128)(2,1)} %get-tuple-element.117.refs_3_) | copy-start | bytes 786436
  299.6 118.2 %reduce-scatter.10.cloned.1.call-start = ((), (), s32[]{:S(2)}) async-start(), calls=%async_computation.7 | async-start | bytes 2621440 | tf_op jit(solution)/shard_map/reduce_scatter | solution.py:960
  351.3 82.1 %reduce-scatter.12.cloned.1.call-start = ((), (), s32[]{:S(2)}) async-start(), calls=%async_computation.8 | async-start | bytes 1310720 | tf_op jit(solution)/shard_map/reduce_scatter | solution.py:960
  400.6 73.0 %reduce-scatter.14.cloned.1.call-start = ((), (), s32[]{:S(2)}) async-start(), calls=%async_computation.9 | async-start | bytes 1310720 | tf_op jit(solution)/shard_map/reduce_scatter | solution.py:960
  470.6 11.2 %copy-start.12 = (f32[4,4,64,128]{3,2,1,0:T(8,128)}, f32[4,4,64,128]{3,2,1,0:T(8,128)S(1)}, u32[]{:S(2)}) copy-start(f32[4,4,64,128]{3,2,1,0:T(8,128)S(1)} %copy_bitcast_fusion.1) | copy-start | bytes 1572868
  471.4 10.5 %copy-start.13 = (f32[4,4,64,128]{3,2,1,0:T(8,128)}, f32[4,4,64,128]{3,2,1,0:T(8,128)S(1)}, u32[]{:S(2)}) copy-start(f32[4,4,64,128]{3,2,1,0:T(8,128)S(1)} %copy_bitcast_fusion) | copy-start | bytes 1572868
  481.9 1.7 copy-start.14
  484.6 2.0 slice-start
  484.7 2.8 slice-start.1
  485.5 5.8 %slice-start.2 = ((f32[4,4,64,128]{3,2,1,0:T(8,128)}), f32[3,4,64,128]{3,2,1,0:T(8,128)S(1)}, s32[]{:S(2)}) async-start(f32[4,4,64,128]{3,2,1,0:T(8,128)} %copy-done.14), calls=%async_computation.15 | async-start | bytes 786432 | tf_op jit(solution)/shard_map/slice | solution.py:1407
  (11 other events, 11.6 us)
Sparse Core Ops, SparseCore 0:
  38.4 46.7 all-gather.8
  86.8 63.4 all-gather.6
  151.9 45.7 all-gather.10
  257.0 42.2 reduce-scatter.5
  301.5 28.7 reduce-scatter.7
  351.4 44.7 reduce-scatter.9
  400.7 25.5 reduce-scatter.11
  432.1 41.4 reduce-scatter.13

commit v4 on v3

--- a/solution.py
+++ b/solution.py
@@ -23,6 +23,8 @@
         self.fetched, self.kept = [], []
 
     def take(self, array, space=pltpu.VMEM):
+        if isinstance(array, tuple):
+            return array
         for i, known in enumerate(self.known):
             if known is array and self.specs[i].memory_space == space:
                 return ("in", i)
@@ -34,6 +36,8 @@
         return ("in", len(self.arrays) - 1)
 
     def fetch(self, array):
+        if isinstance(array, tuple):
+            return array
         source = self.take(array, pltpu.HBM)
         for i, (known, room, sem) in enumerate(self.fetched):
             if known == source:
@@ -76,7 +80,7 @@
 
         def kernel(*refs):
             parts = {"in": refs[:ins], "out": refs[ins : ins + outs], "tmp": refs[ins + outs :]}
-            here, self.saves = set(), []
+            here, self.saves, self.waited = set(), [], []
 
             def get(handle):
                 kind, i = handle
@@ -205,20 +209,26 @@
         return get(self.room)[:, first : first + count, :].reshape(4 * count, 1024)
 
 
+def stack(blocks):
+    return blocks[0] if len(blocks) == 1 else jnp.concatenate(blocks, 0)
+
+
 class Feed:
     def __init__(self, call, rows, up, down):
         self.call, self.rows, self.weights = call, call.fetch(rows), [up, down]
         self.hidden = call.keep((4, 128, 1024), BF16, 4)
         self.slope = call.keep((4, 128, 1024), F32, 4)
 
-    def part(self, get, row):
+    def part(self, get, *rows):
         up, down = self.weights
-        made, slope = gelu_pair(nt(get(self.rows)[row], up.matrix(get, 0, 256)))
+        whole = stack([get(self.rows)[row] for row in rows])
+        made, slope = gelu_pair(nt(whole, up.matrix(get, 0, 256)))
         made = made.astype(BF16)
-        get(self.hidden)[row] = made
-        get(self.slope)[row] = slope
-        self.call.save(get, self.hidden, row)
-        self.call.save(get, self.slope, row)
+        for i, row in enumerate(rows):
+            get(self.hidden)[row] = made[i * 128 : (i + 1) * 128]
+            get(self.slope)[row] = slope[i * 128 : (i + 1) * 128]
+            self.call.save(get, self.hidden, row)
+            self.call.save(get, self.slope, row)
         return nn(made, down.matrix(get, 0, 256))
 
 
@@ -242,14 +252,14 @@
     def lefts(self):
         return self.left.weights if isinstance(self.left, Feed) else [self.left[1]]
 
-    def part(self, get, row):
+    def part(self, get, *rows):
         if isinstance(self.left, Feed):
-            return self.left.part(get, row)
+            return self.left.part(get, *rows)
         unused, weight, picks, column = self.left
         total = None
         for first, count in picks:
             width = 4 * count
-            left = get(self.rows_in)[row, :, column : column + width]
+            left = stack([get(self.rows_in)[row, :, column : column + width] for row in rows])
             term = nn(left, weight.matrix(get, first, count))
             total = term if total is None else total + term
             column += width
@@ -278,15 +288,13 @@
         self.copies[1] = self.send(
             get, 1, first.at[0, pl.ds(64, 64)], landed.at[1], at["y"]
         )
-        part = self.part(get, at["x_row"])
+        part = self.part(get, at["x_row"], at["y_row"])
         edge[0] = part[:64].astype(BF16)
-        keep[0] = part[64:]
+        keep[0] = part[64:128]
         self.copies[2] = self.send(get, 2, edge.at[0], landed.at[2], at["x"])
-        part = self.part(get, at["y_row"])
-        edge[1] = part[64:].astype(BF16)
-        keep[1] = part[:64]
+        edge[1] = part[192:].astype(BF16)
+        keep[1] = part[128:192]
         self.copies[3] = self.send(get, 3, edge.at[1], landed.at[3], at["y"])
-        get(self.own)[...] = self.part(get, at["own_row"])
 
     def sum_forward(self, get, at):
         late, landed, keep = get(self.out_late), get(self.landed), get(self.keep)
@@ -296,6 +304,9 @@
         self.copies[1].wait_recv()
         late[0] = (keep[0] + landed[1].astype(F32)).astype(BF16)
         self.copies[5] = self.send(get, 5, late.at[0], landed.at[5], at["x"])
+
+    def sum_own(self, get, at):
+        get(self.own)[...] = self.part(get, at["own_row"])
 
     def sum_end(self, get):
         landed, own = get(self.landed), get(self.own)
@@ -367,25 +378,41 @@
     def finish(self, get, at):
         return None
 
-
-def run_stage(call, jobs, weights, name, collective, finish=None, flops=0, core=False, more=()):
-    def body(get):
-        at = place()
-        for weight in weights:
+    def begin(self, get):
+        return None
+
+    def run(self, get, at):
+        self.middle(get, at)
+        self.start(get, at)
+        self.late(get, at)
+        self.finish(get, at)
+
+
+class Stage(Extra):
+    def __init__(self, call, jobs, weights=(), finish=None, core=False, more=()):
+        self.call, self.jobs, self.weights = call, jobs, weights
+        self.end, self.core, self.more = finish, core, more
+
+    def partners(self, at):
+        found = [at["x"], at["y"]] + ([at["core"]] if self.core else [])
+        for extra in self.more:
+            found += extra.partners(at)
+        return found
+
+    def begin(self, get):
+        for weight in self.weights:
             weight.start(get)
-        partners = [at["x"], at["y"]] + ([at["core"]] if core else [])
-        for extra in more:
-            partners += [p for p in extra.partners(at) if all(p is not q for q in partners)]
-        greet(partners)
+
+    def run(self, get, at):
+        call, jobs, more = self.call, self.jobs, self.more
         lefts = [job for job in jobs if job.left is not None]
         movers = [job for job in jobs if job.right is not None]
         rights = [job for job in movers if job.right[0] is not None]
-        waited = []
 
         def ready(weight):
-            if weight not in waited:
+            if weight not in call.waited:
                 weight.wait(get)
-                waited.append(weight)
+                call.waited.append(weight)
 
         def arrived(job, row):
             call.save(get, job.gathered, row)
@@ -398,6 +425,8 @@
             job.sum_start(get, at)
         for job in lefts:
             job.sum_forward(get, at)
+        for job in lefts:
+            job.sum_own(get, at)
         for extra in more:
             extra.middle(get, at)
         for job in jobs:
@@ -406,7 +435,7 @@
                 job.rows_start(get, at, normed)
         for extra in more:
             extra.start(get, at)
-        for weight in weights:
+        for weight in self.weights:
             ready(weight)
         for extra in more:
             extra.late(get, at)
@@ -425,12 +454,36 @@
             arrived(job, at["d_row"])
         for job in jobs:
             job.drain()
-        if finish is not None:
-            finish(get)
+        if self.end is not None:
+            self.end(get)
         for extra in more:
             extra.finish(get, at)
 
+
+def run_steps(call, steps, name, collective, flops=0):
+    def body(get):
+        at = place()
+        for step in steps:
+            step.begin(get)
+        partners = []
+        for step in steps:
+            for partner in step.partners(at):
+                if all(partner is not known for known in partners):
+                    partners.append(partner)
+        greet(partners)
+        for step in steps:
+            step.run(get, at)
+
     return call.run(body, name, collective, flops)
+
+
+def run_stage(call, jobs, weights, name, collective, finish=None, flops=0, core=False, more=()):
+    return run_steps(call, [Stage(call, jobs, weights, finish, core, more)], name, collective, flops)
+
+
+class Kept:
+    def __init__(self, out, store):
+        self.out, self.store = out, store
 
 
 class Plain:
@@ -500,31 +553,32 @@
     return jnp.where(allowed, 0.0, MASKED)
 
 
-def attend(queries, key_value, facts, keys, causal):
-    rows, width = 512, queries.shape[-1]
-    half = rows // 2
-    call = Call()
-    q_in = call.fetch(queries.reshape(rows, width))
-    kv_in = call.fetch(key_value.reshape(1024, 2 * width))
-    facts_in, keys_in = call.take(facts), call.take(keys)
-    mixed_out, total_out = call.keep((rows, width), BF16, 2), call.give((8, rows), F32)
-    bias = call.hold((1024, rows), F32)
-
-    def body(get):
-        mask = get(bias)
-        mask[...] = allowed_bias(get(facts_in), get(keys_in), causal)
-        q_ref, kv_ref, mixed_ref, total_ref = get(q_in), get(kv_in), get(mixed_out), get(total_out)
+class Attend(Extra):
+    def __init__(self, call, queries, key_value, facts, keys, causal):
+        self.call, self.causal = call, causal
+        self.queries, self.key_value = call.fetch(queries), call.fetch(key_value)
+        self.facts, self.keys = call.take(facts), call.take(keys)
+        self.mixed = call.keep((4, 128, 256), BF16)
+        self.total = call.give((8, 512), F32)
+        self.bias = call.hold((1024, 512), F32)
+
+    def late(self, get, at):
+        mask = get(self.bias)
+        mask[...] = allowed_bias(get(self.facts), get(self.keys), self.causal)
+        q_ref, kv_ref = get(self.queries), get(self.key_value)
+        mixed_ref, total_ref = get(self.mixed), get(self.total)
 
         def pair_step(pair, carry):
             lanes = pl.ds(pl.multiple_of(pair * 128, 128), 128)
             value_lanes = pl.ds(pl.multiple_of(256 + pair * 128, 128), 128)
-            keys, values = kv_ref[:, lanes], kv_ref[:, value_lanes]
+            keys = kv_ref[:, :, :, lanes].reshape(1024, 128)
+            values = kv_ref[:, :, :, value_lanes].reshape(1024, 128)
             for block in range(2):
-                span = slice(block * half, (block + 1) * half)
-                queries = q_ref[span, lanes]
+                span = slice(block * 256, block * 256 + 256)
+                queries = q_ref[2 * block : 2 * block + 2, :, lanes].reshape(256, 128)
                 mixed = []
                 for head in range(2):
-                    picked = jnp.where(lanes_of(head, half), queries * 0.125, 0.0).astype(BF16)
+                    picked = jnp.where(lanes_of(head, 256), queries * 0.125, 0.0).astype(BF16)
                     scores = nt(keys, picked) + mask[:, span]
                     top = jnp.max(scores, 0, keepdims=True)
                     raised = jnp.exp(scores - top)
@@ -532,54 +586,49 @@
                     probs = (raised * (1.0 / total)).astype(BF16)
                     mixed.append(tn(values, probs)[head * HEAD_DIM : (head + 1) * HEAD_DIM])
                     total_ref[pl.ds(pair * 2 + head, 1), span] = top + jnp.log(total)
-                mixed_ref[span, lanes] = jnp.concatenate(mixed, 0).T.astype(BF16)
+                mixed = jnp.concatenate(mixed, 0).T.astype(BF16)
+                mixed_ref[2 * block : 2 * block + 2, :, lanes] = mixed.reshape(2, 128, 128)
             return carry
 
         lax.fori_loop(0, 2, pair_step, 0)
-        call.save(get, mixed_out)
-
-    mixed, total = call.run(body, "attend", None, 8 * MICROSECOND)
-    return mixed.reshape(4, 128, width), total
-
-
-def attend_back(
-    queries, key_value, grad_mixed, total, facts, keys, causal, collective, done=()
-):
-    rows, width = 512, queries.shape[-1]
-    half = rows // 2
-    call = Call()
-    q_in = call.fetch(queries.reshape(rows, width))
-    kv_in = call.fetch(key_value.reshape(1024, 2 * width))
-    grad_in, total_in = call.fetch(grad_mixed.reshape(rows, width)), call.take(total)
-    facts_in, keys_in = call.take(facts), call.take(keys)
-    for array in done:
-        call.take(array, pltpu.HBM)
-    grad_out = call.keep((rows, 3 * width), BF16)
-    bias = call.hold((1024, rows), F32)
-    gathered = call.hold((1024, 4 * 128), F32)
-    outgoing, landed = call.hold((2, 512, 256), BF16), call.hold((2, 512, 256), BF16)
-    send_sem, recv_sem = call.sems(2), call.sems(2)
-
-    def body(get):
-        at = place()
-        out, mask, sums = get(grad_out), get(bias), get(gathered)
-        away, here = get(outgoing), get(landed)
-        mask[...] = allowed_bias(get(facts_in), get(keys_in), causal)
-        greet([at["core"]])
-        q_ref, kv_ref, grad_ref, total_ref = get(q_in), get(kv_in), get(grad_in), get(total_in)
+        self.call.save(get, self.mixed)
+
+
+class AttendBack(Extra):
+    def __init__(self, call, queries, key_value, grad_mixed, total, facts, keys, causal):
+        self.call, self.causal = call, causal
+        self.queries, self.key_value = call.fetch(queries), call.fetch(key_value)
+        self.grad_mixed, self.total = call.fetch(grad_mixed), call.take(total)
+        self.facts, self.keys = call.take(facts), call.take(keys)
+        self.out = call.keep((4, 128, 768), BF16)
+        self.bias, self.sums = call.hold((1024, 512), F32), call.hold((1024, 512), F32)
+        self.away, self.landed = call.hold((2, 512, 256), BF16), call.hold((2, 512, 256), BF16)
+        self.send_sem, self.recv_sem = call.sems(2), call.sems(2)
+
+    def partners(self, at):
+        return [at["core"]]
+
+    def late(self, get, at):
+        out, mask, sums = get(self.out), get(self.bias), get(self.sums)
+        away, here = get(self.away), get(self.landed)
+        mask[...] = allowed_bias(get(self.facts), get(self.keys), self.causal)
+        q_ref, kv_ref = get(self.queries), get(self.key_value)
+        grad_ref, total_ref = get(self.grad_mixed), get(self.total)
         copies = []
         for pair in range(2):
             lanes = slice(pair * 128, pair * 128 + 128)
-            keys_pair = kv_ref[:, lanes]
-            values_pair = kv_ref[:, 256 + pair * 128 : 256 + pair * 128 + 128]
+            keys_pair = kv_ref[:, :, :, lanes].reshape(1024, 128)
+            values_pair = kv_ref[:, :, :, 256 + pair * 128 : 384 + pair * 128].reshape(1024, 128)
             key_sum = slice(pair * 256, pair * 256 + 128)
             value_sum = slice(pair * 256 + 128, pair * 256 + 256)
             for block in range(2):
-                span = slice(block * half, (block + 1) * half)
-                q_block, g_block = q_ref[span, lanes], grad_ref[span, lanes]
+                span = slice(block * 256, block * 256 + 256)
+                two = slice(2 * block, 2 * block + 2)
+                q_block = q_ref[two, :, lanes].reshape(256, 128)
+                g_block = grad_ref[two, :, lanes].reshape(256, 128)
                 grad_query = []
                 for head in range(2):
-                    inside = lanes_of(head, half)
+                    inside = lanes_of(head, 256)
                     picked = jnp.where(inside, q_block * 1.0, 0.0).astype(BF16)
                     grads = jnp.where(inside, g_block * 1.0, 0.0).astype(BF16)
                     scores = nt(keys_pair, picked) * 0.125 + mask[:, span]
@@ -596,13 +645,14 @@
                         sums[:, key_sum] += key_term
                         sums[:, value_sum] += value_term
                     grad_query.append(tn(keys_pair, grad_raw)[head * HEAD_DIM : (head + 1) * HEAD_DIM])
-                out[span, lanes] = jnp.concatenate(grad_query, 0).T.astype(BF16)
+                grad_query = jnp.concatenate(grad_query, 0).T.astype(BF16)
+                out[two, :, lanes] = grad_query.reshape(2, 128, 128)
             away[pair] = sums[512:, pair * 256 : pair * 256 + 256].astype(BF16)
             copy = pltpu.make_async_remote_copy(
                 src_ref=away.at[pair],
                 dst_ref=here.at[pair],
-                send_sem=get(send_sem).at[pair],
-                recv_sem=get(recv_sem).at[pair],
+                send_sem=get(self.send_sem).at[pair],
+                recv_sem=get(self.recv_sem).at[pair],
                 device_id=at["core"],
                 device_id_type=MESH_ID,
             )
@@ -611,26 +661,26 @@
         for pair in range(2):
             copies[pair].wait()
             both = sums[:512, pair * 256 : pair * 256 + 256] + here[pair].astype(F32)
-            out[:, width + pair * 128 : width + pair * 128 + 128] = both[:, :128].astype(BF16)
-            out[:, 2 * width + pair * 128 : 2 * width + pair * 128 + 128] = both[:, 128:].astype(BF16)
-        call.save(get, grad_out)
-
-    (grads,) = call.run(body, "attend_back", collective, 16 * MICROSECOND)
-    return grads.reshape(4, 128, 3 * width)
+            both = both.astype(BF16).reshape(4, 128, 256)
+            out[:, :, 256 + pair * 128 : 384 + pair * 128] = both[:, :, :128]
+            out[:, :, 512 + pair * 128 : 640 + pair * 128] = both[:, :, 128:]
+        self.call.save(get, self.out)
 
 
 class Shares(Extra):
-    def __init__(self, call, pairs, count):
-        self.call, self.count = call, count
+    def __init__(self, call, pairs, count, out=None, base=0):
+        self.call, self.count, self.base = call, count, base
         self.handles = [
-            (call.fetch(left.reshape(512, -1)), column, call.fetch(by_owner(right).reshape(512, 1024)))
+            (call.fetch(left), column, call.fetch(by_owner(right)))
             for left, column, right in pairs
         ]
         shape = (4, 4, len(pairs) * count, 128)
         sends = len(pairs) * max(1, count // 64)
         self.made, self.landed = call.hold((2,) + shape, BF16), call.hold(shape, BF16)
         self.send_sem, self.recv_sem = call.sems(sends), call.sems(sends)
-        self.out = call.keep(shape, BF16)
+        self.rows = shape[2]
+        self.out = call.give(shape, BF16, pltpu.HBM) if out is None else out
+        self.room, self.save_sem = call.hold(shape, BF16), call.sems(1)
 
     def partners(self, at):
         return [at["core"]]
@@ -655,7 +705,10 @@
             left, right = get(left), get(right)
             span = slice(m * count, (m + 1) * count)
             for first in range(0, 4 * count, 256):
-                product = tn(left[:, column + first : column + first + 256], right[...])
+                start = column + first
+                product = tn(
+                    left[:, :, start : start + 256].reshape(512, 256), right[...].reshape(512, 1024)
+                )
                 for inner in range(0, 256, count):
                     z = (first + inner) // count
                     for d in range(8):
@@ -672,29 +725,31 @@
         for part, copy in self.copies:
             copy.wait()
             own = get(self.made)[(core,) + part].astype(F32)
-            get(self.out)[part] = (own + get(self.landed)[part].astype(F32)).astype(BF16)
-        self.call.save(get, self.out)
-
-
-def weight_shares(pairs, count, collective):
-    call = Call()
-    shares = Shares(call, pairs, count)
-
-    def body(get):
-        at = place()
-        greet([at["core"]])
-        shares.middle(get, at)
-        shares.finish(get, at)
-
-    (made,) = call.run(body, "weight_shares", collective, len(pairs) * count // 64 * MICROSECOND)
-    return made
+            get(self.room)[part] = (own + get(self.landed)[part].astype(F32)).astype(BF16)
+        target = get(self.out).at[:, :, pl.ds(self.base, self.rows)]
+        copy = pltpu.make_async_copy(get(self.room), target, get(self.save_sem).at[0])
+        copy.start()
+        self.call.saves.append((None, copy))
+
+
+class Carry(Extra):
+    def __init__(self, call, array, out, base):
+        self.call, self.array, self.out, self.base = call, call.take(array, pltpu.HBM), out, base
+        self.rows, self.sem = array.shape[2], call.sems(1)
+
+    def begin(self, get):
+        target = get(self.out).at[:, :, pl.ds(self.base, self.rows)]
+        copy = pltpu.make_async_copy(get(self.array), target, get(self.sem).at[0])
+        copy.start()
+        self.call.saves.append((None, copy))
 
 
 class Swap(Extra):
     def __init__(self, call, packs):
         self.packs = [call.take(pack) for pack in packs]
         self.outs = [call.give(pack.shape, pack.dtype) for pack in packs]
-        self.send_sem, self.recv_sem = call.sems(3 * len(packs)), call.sems(3 * len(packs))
+        count = max(1, 3 * len(packs))
+        self.send_sem, self.recv_sem = call.sems(count), call.sems(count)
 
     def start(self, get, at):
         hi, k, y, c, z = at["mesh"]
@@ -977,7 +1032,7 @@
 
 def by_owner(rights):
     copies = lax.axis_size("k")
-    if copies == 1:
+    if copies == 1 or isinstance(rights, tuple):
         return rights
     shape = rights.shape
     rights = rights.reshape(-1, 2, copies, 2, 2, 128 // copies).transpose(0, 1, 3, 4, 2, 5)
@@ -1120,7 +1175,7 @@
             get(out)[row] = (value * get(slope)[row]).astype(BF16)
             call.save(get, out, row)
 
-        return store
+        return Kept(out, store)
 
     call = Call()
 
@@ -1143,87 +1198,116 @@
     second_w = gather_weights(second_p)
 
     call = Call()
-    made, finishes, plans = [], [], []
     swap = Swap(call, [third_p])
+    plans = []
     for rows, base in ((rows_a, 0), (rows_c, SELF)):
-        weight = pick(call, first_w, QKV, base)
-        store, finish = query_and_shared(call, 256)
-        plans.append((call.fetch(rows), weight, store))
-        finishes.append(finish)
-
-    def project(get):
-        at = place()
-        for unused, weight, unused2 in plans:
-            weight.start(get)
-        greet([at["core"]] + swap.partners(at))
-        swap.start(get, at)
-        for rows, weight, store in plans:
-            weight.wait(get)
-            for row in range(4):
-                for m in range(3):
-                    store(
-                        get, at, row, m * 256, nt(get(rows)[row], weight.matrix(get, m * 64, 64))
-                    )
-        for finish in finishes:
-            finish(get)
-        swap.finish(get, at)
-
-    third_p, enc_q, enc_kv, self_q, self_kv = call.run(project, "project", 1, 8 * MICROSECOND)
-    third_w = gather_weights(third_p)
-
-    enc_mixed, enc_total = attend(enc_q, enc_kv, source_facts, source_keys, False)
-    self_mixed, self_total = attend(self_q, self_kv, target_facts, target_keys, True)
-
-    call = Call()
+        query, shared = Plain(call, 256), Shared(call, 512, 256)
+        plans.append((call.fetch(rows), pick(call, first_w, QKV, base), query, shared))
+    enc_step = Attend(call, plans[0][2].out, plans[0][3].out, source_facts, source_keys, False)
+    self_step = Attend(call, plans[1][2].out, plans[1][3].out, target_facts, target_keys, True)
     enc_o, self_o = pick(call, first_w, O), pick(call, first_w, O, SELF)
     mid = forward_mid(call, stream_in, ENC_G + 1, ENC_B + 1)
-    job_b = Job(call, (enc_mixed, enc_o, [(0, 64)], 0), mid, (None, None, None))
+    job_b = Job(call, (enc_step.mixed, enc_o, [(0, 64)], 0), mid, (None, None, None))
     mid = forward_mid(call, target_in, DEC_G + 1, DEC_B + 1)
-    job_d = Job(call, (self_mixed, self_o, [(0, 64)], 0), mid, (None, None, None))
-    stream_mid, rows_b, target_mid, rows_d = run_stage(
-        call, [job_b, job_d], [enc_o, self_o], "after_self", 2, flops=34 * MICROSECOND
-    )
+    job_d = Job(call, (self_step.mixed, self_o, [(0, 64)], 0), mid, (None, None, None))
+
+    class Project(Extra):
+        def partners(self, at):
+            return [at["core"]] + swap.partners(at)
+
+        def begin(self, get):
+            for plan in plans:
+                plan[1].start(get)
+
+        def run(self, get, at):
+            swap.start(get, at)
+            for rows, weight, query, shared in plans:
+                weight.wait(get)
+                for row in range(4):
+                    for m in range(3):
+                        made = nt(get(rows)[row], weight.matrix(get, m * 64, 64))
+                        (query if m == 0 else shared).store(get, at, row, m * 256, made)
+            for plan in plans:
+                plan[3].finish(get)
+            swap.finish(get, at)
+
+    (
+        third_p,
+        enc_q,
+        enc_kv,
+        self_q,
+        self_kv,
+        enc_mixed,
+        enc_total,
+        self_mixed,
+        self_total,
+        stream_mid,
+        rows_b,
+        target_mid,
+        rows_d,
+    ) = run_steps(
+        call,
+        [Project(), enc_step, self_step, Stage(call, [job_b, job_d], [enc_o, self_o])],
+        "self_attention",
+        1,
+        58 * MICROSECOND,
+    )
+    third_w = gather_weights(third_p)
 
     call = Call()
     enc_u, enc_d = pick(call, second_w, ENC_UP), pick(call, second_w, ENC_DOWN)
     cross_a, cross_b = pick(call, second_w, Q), pick(call, second_w, KV)
+    cross_o = pick(call, second_w, O)
     feed = Feed(call, rows_b, enc_u, enc_d)
     mid = forward_mid(call, stream_mid, ENC_G + 2, ENC_B + 2)
     shared, query, rows_in = Shared(call, 512), Plain(call, 256), call.fetch(rows_d)
-    job = Job(call, feed, mid, (cross_b, [(0, 64), (64, 64)], shared.store))
+    job_m = Job(call, feed, mid, (cross_b, [(0, 64), (64, 64)], shared.store))
+    cross_step = Attend(call, query.out, shared.out, target_facts, source_keys, False)
+    mid = forward_mid(call, target_mid, DEC_G + 2, DEC_B + 2)
+    job_e = Job(call, (cross_step.mixed, cross_o, [(0, 64)], 0), mid, (None, None, None))
+    slots = Slots(call, [cotangent], True)
 
     def queries(get, at):
         for row in range(4):
             query.store(get, at, row, 0, nt(get(rows_in)[row], cross_a.matrix(get, 0, 64)))
 
-    enc_hidden, enc_slope, stream_end, cross_kv, cross_q, memory = run_stage(
+    (
+        enc_hidden,
+        enc_slope,
+        stream_end,
+        cross_kv,
+        cross_q,
+        memory,
+        cross_mixed,
+        cross_total,
+        target_late,
+        rows_e,
+        grad_out,
+    ) = run_steps(
         call,
-        [job],
-        [enc_u, enc_d, cross_a, cross_b],
-        "memory",
+        [
+            Stage(
+                call,
+                [job_m],
+                [enc_u, enc_d, cross_b, cross_a],
+                shared.finish,
+                True,
+                [Local(queries)],
+            ),
+            cross_step,
+            Stage(call, [job_e], [cross_o], more=[slots]),
+        ],
+        "cross_attention",
         3,
-        shared.finish,
-        24 * MICROSECOND,
-        core=True,
-        more=[Local(queries)],
-    )
-
-    cross_mixed, cross_total = attend(cross_q, cross_kv, target_facts, source_keys, False)
-
-    call = Call()
-    cross_o = pick(call, second_w, O)
-    mid = forward_mid(call, target_mid, DEC_G + 2, DEC_B + 2)
-    slots = Slots(call, [cotangent], True)
-    job = Job(call, (cross_mixed, cross_o, [(0, 64)], 0), mid, (None, None, None))
-    target_late, grad_out, rows_e = run_stage(
-        call, [job], [cross_o], "after_cross", 4, flops=20 * MICROSECOND, more=[slots]
+        52 * MICROSECOND,
     )
 
     call = Call()
     dec_u, dec_d = pick(call, third_w, DEC_UP), pick(call, third_w, DEC_DOWN)
+    cross_o = pick(call, second_w, O)
     feed = Feed(call, rows_e, dec_u, dec_d)
     vec, res, cot = call.take(vectors), call.fetch(target_late), call.fetch(grad_out)
-    decoded_out, grad_end_out = call.keep((128, 1024), BF16), call.keep((128, 1024), F32)
+    decoded_out, grad_end = call.keep((128, 1024), BF16), call.hold((128, 1024), F32)
     share_out = call.give((2, 1024), F32)
 
     def last_mid(get, total):
@@ -1232,62 +1316,78 @@
         unit, unused = unit_of(stream)
         get(decoded_out)[...] = (unit * gain + shift).astype(BF16)
         grad, shares = norm_back(stream, gain, get(cot)[...].astype(F32))
-        get(grad_end_out)[...] = grad
+        get(grad_end)[...] = grad
         get(share_out)[...] = shares
         call.save(get, decoded_out)
-        call.save(get, grad_end_out)
         return grad.astype(BF16)
 
-    job = Job(call, feed, last_mid, (dec_d, [(0, 256)], deactivated(call, feed.slope)))
-    dec_hidden, dec_slope, decoded, grad_end, norm_3, dec_grad_act, grad_rows_e = run_stage(
-        call, [job], [dec_u, dec_d], "turn", 5, flops=24 * MICROSECOND
-    )
-    dec_s = weight_shares(
-        [(dec_grad_act, 0, rows_e), (dec_hidden, 0, grad_rows_e)], 256, 15
-    )
-    dec_g = over_slots(dec_s)
-
-    call = Call()
-    call.take(dec_s, pltpu.HBM)
-    dec_u, cross_o = pick(call, third_w, DEC_UP), pick(call, second_w, O)
+    active = deactivated(call, feed.slope)
+    job_t = Job(call, feed, last_mid, (dec_d, [(0, 256)], active.store))
     mid = backward_mid(call, target_late, DEC_G + 2, grad_end)
     query = Plain(call, 256)
-    job = Job(call, (dec_grad_act, dec_u, [(0, 256)], 0), mid, (cross_o, [(0, 64)], query.store))
-    grad_late, norm_2, cross_grad_mixed, grad_rows_d = run_stage(
-        call, [job], [dec_u, cross_o], "back_cross", 6, flops=20 * MICROSECOND
-    )
-
-    cross_grads = attend_back(
-        cross_q, cross_kv, cross_grad_mixed, cross_total, target_facts, source_keys, False, 7
-    )
-    cross_s = weight_shares(
+    job_c = Job(call, (active.out, dec_u, [(0, 256)], 0), mid, (cross_o, [(0, 64)], query.store))
+    dec_shares = Shares(
+        call, [(active.out, 0, feed.rows), (feed.hidden, 0, job_t.gathered)], 256
+    )
+    back = AttendBack(
+        call, cross_q, cross_kv, query.out, cross_total, target_facts, source_keys, False
+    )
+    cross_shares = Shares(
+        call,
         [
-            (cross_grads, 0, rows_d),
-            (cross_grads, 256, memory),
-            (cross_grads, 512, memory),
-            (cross_mixed, 0, grad_rows_d),
+            (back.out, 0, rows_d),
+            (back.out, 256, memory),
+            (back.out, 512, memory),
+            (cross_mixed, 0, job_c.gathered),
         ],
         64,
-        16,
-    )
-    cross_g = over_slots(cross_s)
+    )
+    (
+        dec_hidden,
+        dec_slope,
+        decoded,
+        norm_3,
+        dec_grad_act,
+        grad_rows_e,
+        grad_late,
+        norm_2,
+        cross_grad_mixed,
+        grad_rows_d,
+        dec_s,
+        cross_grads,
+        cross_s,
+    ) = run_steps(
+        call,
+        [
+            Stage(call, [job_t], [dec_u, dec_d]),
+            Stage(call, [job_c], [cross_o], more=[dec_shares]),
+            back,
+            cross_shares,
+        ],
+        "back_cross",
+        5,
+        60 * MICROSECOND,
+    )
+    dec_g = over_slots(dec_s)
 
     call = Call()
-    call.take(cross_s, pltpu.HBM)
     cross_a, cross_b = pick(call, second_w, Q), pick(call, second_w, KV)
     self_o, enc_d = pick(call, first_w, O, SELF), pick(call, second_w, ENC_DOWN)
     slots = Slots(call, [decoded], False)
     mid = backward_mid(call, target_mid, DEC_G + 1, grad_late)
     query = Plain(call, 256)
-    job_t = Job(
-        call, (cross_grads, cross_a, [(0, 64)], 0), mid, (self_o, [(0, 64)], query.store)
-    )
+    job_t = Job(call, (cross_grads, cross_a, [(0, 64)], 0), mid, (self_o, [(0, 64)], query.store))
     mid = backward_mid(call, stream_end, ENC_G + 2)
+    active = deactivated(call, call.fetch(enc_slope))
     job_s = Job(
         call,
         (cross_grads, cross_b, [(0, 64), (64, 64)], 256),
         mid,
-        (enc_d, [(0, 256)], deactivated(call, call.fetch(enc_slope))),
+        (enc_d, [(0, 256)], active.store),
+    )
+    both = call.give((4, 4, 768, 128), BF16, pltpu.HBM)
+    shares = Shares(
+        call, [(active.out, 0, rows_b), (enc_hidden, 0, job_s.gathered)], 256, both, 256
     )
     (
         decoded,
@@ -1299,84 +1399,93 @@
         enc_norm_2,
         enc_grad_act,
         grad_rows_b,
-    ) = run_stage(
+        both_s,
+    ) = run_steps(
         call,
-        [job_t, job_s],
-        [cross_a, cross_b, self_o, enc_d],
+        [
+            Carry(call, cross_s, both, 0),
+            Stage(call, [job_s, job_t], [cross_a, cross_b, self_o, enc_d], more=[slots]),
+            shares,
+        ],
         "back_both",
         8,
-        flops=38 * MICROSECOND,
-        more=[slots],
-    )
-    feed_s = weight_shares(
-        [(enc_grad_act, 0, rows_b), (enc_hidden, 0, grad_rows_b)], 256, 17
-    )
-    feed_g = over_slots(feed_s)
-
-    self_grads = attend_back(
-        self_q, self_kv, self_grad_mixed, self_total, target_facts, target_keys, True, 9, [feed_s]
-    )
+        46 * MICROSECOND,
+    )
+    both_g = over_slots(both_s)
+
     call = Call()
+    call.take(both_s, pltpu.HBM)
     call.take(dec_g, pltpu.HBM)
-    shares = Shares(
-        call,
-        [
-            (self_grads, 0, rows_c),
-            (self_grads, 256, rows_c),
-            (self_grads, 512, rows_c),
-            (self_mixed, 0, grad_rows_c),
-        ],
-        64,
-    )
     enc_u, enc_o = pick(call, second_w, ENC_UP), pick(call, first_w, O)
     self_a = pick(call, first_w, QKV, SELF)
+    self_back = AttendBack(
+        call, self_q, self_kv, self_grad_mixed, self_total, target_facts, target_keys, True
+    )
     mid = backward_mid(call, stream_mid, ENC_G + 1, grad_stream)
     query = Plain(call, 256)
     job_s = Job(call, (enc_grad_act, enc_u, [(0, 256)], 0), mid, (enc_o, [(0, 64)], query.store))
     mid = backward_mid(call, target_in, DEC_G, grad_mid)
-    job_t = Job(call, (self_grads, self_a, [(0, 64), (64, 64), (128, 64)], 0), mid, None)
+    job_t = Job(call, (self_back.out, self_a, [(0, 64), (64, 64), (128, 64)], 0), mid, None)
+    last = call.give((4, 4, 512, 128), BF16, pltpu.HBM)
+    self_shares = Shares(
+        call,
+        [
+            (self_back.out, 0, rows_c),
+            (self_back.out, 256, rows_c),
+            (self_back.out, 512, rows_c),
+            (self_mixed, 0, grad_rows_c),
+        ],
+        64,
+        last,
+        0,
+    )
+    enc_back = AttendBack(
+        call, enc_q, enc_kv, query.out, enc_total, source_facts, source_keys, False
+    )
+    enc_shares = Shares(
+        call,
+        [
+            (enc_back.out, 0, rows_a),
+            (enc_back.out, 256, rows_a),
+            (enc_back.out, 512, rows_a),
+            (enc_mixed, 0, job_s.gathered),
+        ],
+        64,
+        last,
+        256,
+    )
     (
-        self_s,
+        self_grads,
         grad_stream,
         enc_norm_1,
         enc_grad_mixed,
         grad_rows_a,
         target_grad,
         norm_0,
-    ) = run_stage(
+        last_s,
+        enc_grads,
+    ) = run_steps(
         call,
-        [job_s, job_t],
-        [enc_u, self_a, enc_o],
+        [
+            self_back,
+            Stage(call, [job_s, job_t], [enc_u, self_a, enc_o], more=[self_shares]),
+            enc_back,
+            enc_shares,
+        ],
         "back_self",
         10,
-        flops=28 * MICROSECOND,
-        more=[shares],
-    )
-    self_g = over_slots(self_s)
-
-    enc_grads = attend_back(
-        enc_q, enc_kv, enc_grad_mixed, enc_total, source_facts, source_keys, False, 11, [cross_g]
-    )
-    enc_s = weight_shares(
-        [
-            (enc_grads, 0, rows_a),
-            (enc_grads, 256, rows_a),
-            (enc_grads, 512, rows_a),
-            (enc_mixed, 0, grad_rows_a),
-        ],
-        64,
-        19,
-    )
-    enc_g = over_slots(enc_s)
+        58 * MICROSECOND,
+    )
+    last_g = over_slots(last_s)
 
     call = Call()
-    for done in (enc_s, feed_g):
-        call.take(done, pltpu.HBM)
+    call.take(last_s, pltpu.HBM)
     enc_a = pick(call, first_w, QKV)
     mid = backward_mid(call, stream_in, ENC_G, grad_stream)
     job = Job(call, (enc_grads, enc_a, [(0, 64), (64, 64), (128, 64)], 0), mid, None)
-    source_grad, enc_norm_0 = run_stage(
-        call, [job], [enc_a], "back_first", 12, flops=12 * MICROSECOND
+    swap = Swap(call, [dec_g, both_g])
+    source_grad, enc_norm_0, dec_g, both_g = run_stage(
+        call, [job], [enc_a], "back_first", 12, flops=14 * MICROSECOND, more=[swap]
     )
 
     norm_share = jnp.stack(
@@ -1390,17 +1499,18 @@
         ],
         0,
     )
-    (source_grad, target_grad), swapped, norm_grad = close_program(
+    (source_grad, target_grad), unused, norm_grad = close_program(
         [source_grad.astype(BF16), target_grad.astype(BF16)],
         by_owner(norm_share),
-        [dec_g, cross_g, feed_g, self_g],
+        [],
     )
     norm_grad = norm_grad.reshape(16, copies, 4, 32 // copies)
     if copies > 1:
         norm_grad = lax.psum_scatter(norm_grad, "k", scatter_dimension=1)
     norm_grad = norm_grad.reshape(16, 4, -1)
     norm_grad = lax.dynamic_index_in_dim(norm_grad, z, 1, False)
-    (enc_g,) = swap_packs([enc_g], 20)
+    (last_g,) = swap_packs([last_g], 20)
+    self_g, enc_g = last_g[:, :256], last_g[:, 256:]
 
     def attend_shares(packed):
         grads = unpack(narrow(packed), 4)
@@ -1410,11 +1520,11 @@
         grads = unpack(narrow(packed), 2)
         return grads[0].T, grads[1]
 
-    dec_u, dec_d = feed_shares(swapped[0])
-    enc_u, enc_d = feed_shares(swapped[2])
+    dec_u, dec_d = feed_shares(dec_g)
+    enc_u, enc_d = feed_shares(both_g[:, 256:])
     enc_a, enc_o = attend_shares(enc_g)
-    cross_a, cross_o = attend_shares(swapped[1])
-    self_a, self_o = attend_shares(swapped[3])
+    cross_a, cross_o = attend_shares(both_g[:, :256])
+    self_a, self_o = attend_shares(self_g)
     return (
         decoded,
         source_grad.astype(F32),

time: 506 us -> 480 us (0.949)
  Pallas kernels: 445 us -> 416 us
    pallas_call x23 -> x10, Pallas kernels: 445 us -> 416 us  [run(): pl.pallas_call(kernel, out_shape=tuple(self.shapes), in_specs=self.specs,...]
    unnamed x86 -> x78, local copies, waits for them, and re-layouts: 12 us -> 12.2 us
  transfers between devices with their start and end apart: 8 -> 6, of which waited for: 2 -> 3; matrix products, arithmetic and copies ran while one was open for 2% -> 3% of each run, Pallas kernels for 75% -> 67%
where the time goes in v4:
time: 480 us; the launch traced here: 474 us
  Pallas kernels  416 us (87%)
  local copies, waits for them, and re-layouts  24 us (5%)
  between operations  15.2 us (3%)
  waiting for transfers between devices  13.8 us (3%)
  other arithmetic  4.86 us (1%)
    pallas_call x10, Pallas kernels, run(): pl.pallas_call(kernel, out_shape=tuple(self.shapes), in_specs=self.specs,...  416 us
    unnamed x78, local copies, waits for them, and re-layouts  12.2 us
  transfers between devices with their start and end apart: 6, of which 3 were waited for; matrix products, arithmetic and copies ran while one was open for 3% of the time, Pallas kernels for 67%

profile of v4, /device:TPU:0, one launch (start us, length us, event | category | flops | bytes accessed | tf_op | source)
XLA Modules:
  0.0 474.4 jit_solution(12775477032261689554)
XLA Ops:
  7.4 1.0 fusion.10
  8.8 0.9 fusion.9
  10.1 0.9 constant_dynamic-update-slice_fusion.4
  11.6 25.2 %open_program.1 = (bf16[128,1024]{1,0:T(8,128)(2,1)S(1)}, bf16[128,1024]{1,0:T(8,128)(2,1)S(1)}, bf16[4,512,128]{2,1,0:T(8,128)(2,1)}, f32[16,1024]{1,0:T(8,128)S(1)}, s32[2,40,128]{2,1,0:T(8,128)S(1)}) custom-call(bf16[2,64,1024]{2,1,0:T(8,128)(2,1)S(1)} %copy-done.3, bf16[2,64,1024]{2,1,0:T(8,128)(2,1)S(1)} %copy-done.4, ...), custom_call_target="tpu_custom_call" | custom-call | flops 12000000000 | tf_op jit(solution)/shard_map/open_program/pallas_call | solution.py:109
  39.5 33.0 %first_rows.1 = (bf16[4,128,1024]{2,1,0:T(8,128)(2,1)}, bf16[4,128,1024]{2,1,0:T(8,128)(2,1)}, bf16[4,768,128]{2,1,0:T(8,128)(2,1)}) custom-call(f32[16,1024]{1,0:T(8,128)S(1)} %get-tuple-element.78.refs_0_.refs_8_.refs_2_.refs_3_.refs_10_, bf16[128,1024]{1,0:T(8,128)(2,1)} %copy-done.6, bf16[128,1024]{1,0:T(8,128)(2,1)} %copy-done.7, ...), custom_call_target="tpu_custom_call" | custom-call | flops 24000000000 | tf_op jit(solution)/shard_map/first_rows/pallas_call | solution.py:109
  74.4 1.3 compare_convert_fusion
  76.8 8.4 %all-gather.9.cloned.1.call-done = bf16[32,512,128]{2,1,0:T(8,128)(2,1)} async-done(((bf16[4,512,128]{2,1,0:T(8,128)(2,1)}), bf16[32,512,128]{2,1,0:T(8,128)(2,1)}) %all-gather.9.cloned.1.call-update) | async-done | bytes 4194320 | tf_op jit(solution)/shard_map/all_gather | solution.py:1025
  85.2 64.0 %self_attention.1 = (bf16[4,512,128]{2,1,0:T(8,128)(2,1)}, bf16[4,128,256]{2,1,0:T(8,128)(2,1)}, bf16[2,4,128,512]{3,2,1,0:T(8,128)(2,1)}, bf16[4,128,256]{2,1,0...) custom-call(bf16[4,512,128]{2,1,0:T(8,128)(2,1)S(1)} %bitcast.166, ...), custom_call_target="tpu_custom_call" | custom-call | flops 57999998976 | tf_op jit(solution)/shard_map/self_attention/pallas_call | solution.py:109
  149.4 1.0 all-gather.7.cloned.1.call-done
  150.4 60.2 %cross_attention.1 = (bf16[4,128,1024]{2,1,0:T(8,128)(2,1)}, f32[4,128,1024]{2,1,0:T(8,128)}, f32[128,1024]{1,0:T(8,128)}, bf16[2,4,128,512]{3,2,1,0:T(8,128)(2,...) custom-call(bf16[2,4,4,768,128]{4,3,2,1,0:T(8,128)(2,1)} %bitcast.22, ...), custom_call_target="tpu_custom_call" | custom-call | flops 51999997952 | tf_op jit(solution)/shard_map/cross_attention/pallas_call | solution.py:109
  211.3 63.4 %back_cross.1 = (bf16[4,128,1024]{2,1,0:T(8,128)(2,1)}, f32[4,128,1024]{2,1,0:T(8,128)}, bf16[128,1024]{1,0:T(8,128)(2,1)}, f32[2,1024]{1,0:T(2,128)S(1)}, bf16[...) custom-call(bf16[2,4,4,512,128]{4,3,2,1,0:T(8,128)(2,1)} %bitcast.23, ...), custom_call_target="tpu_custom_call" | custom-call | flops 60000002048 | tf_op jit(solution)/shard_map/back_cross/pallas_call | solution.py:109
  274.7 0.9 copy-done.8
  275.6 50.7 %back_both.1 = (bf16[2,64,1024]{2,1,0:T(8,128)(2,1)S(1)}, f32[128,1024]{1,0:T(8,128)}, f32[2,1024]{1,0:T(2,128)S(1)}, bf16[4,128,256]{2,1,0:T(8,128)(2,1)}, bf16...) custom-call(bf16[2,4,4,768,128]{4,3,2,1,0:T(8,128)(2,1)} %bitcast.23, ...), custom_call_target="tpu_custom_call" | custom-call | flops 46000001024 | tf_op jit(solution)/shard_map/back_both/pallas_call | solution.py:109
  326.8 54.7 %back_self.1 = (bf16[4,128,768]{2,1,0:T(8,128)(2,1)}, f32[128,1024]{1,0:T(8,128)}, f32[2,1024]{1,0:T(2,128)S(1)}, bf16[4,128,256]{2,1,0:T(8,128)(2,1)}, bf16[4,1...) custom-call(bf16[4,4,768,128]{3,2,1,0:T(8,128)(2,1)} %get-tuple-elem, ...), custom_call_target="tpu_custom_call" | custom-call | flops 57999998976 | tf_op jit(solution)/shard_map/back_self/pallas_call | solution.py:109
  381.6 1.1 convert_element_type.40.refs_1_
  382.8 4.4 reduce-scatter.6.cloned.1.call-done
  387.1 1.1 copy-done
  388.3 29.0 %back_first.1 = (f32[128,1024]{1,0:T(8,128)}, f32[2,1024]{1,0:T(2,128)S(1)}, bf16[4,512,128]{2,1,0:T(8,128)(2,1)S(1)}, bf16[4,768,128]{2,1,0:T(8,128)(2,1)S(1)}) custom-call(bf16[4,4,512,128]{3,2,1,0:T(8,128)(2,1)} %get-tuple-element.122.refs_0_, bf16[2,4,4,512,128]{4,3,2,1,0:T(8,128)(2,1)} %bitcast.235, ...), custom_call_target="tpu_custom_call" | custom-call | flops 14000000000 | tf_op jit(solution)/shard_map/back_first/pallas_call | solution.py:109
  417.5 0.7 slice.239
  418.3 0.9 fusion.6
  419.1 1.0 copy.187
  420.2 0.9 fusion.5
  421.1 1.0 copy.188
  422.2 27.1 %close_program.1 = (bf16[2,64,1024]{2,1,0:T(8,128)(2,1)S(1)}, bf16[2,64,1024]{2,1,0:T(8,128)(2,1)S(1)}, f32[16,128]{1,0:T(8,128)S(1)}) custom-call(bf16[128,1024]{1,0:T(8,128)(2,1)S(1)} %convert_element_type.39.refs_0_, bf16[128,1024]{1,0:T(8,128)(2,1)S(1)} %convert_element_type.40.refs_1_, f32[16,1024]{1,0:T(8,128)S(1)} %maximum_maximum_fusion.refs_2_), custom_call_target="tpu_custom_call" | custom-call | flops 16000000000 | tf_op jit(solution)/shard_map/close_program/pallas_call | solution.py:109
  449.3 0.8 convert_element_type.41
  450.2 0.8 convert_element_type.42
  451.0 0.9 copy.184
  453.8 1.0 copy-done.2
  454.8 8.5 %swap_packs.1 = bf16[4,512,128]{2,1,0:T(8,128)(2,1)S(1)} custom-call(bf16[4,512,128]{2,1,0:T(8,128)(2,1)S(1)} %bitcast.178), custom_call_target="tpu_custom_call" | custom-call | flops 5000000000 | tf_op jit(solution)/shard_map/swap_packs/pallas_call | solution.py:109
  464.8 0.9 copy.182
  465.7 0.9 copy.183
  466.7 0.7 copy.222
  (177 shorter events, 12.0 us)
Async XLA Ops:
  7.2 3.8 copy-start.17
  7.2 3.9 copy-start.21
  7.2 3.9 slice-start.1
  7.2 3.9 copy-start.22
  7.2 3.9 copy-start.23
  7.2 3.9 copy-start.24
  7.3 4.1 copy-start.25
  7.3 4.2 copy-start.26
  7.3 4.2 copy-start.20
  7.3 4.2 copy-start.19
  7.3 4.3 copy-start.3
  7.3 4.3 copy-start.4
  7.3 77.9 %all-gather.9.cloned.1.call-start = ((), (), s32[]{:S(2)}) async-start(), calls=%async_computation.7 | async-start | bytes 4718592 | tf_op jit(solution)/shard_map/all_gather | solution.py:1025
  11.6 26.8 %copy-start.16 = (bf16[3,128,256]{2,1,0:T(8,128)(2,1)S(1)}, bf16[3,128,256]{2,1,0:T(8,128)(2,1)}, u32[]{:S(2)}) copy-start(bf16[3,128,256]{2,1,0:T(8,128)(2,1)} %param.36) | copy-start | bytes 589828
  11.6 27.1 %copy-start.18 = (bf16[256,128]{1,0:T(8,128)(2,1)S(1)}, bf16[256,128]{1,0:T(8,128)(2,1)}, u32[]{:S(2)}) copy-start(bf16[256,128]{1,0:T(8,128)(2,1)} %param.37) | copy-start | bytes 196612
  38.3 0.9 copy-start.12
  38.3 1.1 copy-start.14
  38.3 112.1 %all-gather.7.cloned.1.call-start = ((), (), s32[]{:S(2)}) async-start(), calls=%async_computation.6 | async-start | bytes 7077888 | tf_op jit(solution)/shard_map/all_gather | solution.py:1025
  72.5 3.9 copy-start.13
  72.6 4.1 copy-start.15
  72.6 138.7 %all-gather.11.cloned.1.call-start = ((), (), s32[]{:S(2)}) async-start(), calls=%async_computation.8 | async-start | bytes 4718592 | tf_op jit(solution)/shard_map/all_gather | solution.py:1025
  85.2 65.2 %copy-start.5 = (bf16[2,64,1024]{2,1,0:T(8,128)(2,1)S(1)}, bf16[2,64,1024]{2,1,0:T(8,128)(2,1)}, u32[]{:S(2)}) copy-start(bf16[2,64,1024]{2,1,0:T(8,128)(2,1)} %refs_8_.1) | copy-start | bytes 786436
  149.2 177.6 %reduce-scatter.4.cloned.1.call-start = ((), (), s32[]{:S(2)}) async-start(), calls=%async_computation.3 | async-start | bytes 2621440 | tf_op jit(solution)/shard_map/reduce_scatter | solution.py:1015
  274.7 1.0 copy-start.8
  274.7 112.5 %reduce-scatter.6.cloned.1.call-start = ((), (), s32[]{:S(2)}) async-start(), calls=%async_computation.4 | async-start | bytes 3932160 | tf_op jit(solution)/shard_map/reduce_scatter | solution.py:1015
  326.3 127.5 %reduce-scatter.8.cloned.1.call-start = ((), (), s32[]{:S(2)}) async-start(), calls=%async_computation.5 | async-start | bytes 2621440 | tf_op jit(solution)/shard_map/reduce_scatter | solution.py:1015
  381.6 5.6 %copy-start.1 = (bf16[1,4,512,128]{3,2,1,0:T(8,128)(2,1)S(1)}, bf16[1,4,512,128]{3,2,1,0:T(8,128)(2,1)}, u32[]{:S(2)}) copy-start(bf16[1,4,512,128]{3,2,1,0:T(8,128)(2,1)} %reduce-scatter.4.cloned.1.call-done) | copy-start | bytes 1572868
  387.1 1.1 copy-start
  417.5 1.7 copy-start.10
  420.1 2.0 copy-start.11
  422.2 28.8 %slice-start = ((f32[4,4,64,128]{3,2,1,0:T(8,128)}), f32[3,4,64,128]{3,2,1,0:T(8,128)S(1)}, s32[]{:S(2)}) async-start(f32[4,4,64,128]{3,2,1,0:T(8,128)} %copy-done.10), calls=%async_computation.9 | async-start | bytes 786432 | tf_op jit(solution)/shard_map/slice | solution.py:1517
  453.8 1.0 copy-start.2
  (3 other events, 2.1 us)
Sparse Core Ops, SparseCore 0:
  38.4 46.7 all-gather.8
  86.8 63.5 all-gather.6
  152.0 45.7 all-gather.10
  274.8 49.3 reduce-scatter.3
  326.5 60.6 reduce-scatter.5
  389.4 55.7 reduce-scatter.7

commit v5 on v4

v5 whole, which is shorter than its diff:
```python
import math

import jax
import jax.numpy as jnp
from jax import lax
from jax.experimental import pallas as pl
from jax.experimental.pallas import tpu as pltpu
from jax.sharding import Mesh, PartitionSpec as P

HEAD_DIM = 64
EPSILON = 1e-05
MASKED = -1000000000.0
PAIRS = 8
AXES = ("hi", "k", "y", "c", "mp")
MESH_ID = pl.DeviceIdType.MESH
F32 = jnp.float32
BF16 = jnp.bfloat16


class Call:
    def __init__(self):
        self.known, self.arrays, self.specs = [], [], []
        self.shapes, self.places, self.scratch = [], [], []
        self.fetched, self.kept, self.rows_of = [], [], {}

    def take(self, array, space=pltpu.VMEM):
        if isinstance(array, tuple):
            return array
        for i, known in enumerate(self.known):
            if known is array and self.specs[i].memory_space == space:
                return ("in", i)
        self.known.append(array)
        if space == pltpu.HBM:
            array = pltpu.with_memory_space_constraint(array, pltpu.HBM)
        self.arrays.append(array)
        self.specs.append(pl.BlockSpec(memory_space=space))
        return ("in", len(self.arrays) - 1)

    def fetch(self, array):
        if isinstance(array, tuple):
            return array
        source = self.take(array, pltpu.HBM)
        for i, (known, room, sem) in enumerate(self.fetched):
            if known == source:
                return ("fetch", i)
        self.fetched.append((source, self.hold(array.shape, array.dtype), self.sems(1)))
        return ("fetch", len(self.fetched) - 1)

    def give(self, shape, dtype, space=pltpu.VMEM):
        if space == pltpu.HBM:
            self.shapes.append(pltpu.HBM(shape, dtype))
        else:
            self.shapes.append(jax.ShapeDtypeStruct(shape, dtype))
        self.places.append(pl.BlockSpec(memory_space=space))
        return ("out", len(self.shapes) - 1)

    def keep(self, shape, dtype, parts=1):
        target = self.give(shape, dtype, pltpu.HBM)
        self.kept.append((target, self.hold(shape, dtype), self.sems(parts)))
        return ("keep", len(self.kept) - 1)

    def hold(self, shape, dtype):
        self.scratch.append(pltpu.VMEM(shape, dtype))
        return ("tmp", len(self.scratch) - 1)

    def sems(self, count):
        self.scratch.append(pltpu.SemaphoreType.DMA((count,)))
        return ("tmp", len(self.scratch) - 1)

    def save(self, get, handle, row=None):
        target, room, sems = (get(part) for part in self.kept[handle[1]])
        if row is not None:
            target, room = target.at[row], room.at[row]
        count = sum(1 for known, unused in self.saves if known == handle)
        copy = pltpu.make_async_copy(room, target, sems.at[count])
        copy.start()
        self.saves.append((handle, copy))

    def run(self, body, name, collective=None, flops=0):
        ins, outs = len(self.arrays), len(self.shapes)

        def kernel(*refs):
            parts = {"in": refs[:ins], "out": refs[ins : ins + outs], "tmp": refs[ins + outs :]}
            here, self.saves, self.waited = set(), [], []

            def get(handle):
                kind, i = handle
                if kind == "keep":
                    return get(self.kept[i][1])
                if kind != "fetch":
                    return parts[kind][i]
                source, room, sem = (get(part) for part in self.fetched[i])
                if i not in here:
                    here.add(i)
                    pltpu.make_async_copy(source, room, sem.at[0]).wait()
                return room

            for source, room, sem in self.fetched:
                pltpu.make_async_copy(get(source), get(room), get(sem).at[0]).start()
            body(get)
            for i in range(len(self.fetched)):
                get(("fetch", i))
            for handle, copy in self.saves:
                copy.wait()

        held = [a for a, spec in zip(self.arrays, self.specs) if spec.memory_space == pltpu.VMEM]
        held += [a for a, spec in zip(self.shapes, self.places) if spec.memory_space == pltpu.VMEM]
        held += [x for x in self.scratch if x.dtype in (BF16, F32)]
        room = sum(math.prod(x.shape) * jnp.dtype(x.dtype).itemsize for x in held)
        return pl.pallas_call(
            kernel,
            out_shape=tuple(self.shapes),
            in_specs=self.specs,
            out_specs=tuple(self.places),
            scratch_shapes=self.scratch,
            compiler_params=pltpu.CompilerParams(
                collective_id=collective,
                has_side_effects=collective is not None,
                vmem_limit_bytes=room + (8 << 20),
            ),
            cost_estimate=pl.CostEstimate(flops=flops, bytes_accessed=0, transcendentals=0),
            name=name,
        )(*self.arrays)


MICROSECOND = 1_000_000_000


def nt(left, right):
    return lax.dot_general(left, right, (((1,), (1,)), ((), ())), preferred_element_type=F32)


def nn(left, right):
    return lax.dot_general(left, right, (((1,), (0,)), ((), ())), preferred_element_type=F32)


def tn(left, right):
    return lax.dot_general(left, right, (((0,), (0,)), ((), ())), preferred_element_type=F32)


def unit_of(stream):
    average = jnp.mean(stream, -1, keepdims=True)
    centred = stream - average
    scale = lax.rsqrt(jnp.mean(centred * centred, -1, keepdims=True) + EPSILON)
    return centred * scale, scale


def norm_back(stream, gain, upstream):
    unit, scale = unit_of(stream)
    inner = upstream * gain
    grad = scale * (
        inner - jnp.mean(inner, -1, keepdims=True) - unit * jnp.mean(inner * unit, -1, keepdims=True)
    )
    shares = jnp.concatenate(
        [jnp.sum(upstream * unit, 0, keepdims=True), jnp.sum(upstream, 0, keepdims=True)], 0
    )
    return grad, shares


def gelu_pair(act):
    bell = 0.5 + 0.5 * lax.erf(act * 0.7071067811865476)
    slope = bell + act * (jnp.exp(act * act * -0.5) * 0.3989422804014327)
    return act * bell, slope


def place():
    hi, k, y, c, z = (lax.axis_index(name) for name in AXES)
    return {
        "x": (1 - hi, k, y, c, z),
        "y": (hi, k, 1 - y, c, z),
        "d": (1 - hi, k, 1 - y, c, z),
        "core": (hi, k, y, 1 - c, z),
        "mesh": (hi, k, y, c, z),
        "own_row": y * 2 + hi,
        "x_row": y * 2 + 1 - hi,
        "y_row": (1 - y) * 2 + hi,
        "d_row": (1 - y) * 2 + 1 - hi,
    }


def greet(partners):
    barrier = pltpu.get_barrier_semaphore()
    for partner in partners:
        pl.semaphore_signal(barrier, inc=1, device_id=partner, device_id_type=MESH_ID)
    pl.semaphore_wait(barrier, len(partners))


def along(at):
    hi, k, y, c, z = at["mesh"]
    return [(hi, k, y, c, lax.rem(z + n, 4)) for n in range(1, 4)]


class Weight:
    def __init__(self, call, packed, first, count):
        self.call, self.source = call, call.take(packed, pltpu.HBM)
        self.room = call.hold((4, count, 1024), BF16)
        self.sem = call.sems(1)
        self.first, self.count = first, count

    def start(self, get):
        source, room, sem = get(self.source), get(self.room), get(self.sem)
        for q in range(4):
            for c in range(2):
                pltpu.make_async_copy(
                    source.at[c, :, q, pl.ds(self.first, self.count), :],
                    room.at[:, :, pl.ds((q * 2 + c) * 128, 128)],
                    sem.at[0],
                ).start()

    def wait(self, get):
        if self in self.call.waited:
            return
        self.call.waited.append(self)
        room = get(self.room)
        pltpu.make_async_copy(room, room, get(self.sem).at[0]).wait()

    def matrix(self, get, first, count):
        return get(self.room)[:, first : first + count, :].reshape(4 * count, 1024)


def stack(blocks):
    return blocks[0] if len(blocks) == 1 else jnp.concatenate(blocks, 0)


class Feed:
    def __init__(self, call, rows, up, down):
        self.call, self.rows, self.weights = call, call.fetch(rows), [up, down]
        self.hidden = call.keep((4, 128, 1024), BF16, 4)
        self.slope = call.keep((4, 128, 1024), F32, 4)

    def part(self, get, *rows):
        up, down = self.weights
        whole = stack([get(self.rows)[row] for row in rows])
        made, slope = gelu_pair(nt(whole, up.matrix(get, 0, 256)))
        made = made.astype(BF16)
        for i, row in enumerate(rows):
            get(self.hidden)[row] = made[i * 128 : (i + 1) * 128]
            get(self.slope)[row] = slope[i * 128 : (i + 1) * 128]
            self.call.save(get, self.hidden, row)
            self.call.save(get, self.slope, row)
        return nn(made, down.matrix(get, 0, 256))


class Job:
    def __init__(self, call, left, mid, right):
        self.call, self.left, self.mid, self.right = call, left, mid, right
        self.kept, self.shares = getattr(mid, "kept", None), getattr(mid, "shares", None)
        if left is not None:
            self.rows_in = None if isinstance(left, Feed) else call.fetch(left[0])
            self.out_first = call.hold((2, 128, 1024), BF16)
            self.out_edge = call.hold((2, 64, 1024), BF16)
            self.out_late = call.hold((2, 64, 1024), BF16)
            self.keep = call.hold((2, 64, 1024), F32)
            self.own = call.hold((128, 1024), F32)
            self.landed = call.hold((6, 64, 1024), BF16)
            self.sum_send, self.sum_recv = call.sems(6), call.sems(6)
        self.gathered = None
        if right is not None:
            self.gathered = call.keep((4, 128, 1024), BF16, 4)
            self.row_send, self.row_recv = call.sems(6), call.sems(6)

    def lefts(self):
        return self.left.weights if isinstance(self.left, Feed) else [self.left[1]]

    def part(self, get, *rows):
        if isinstance(self.left, Feed):
            return self.left.part(get, *rows)
        unused, weight, picks, column = self.left
        total = None
        for first, count in picks:
            width = 4 * count
            left = stack([get(self.rows_in)[row, :, column : column + width] for row in rows])
            term = nn(left, weight.matrix(get, first, count))
            total = term if total is None else total + term
            column += width
        return total

    def send(self, get, i, source, target, partner):
        copy = pltpu.make_async_remote_copy(
            src_ref=source,
            dst_ref=target,
            send_sem=get(self.sum_send).at[i],
            recv_sem=get(self.sum_recv).at[i],
            device_id=partner,
            device_id_type=MESH_ID,
        )
        copy.start()
        return copy

    def sum_start(self, get, at):
        first, edge, landed = get(self.out_first), get(self.out_edge), get(self.landed)
        keep = get(self.keep)
        self.copies = [None] * 6
        first[0] = self.part(get, at["d_row"]).astype(BF16)
        self.copies[0] = self.send(
            get, 0, first.at[0, pl.ds(0, 64)], landed.at[0], at["x"]
        )
        self.copies[1] = self.send(
            get, 1, first.at[0, pl.ds(64, 64)], landed.at[1], at["y"]
        )
        part = self.part(get, at["x_row"], at["y_row"])
        edge[0] = part[:64].astype(BF16)
        keep[0] = part[64:128]
        self.copies[2] = self.send(get, 2, edge.at[0], landed.at[2], at["x"])
        edge[1] = part[192:].astype(BF16)
        keep[1] = part[128:192]
        self.copies[3] = self.send(get, 3, edge.at[1], landed.at[3], at["y"])

    def sum_forward(self, get, at):
        late, landed, keep = get(self.out_late), get(self.landed), get(self.keep)
        self.copies[0].wait_recv()
        late[1] = (keep[1] + landed[0].astype(F32)).astype(BF16)
        self.copies[4] = self.send(get, 4, late.at[1], landed.at[4], at["y"])
        self.copies[1].wait_recv()
        late[0] = (keep[0] + landed[1].astype(F32)).astype(BF16)
        self.copies[5] = self.send(get, 5, late.at[0], landed.at[5], at["x"])

    def sum_own(self, get, at):
        get(self.own)[...] = self.part(get, at["own_row"])

    def sum_end(self, get):
        landed, own = get(self.landed), get(self.own)
        for i in (2, 3, 4, 5):
            self.copies[i].wait_recv()
        upper = own[:64] + landed[2].astype(F32) + landed[4].astype(F32)
        lower = own[64:] + landed[5].astype(F32) + landed[3].astype(F32)
        return jnp.concatenate([upper, lower], 0)

    def row_copy(self, get, i, row, half, partner):
        block = get(self.gathered).at[row, pl.ds(half * 64, 64)]
        copy = pltpu.make_async_remote_copy(
            src_ref=block,
            dst_ref=block,
            send_sem=get(self.row_send).at[i],
            recv_sem=get(self.row_recv).at[i],
            device_id=partner,
            device_id_type=MESH_ID,
        )
        copy.start()
        return copy

    def rows_start(self, get, at, normed):
        get(self.gathered)[at["own_row"]] = normed
        self.call.save(get, self.gathered, at["own_row"])
        self.moves = [
            self.row_copy(get, 0, at["own_row"], 0, at["y"]),
            self.row_copy(get, 1, at["own_row"], 1, at["x"]),
            self.row_copy(get, 2, at["own_row"], 1, at["y"]),
            self.row_copy(get, 3, at["own_row"], 0, at["x"]),
        ]

    def rows_forward(self, get, at):
        self.moves[0].wait_recv()
        self.moves.append(self.row_copy(get, 4, at["y_row"], 0, at["x"]))
        self.moves[1].wait_recv()
        self.moves.append(self.row_copy(get, 5, at["x_row"], 1, at["y"]))

    def product(self, get, at, row):
        weight, picks, store = self.right
        if weight is None:
            return
        weight.wait(get)
        rows = get(self.gathered)[row]
        column = 0
        for first, count in picks:
            store(get, at, row, column, nt(rows, weight.matrix(get, first, count)))
            column += 4 * count

    def sums(self, get, at):
        for weight in self.lefts():
            weight.wait(get)
        self.sum_start(get, at)

    def settle(self, get, at):
        normed = self.mid(get, self.sum_end(get) if self.left is not None else None)
        if self.right is not None:
            self.rows_start(get, at, normed)

    def collect(self, get, at, sides=True, far=True):
        for moves, row in (((3,), "x_row"), ((2,), "y_row"), ((4, 5), "d_row")):
            if far if row == "d_row" else sides:
                for i in moves:
                    self.moves[i].wait_recv()
                self.call.save(get, self.gathered, at[row])
                self.product(get, at, at[row])

    def drain(self):
        if self.left is not None:
            for copy in self.copies:
                copy.wait_send()
        if self.right is not None:
            for copy in self.moves:
                copy.wait_send()


def run_body(call, work, names, name, collective, flops):
    groups = {"all": meeting, "z": along, "ways": lambda at: all_partners(at)[1]}

    def body(get):
        at = place()
        partners = []
        for group in names:
            partners += groups[group](at) if group in groups else [at[group]]
        greet(partners)
        work(get, at)

    return call.run(body, name, collective, flops)


class Kept:
    def __init__(self, out, store):
        self.out, self.store = out, store


class Plain:
    def __init__(self, call, width):
        self.call, self.width = call, width
        self.out = call.keep((4, 128, width), BF16, 4)

    def store(self, get, at, row, column, value):
        get(self.out)[row, :, column : column + value.shape[1]] = value.astype(BF16)
        if column + value.shape[1] == self.width:
            self.call.save(get, self.out, row)


class Shared:
    def __init__(self, call, width, skip=0):
        self.call, self.out = call, call.keep((2, 4, 128, width), BF16, 2)
        self.send_sem, self.recv_sem = call.sems(4), call.sems(4)
        self.width, self.skip, self.copies, self.blocks = width, skip, [], 0

    def store(self, get, at, row, column, value):
        out = get(self.out)
        column = column - self.skip
        out[0, row, :, column : column + value.shape[1]] = value.astype(BF16)
        if column + value.shape[1] == self.width:
            i = len(self.copies)
            copy = pltpu.make_async_remote_copy(
                src_ref=out.at[0, row],
                dst_ref=out.at[1, row],
                send_sem=get(self.send_sem).at[i],
                recv_sem=get(self.recv_sem).at[i],
                device_id=at["core"],
                device_id_type=MESH_ID,
            )
            copy.start()
            self.copies.append(copy)

    def finish(self, get):
        self.call.save(get, self.out, 0)
        for copy in self.copies:
            copy.wait()
        self.call.save(get, self.out, 1)


def query_and_shared(call, width):
    query, shared = Plain(call, width), Shared(call, 2 * width, skip=width)

    def store(get, at, row, column, value):
        if column < width:
            query.store(get, at, row, column, value)
        else:
            shared.store(get, at, row, column, value)

    return store, shared.finish


def lanes_of(head, rows):
    lane = lax.broadcasted_iota(jnp.int32, (rows, 128), 1)
    return lane // HEAD_DIM == head


SOURCE, TARGET, PLACE, LIVE = 0, 1, 2, 3


def allowed_bias(rows, columns, query_kind, key_kind, causal):
    allowed = columns[:, key_kind : key_kind + 1] == rows[query_kind : query_kind + 1, :512]
    allowed = allowed & (columns[:, LIVE + key_kind : LIVE + key_kind + 1] > 0.5)
    if causal:
        allowed = allowed & (columns[:, PLACE : PLACE + 1] <= rows[PLACE : PLACE + 1, :512])
    return jnp.where(allowed, 0.0, MASKED)


class Attend:
    def __init__(self, call, queries, key_value, rows, columns, kinds):
        self.call, self.kinds = call, kinds
        self.queries, self.key_value = call.fetch(queries), call.fetch(key_value)
        self.rows, self.columns = call.take(rows), call.fetch(columns)
        self.mixed = call.keep((4, 128, 256), BF16)
        self.total = call.give((8, 512), F32)
        self.bias = call.hold((1024, 512), F32)

    def late(self, get, at):
        self.prepare(get)
        self.pairs(get, 0, 2)
        self.call.save(get, self.mixed)

    def prepare(self, get):
        mask = get(self.bias)
        mask[...] = allowed_bias(get(self.rows), get(self.columns), *self.kinds)

    def pairs(self, get, first, last):
        mask = get(self.bias)
        q_ref, kv_ref = get(self.queries), get(self.key_value)
        mixed_ref, total_ref = get(self.mixed), get(self.total)

        def pair_step(pair, carry):
            lanes = pl.ds(pl.multiple_of(pair * 128, 128), 128)
            value_lanes = pl.ds(pl.multiple_of(256 + pair * 128, 128), 128)
            keys = kv_ref[:, :, :, lanes].reshape(1024, 128)
            values = kv_ref[:, :, :, value_lanes].reshape(1024, 128)
            for block in range(2):
                span = slice(block * 256, block * 256 + 256)
                queries = q_ref[2 * block : 2 * block + 2, :, lanes].reshape(256, 128)
                mixed = []
                for head in range(2):
                    picked = jnp.where(lanes_of(head, 256), queries * 0.125, 0.0).astype(BF16)
                    scores = nt(keys, picked) + mask[:, span]
                    top = jnp.max(scores, 0, keepdims=True)
                    raised = jnp.exp(scores - top)
                    total = jnp.sum(raised, 0, keepdims=True)
                    probs = (raised * (1.0 / total)).astype(BF16)
                    mixed.append(tn(values, probs)[head * HEAD_DIM : (head + 1) * HEAD_DIM])
                    total_ref[pl.ds(pair * 2 + head, 1), span] = top + jnp.log(total)
                mixed = jnp.concatenate(mixed, 0).T.astype(BF16)
                mixed_ref[2 * block : 2 * block + 2, :, lanes] = mixed.reshape(2, 128, 128)
            return carry

        lax.fori_loop(first, last, pair_step, 0)


class AttendBack:
    def __init__(self, call, queries, key_value, grad_mixed, total, rows, columns, kinds):
        self.call, self.kinds = call, kinds
        self.queries, self.key_value = call.fetch(queries), call.fetch(key_value)
        self.grad_mixed, self.total = call.fetch(grad_mixed), call.take(total)
        self.rows, self.columns = call.take(rows), call.fetch(columns)
        self.out = call.keep((4, 128, 768), BF16)
        self.bias, self.sums = call.hold((1024, 512), F32), call.hold((1024, 512), F32)
        self.away, self.landed = call.hold((2, 512, 256), BF16), call.hold((2, 512, 256), BF16)
        self.send_sem, self.recv_sem = call.sems(2), call.sems(2)

    def partners(self, at):
        return [at["core"]]

    def late(self, get, at):
        self.prepare(get)
        for pair in range(2):
            self.pair(get, at, pair)
        self.end(get)

    def prepare(self, get):
        mask = get(self.bias)
        mask[...] = allowed_bias(get(self.rows), get(self.columns), *self.kinds)
        self.copies = []

    def pair(self, get, at, pair):
        out, mask, sums = get(self.out), get(self.bias), get(self.sums)
        away, here = get(self.away), get(self.landed)
        q_ref, kv_ref = get(self.queries), get(self.key_value)
        grad_ref, total_ref = get(self.grad_mixed), get(self.total)
        lanes = slice(pair * 128, pair * 128 + 128)
        keys_pair = kv_ref[:, :, :, lanes].reshape(1024, 128)
        values_pair = kv_ref[:, :, :, 256 + pair * 128 : 384 + pair * 128].reshape(1024, 128)
        key_sum = slice(pair * 256, pair * 256 + 128)
        value_sum = slice(pair * 256 + 128, pair * 256 + 256)
        for block in range(2):
            span = slice(block * 256, block * 256 + 256)
            two = slice(2 * block, 2 * block + 2)
            q_block = q_ref[two, :, lanes].reshape(256, 128)
            g_block = grad_ref[two, :, lanes].reshape(256, 128)
            grad_query = []
            for head in range(2):
                inside = lanes_of(head, 256)
                picked = jnp.where(inside, q_block * 1.0, 0.0).astype(BF16)
                grads = jnp.where(inside, g_block * 1.0, 0.0).astype(BF16)
                scores = nt(keys_pair, picked) * 0.125 + mask[:, span]
                probs = jnp.exp(scores - total_ref[pair * 2 + head : pair * 2 + head + 1, span])
                weighted = probs * nt(values_pair, grads)
                inner = jnp.sum(weighted, 0, keepdims=True)
                grad_raw = ((weighted - probs * inner) * 0.125).astype(BF16)
                value_term = nn(probs.astype(BF16), grads)
                key_term = nn(grad_raw, picked)
                if block == 0 and head == 0:
                    sums[:, key_sum] = key_term
                    sums[:, value_sum] = value_term
                else:
                    sums[:, key_sum] += key_term
                    sums[:, value_sum] += value_term
                grad_query.append(tn(keys_pair, grad_raw)[head * HEAD_DIM : (head + 1) * HEAD_DIM])
            grad_query = jnp.concatenate(grad_query, 0).T.astype(BF16)
            out[two, :, lanes] = grad_query.reshape(2, 128, 128)
        away[pair] = sums[512:, pair * 256 : pair * 256 + 256].astype(BF16)
        copy = pltpu.make_async_remote_copy(
            src_ref=away.at[pair],
            dst_ref=here.at[pair],
            send_sem=get(self.send_sem).at[pair],
            recv_sem=get(self.recv_sem).at[pair],
            device_id=at["core"],
            device_id_type=MESH_ID,
        )
        copy.start()
        self.copies.append(copy)

    def end(self, get):
        out, sums, here = get(self.out), get(self.sums), get(self.landed)
        for pair in range(2):
            self.copies[pair].wait()
            both = sums[:512, pair * 256 : pair * 256 + 256] + here[pair].astype(F32)
            both = both.astype(BF16).reshape(4, 128, 256)
            out[:, :, 256 + pair * 128 : 384 + pair * 128] = both[:, :, :128]
            out[:, :, 512 + pair * 128 : 640 + pair * 128] = both[:, :, 128:]
        self.call.save(get, self.out)


class Shares:
    def __init__(self, call, pairs, count, out=None, base=0):
        self.call, self.count, self.base = call, count, base
        self.handles = [
            (call.fetch(left), column, call.fetch(right))
            for left, column, right in pairs
        ]
        shape = (4, 4, len(pairs) * count, 128)
        sends = len(pairs) * max(1, count // 64)
        self.made, self.landed = call.hold((2,) + shape, BF16), call.hold(shape, BF16)
        self.send_sem, self.recv_sem = call.sems(sends), call.sems(sends)
        self.rows = shape[2]
        self.out = call.give(shape, BF16, pltpu.HBM) if out is None else out
        self.saved = out is not False
        self.room, self.save_sem = call.hold(shape, BF16), call.sems(1)

    def partners(self, at):
        return [at["core"]]

    def send(self, get, at, part):
        i = len(self.copies)
        copy = pltpu.make_async_remote_copy(
            src_ref=get(self.made).at[(1 - lax.axis_index("c"),) + part],
            dst_ref=get(self.landed).at[part],
            send_sem=get(self.send_sem).at[i],
            recv_sem=get(self.recv_sem).at[i],
            device_id=at["core"],
            device_id_type=MESH_ID,
        )
        copy.start()
        self.copies.append((part, copy))

    def middle(self, get, at):
        self.copies, every, count = [], slice(None), self.count
        made = get(self.made)
        for m, (left, column, right) in enumerate(self.handles):
            left, right = get(left), get(right)
            span = slice(m * count, (m + 1) * count)
            for first in range(0, 4 * count, 256):
                start = column + first
                product = tn(
                    left[:, :, start : start + 256].reshape(512, 256), right[...].reshape(512, 1024)
                )
                for inner in range(0, 256, count):
                    z = (first + inner) // count
                    for d in range(8):
                        made[d % 2, z, d // 2, span, :] = product[
                            inner : inner + count, d * 128 : d * 128 + 128
                        ].astype(BF16)
                if count == 256:
                    self.send(get, at, (first // 256, every, pl.ds(m * count, count)))
            if count < 256:
                self.send(get, at, (every, every, pl.ds(m * count, count)))

    def finish(self, get, at):
        core = lax.axis_index("c")
        for part, copy in self.copies:
            copy.wait()
            own = get(self.made)[(core,) + part].astype(F32)
            get(self.room)[part] = (own + get(self.landed)[part].astype(F32)).astype(BF16)
        if not self.saved:
            return
        target = get(self.out).at[:, :, pl.ds(self.base, self.rows)]
        copy = pltpu.make_async_copy(get(self.room), target, get(self.save_sem).at[0])
        copy.start()
        self.call.saves.append((None, copy))


def push(source, target, send_sem, recv_sem, partner):
    return pltpu.make_async_remote_copy(
        src_ref=source,
        dst_ref=target,
        send_sem=send_sem,
        recv_sem=recv_sem,
        device_id=partner,
        device_id_type=MESH_ID,
    )


class Spread:
    def __init__(self, call, pack):
        rows = pack.shape if not isinstance(pack, tuple) else (4, call.rows_of[pack], 128)
        self.pack = call.take(pack, pltpu.HBM)
        self.out = call.give((2, 4) + tuple(rows), BF16, pltpu.HBM)
        self.send_sem, self.recv_sem = call.sems(3), call.sems(3)
        self.core_send, self.core_recv, self.own_sem = call.sems(4), call.sems(4), call.sems(1)

    def block(self, get, at, n):
        c, z = at["mesh"][3:]
        return get(self.out).at[c, lax.rem(z + 4 - n, 4)]

    def move(self, get, at, n):
        return push(
            get(self.pack),
            self.block(get, at, 0),
            get(self.send_sem).at[n - 1],
            get(self.recv_sem).at[n - 1],
            along(at)[n - 1],
        )

    def to_core(self, get, at, n):
        target = self.block(get, at, n)
        return push(
            get(self.pack) if n == 0 else target,
            target,
            get(self.core_send).at[n],
            get(self.core_recv).at[n],
            at["core"],
        )

    def own(self, get, at):
        return pltpu.make_async_copy(
            get(self.pack), self.block(get, at, 0), get(self.own_sem).at[0]
        )

    def launch(self, get, at):
        for n in (2, 1, 3):
            self.move(get, at, n).start()
        self.to_core(get, at, 0).start()
        self.own(get, at).start()

    def pass_on(self, get, at):
        for n in (1, 3, 2):
            self.move(get, at, n).wait_recv()
            self.to_core(get, at, n).start()

    def finish(self, get, at):
        self.own(get, at).wait()
        for n in range(4):
            self.to_core(get, at, n).wait()
        for n in range(1, 4):
            self.move(get, at, n).wait_send()


class Gather:
    def __init__(self, call, shares, rows, first=0):
        self.call, self.shares, self.rows, self.first = call, call.take(shares, pltpu.HBM), rows, first
        self.landed, self.own = call.hold((3, 4, rows, 128), BF16), call.hold((4, rows, 128), BF16)
        self.out = call.keep((4, rows, 128), BF16)
        self.send_sem, self.recv_sem, self.own_sem = call.sems(3), call.sems(3), call.sems(1)

    def share(self, get, plane):
        return get(self.shares).at[plane, :, pl.ds(self.first, self.rows)]

    def move(self, get, at, n):
        return push(
            self.share(get, lax.rem(at["mesh"][4] + n, 4)),
            get(self.landed).at[n - 1],
            get(self.send_sem).at[n - 1],
            get(self.recv_sem).at[n - 1],
            along(at)[n - 1],
        )

    def mine(self, get, at):
        return pltpu.make_async_copy(
            self.share(get, at["mesh"][4]), get(self.own), get(self.own_sem).at[0]
        )

    def launch(self, get, at):
        for n in (2, 1, 3):
            self.move(get, at, n).start()
        self.mine(get, at).start()

    def finish(self, get, at):
        self.mine(get, at).wait()
        for n in range(1, 4):
            self.move(get, at, n).wait()
        landed, own, out = get(self.landed), get(self.own), get(self.out)
        for q in range(4):
            total = own[q].astype(F32) + landed[0, q].astype(F32)
            out[q] = (total + landed[1, q].astype(F32) + landed[2, q].astype(F32)).astype(BF16)
        self.call.save(get, self.out)


class Swap:
    def __init__(self, call, pack):
        self.pack = call.take(pack, pltpu.HBM)
        rows = call.rows_of[pack] if isinstance(pack, tuple) else pack.shape[1]
        self.out = call.give((4, rows, 128), BF16, pltpu.HBM)
        call.rows_of[self.out] = rows
        self.send_sem, self.recv_sem, self.own_sem = call.sems(3), call.sems(3), call.sems(1)

    def start(self, get, at):
        hi, k, y, c, z = at["mesh"]
        own = hi * 2 + y
        pack, out = get(self.pack), get(self.out)
        self.copies = [pltpu.make_async_copy(pack.at[own], out.at[own], get(self.own_sem).at[0])]
        for i, (name, q) in enumerate(
            (("d", (1 - hi) * 2 + 1 - y), ("x", (1 - hi) * 2 + y), ("y", hi * 2 + 1 - y))
        ):
            send, recv = get(self.send_sem).at[i], get(self.recv_sem).at[i]
            self.copies.append(push(pack.at[q], out.at[own], send, recv, at[name]))
        for copy in self.copies:
            copy.start()

    def finish(self, get, at):
        for copy in self.copies:
            copy.wait()


class Slots:
    def __init__(self, call, arrays, inward):
        self.inward = inward
        self.call, self.arrays = call, [call.fetch(array) for array in arrays]
        shape = (128, 1024) if inward else (2, 64, 1024)
        self.outs = [call.keep(shape, BF16) for array in arrays]
        self.send_sem, self.recv_sem = call.sems(2 * len(arrays)), call.sems(2 * len(arrays))

    def ends(self, get, at, j, step):
        z = at["mesh"][4]
        low = lax.div(z, 2)
        other = low if step == 0 else 1 - low
        array, out = get(self.arrays[j]), get(self.outs[j])
        if self.inward:
            return array.at[other], out.at[pl.ds(pl.multiple_of(low * 64, 64), 64)]
        return array.at[pl.ds(pl.multiple_of(other * 64, 64), 64)], out.at[low]

    def stays(self, at):
        hi, z = at["mesh"][0], at["mesh"][4]
        return lax.rem(z, 2) == hi

    def copy(self, get, at, j, step):
        hi, k, y, c, z = at["mesh"]
        low = lax.div(z, 2)
        partner = (lax.rem(z, 2), k, y, c, 2 * (low if step == 0 else 1 - low) + hi)
        source, target = self.ends(get, at, j, step)
        return pltpu.make_async_remote_copy(
            src_ref=source,
            dst_ref=target,
            send_sem=get(self.send_sem).at[2 * j + step],
            recv_sem=get(self.recv_sem).at[2 * j + step],
            device_id=partner,
            device_id_type=MESH_ID,
        )

    def start(self, get, at):
        stays = self.stays(at)
        for j in range(len(self.arrays)):
            self.copy(get, at, j, 1).start()

        @pl.when(jnp.logical_not(stays))
        def _():
            for j in range(len(self.arrays)):
                self.copy(get, at, j, 0).start()

        @pl.when(stays)
        def _():
            for j in range(len(self.arrays)):
                source, target = self.ends(get, at, j, 0)
                target[...] = source[...]

    def finish(self, get, at):
        for j in range(len(self.arrays)):
            self.copy(get, at, j, 1).wait()

        @pl.when(jnp.logical_not(self.stays(at)))
        def _():
            for j in range(len(self.arrays)):
                self.copy(get, at, j, 0).wait()

        for out in self.outs:
            self.call.save(get, out)


def all_partners(at):
    hi, k, y, c, z = at["mesh"]
    plane = [
        ((hi + i) % 2, k, (y + j) % 2, (c + n) % 2, z)
        for i in range(2)
        for j in range(2)
        for n in range(2)
        if i + j + n > 0
    ]
    ways = [((hi + i) % 2, k, y, c, (z + n) % 4) for i in range(2) for n in range(1, 4)]
    return plane, ways


def meeting(at):
    plane, ways = all_partners(at)
    return plane + ways


class Vectors:
    def __init__(self, call, vectors, inward):
        self.inward = inward
        self.source = call.take(vectors)
        self.out = call.give((16, 1024) if inward else (16, 128), F32)
        self.landed, self.whole = call.hold((7, 16, 128), F32), call.hold((16, 128), F32)
        self.split, self.along = call.hold((8, 16, 128), F32), call.hold((3, 16, 128), F32)
        self.send_sem, self.recv_sem = call.sems(10), call.sems(10)

    def move(self, get, i, source, target, partner):
        return push(source, target, get(self.send_sem).at[i], get(self.recv_sem).at[i], partner)

    def planes(self, get, at, source):
        return [
            self.move(get, n, source, get(self.along).at[n], partner)
            for n, partner in enumerate(along(at))
        ]

    def block(self, at):
        hi, k, y, c, z = at["mesh"]
        return (hi * 2 + y) * 2 + c

    def start(self, get, at):
        plane = all_partners(at)[0]
        if self.inward:
            self.copies = self.planes(get, at, get(self.source))
        else:
            split = get(self.split)
            for d in range(8):
                split[d] = get(self.source)[:, d * 128 : d * 128 + 128]
            self.copies = [
                self.move(
                    get,
                    3 + i,
                    split.at[(partner[0] * 2 + partner[2]) * 2 + partner[3]],
                    get(self.landed).at[i],
                    partner,
                )
                for i, partner in enumerate(plane)
            ]
        for copy in self.copies:
            copy.start()

    def second(self, get, at):
        plane = all_partners(at)[0]
        for copy in self.copies:
            copy.wait()
        whole, out = get(self.whole), get(self.out)
        if self.inward:
            whole[...] = get(self.source)[...] + jnp.sum(get(self.along)[...], 0)
            block = pl.ds(pl.multiple_of(self.block(at) * 128, 128), 128)
            out[:, block] = whole[...]
            self.copies = [
                self.move(get, 3 + i, whole, out.at[:, block], partner)
                for i, partner in enumerate(plane)
            ]
        else:
            whole[...] = get(self.split)[self.block(at)] + jnp.sum(get(self.landed)[...], 0)
            self.copies = self.planes(get, at, whole)
        for copy in self.copies:
            copy.start()

    def finish(self, get, at):
        for copy in self.copies:
            copy.wait()
        if not self.inward:
            get(self.out)[...] = get(self.whole)[...] + jnp.sum(get(self.along)[...], 0)


class Pack:
    def __init__(self, call, matrices):
        self.parts = [(call.fetch(array), index, across) for array, index, across in matrices]
        counts = [
            (array.shape[-1] if across else array.shape[-2]) // 4
            for array, index, across in matrices
        ]
        self.counts = counts
        self.out = call.hold((4, sum(counts), 128), BF16)
        call.rows_of[self.out] = sum(counts)

    def make(self, get):
        out, base = get(self.out), 0
        for (part, index, across), count in zip(self.parts, self.counts, strict=True):
            part = get(part)
            whole = part[...] if index is None else part[index]
            if across:
                whole = whole.astype(F32).T.astype(BF16)
            out[:, base : base + count, :] = whole.reshape(4, count, 128)
            base += count


def by_owner(rows, back=False):
    copies = lax.axis_size("k")
    if copies == 1:
        return rows
    shape, width = rows.shape, 128 // copies
    if back:
        rows = rows.reshape(-1, 2, 2, 2, copies, width).transpose(0, 1, 4, 2, 3, 5)
    else:
        rows = rows.reshape(-1, 2, copies, 2, 2, width).transpose(0, 1, 3, 4, 2, 5)
    return rows.reshape(shape)


def unpacked(packs, rows, wide):
    call = Call()
    rows_in = [call.fetch(array) for array in rows]
    ins = [call.fetch(array) for array in packs]
    plans = []
    for handle, array, kinds in zip(ins, packs, wide, strict=True):
        base = 0
        for kind in kinds:
            count = 256 if kind in ("up", "down") else 64
            if kind == "q":
                out = call.give((3, 128, 256), F32)
                plans += [(handle, base + i * 64, 64, out, i, True) for i in range(3)]
                base += 192
                continue
            shape = (128, 4 * count) if kind == "up" else (4 * count, 128)
            plans.append((handle, base, count, call.give(shape, F32), None, kind == "up"))
            base += count
    outs = [call.give(array.shape, F32) for array in rows]

    def body(get):
        for handle, base, count, out, index, across in plans:
            whole = get(handle)[:, base : base + count, :].astype(F32).reshape(4 * count, 128)
            whole = whole.T if across else whole
            if index is None:
                get(out)[...] = whole
            else:
                get(out)[index] = whole
        for source, out in zip(rows_in, outs, strict=True):
            get(out)[...] = get(source)[...].astype(F32)

    return call.run(body, "unpacked", None, 4 * MICROSECOND)


def local(
    source,
    target,
    cotangent,
    source_len,
    target_len,
    source_seg,
    target_seg,
    enc_qkv,
    enc_proj,
    enc_up,
    enc_down,
    enc_gain,
    enc_shift,
    dec_qkv,
    dec_proj,
    cross_qkv,
    cross_proj,
    dec_up,
    dec_down,
    dec_gain,
    dec_shift,
):
    copies, z = lax.axis_size("k"), lax.axis_index("mp")
    vectors = jnp.concatenate([enc_gain, enc_shift, dec_gain, dec_shift, dec_shift[:2]], 0)
    if copies > 1:
        vectors = lax.all_gather(vectors, "k", axis=1, tiled=True)
    vectors = vectors.reshape(16, copies, 1, 32 // copies)
    vectors = jnp.where(jnp.arange(4)[:, None] == z, vectors, 0.0).reshape(16, 128)
    facts = jnp.concatenate([source_seg, target_seg], 0)
    lengths = jnp.concatenate([source_len, target_len], 0)
    facts = jnp.concatenate([facts, jnp.broadcast_to(lengths[:, None], (4, 128))], 1)

    def widen(array, axis):
        return array if copies == 1 else lax.all_gather(array, "k", axis=axis, tiled=True)

    enc_qkv, dec_qkv, cross_qkv = (widen(array, 1) for array in (enc_qkv, dec_qkv, cross_qkv))
    enc_proj, dec_proj, cross_proj = (widen(array, 1) for array in (enc_proj, dec_proj, cross_proj))
    enc_up, dec_up = widen(enc_up, 0), widen(dec_up, 0)
    enc_down, dec_down = widen(enc_down, 1), widen(dec_down, 1)

    ENC_G, ENC_B, DEC_G, DEC_B = 0, 3, 6, 10
    SELF, SELF_O = 192, 64
    Q, QKV, KV, O, FIRST_O = (0, 64), (0, 192), (64, 128), (192, 64), (0, 64)
    UP, DOWN = (0, 256), (256, 256)

    def pick(call, packed, span, base=0):
        return Weight(call, packed, base + span[0], span[1])

    def forward_mid(call, residual, gain, shift, normed=None):
        vec, res = call.take(vectors), call.fetch(residual)
        kept = call.keep((128, 1024), F32)

        def mid(get, total):
            stream = get(res)[...].astype(F32) + total
            get(kept)[...] = stream
            call.save(get, kept)
            unit, scale = unit_of(stream)
            made = (unit * get(vec)[gain : gain + 1] + get(vec)[shift : shift + 1]).astype(BF16)
            if normed is not None:
                get(normed)[...] = made
                call.save(get, normed)
            return made

        mid.kept = kept
        return mid

    def backward_mid(call, stream, gain, residual=None, dtype=F32):
        vec, kept = call.take(vectors), call.fetch(stream)
        res = None if residual is None else call.fetch(residual)
        grad_out, share_out = call.keep((128, 1024), dtype), call.give((2, 1024), F32)

        def mid(get, total):
            grad, shares = norm_back(get(kept)[...].astype(F32), get(vec)[gain : gain + 1], total)
            if res is not None:
                grad = grad + get(res)[...]
            get(grad_out)[...] = grad.astype(dtype)
            call.save(get, grad_out)
            get(share_out)[...] = shares
            return grad.astype(BF16)

        mid.kept, mid.shares = grad_out, share_out
        return mid

    def deactivated(call, slope):
        out = call.keep((4, 128, 1024), BF16, 4)

        def store(get, at, row, column, value):
            get(out)[row] = (value * get(slope)[row]).astype(BF16)
            call.save(get, out, row)

        return Kept(out, store)

    call = Call()
    slots = Slots(call, [by_owner(source), by_owner(target)], True)
    stream_h, target_h = slots.outs
    first_vectors = Vectors(call, vectors, True)
    fact_in = call.take(facts)
    fact_own, fact_room = call.hold((2, 8, 128), F32), call.hold((2, 8, 128), F32)
    fact_rows, fact_columns = call.give((8, 1024), F32), call.keep((1024, 128), F32)
    fact_send, fact_recv = call.sems(1), call.sems(1)

    def three(array):
        return [(array, i, True) for i in range(3)]

    pack_1 = Pack(call, three(enc_qkv) + three(dec_qkv))
    pack_o = Pack(call, [(enc_proj, None, False), (dec_proj, None, False)])
    pack_2 = Pack(call, [(enc_up, None, True), (enc_down, None, False)])
    pack_3 = Pack(call, three(cross_qkv) + [(cross_proj, None, False)])
    pack_4 = Pack(call, [(dec_up, None, True), (dec_down, None, False)])
    swap_1, swap_o, swap_2, swap_3, swap_4 = (
        Swap(call, pack.out) for pack in (pack_1, pack_o, pack_2, pack_3, pack_4)
    )
    spread_1, spread_o, spread_2, spread_3, spread_4 = (
        Spread(call, swap.out) for swap in (swap_1, swap_o, swap_2, swap_3, swap_4)
    )

    def count_facts(get):
        given = get(fact_in)[...]
        lane = lax.broadcasted_iota(jnp.int32, (4, 128), 1)
        table = jnp.where(lane == 0, given[:, 1024:].astype(F32), 0.0)
        for p in range(1, PAIRS):
            before = jnp.sum((given[:, :1024] < p).astype(F32), 1, keepdims=True)
            table = table + jnp.where(lane == p, before, 0.0)
        own = get(fact_own)
        own[...] = jnp.zeros_like(own)
        for slot in range(2):
            own[slot, 0:1] = table[slot : slot + 1]
            own[slot, 1:2] = table[2 + slot : 3 + slot]

    def place_facts(get, at):
        hi, k, y, c, z = at["mesh"]
        slot = lax.div(z, 2)
        table = jnp.where(lax.rem(z, 2) == hi, get(fact_own)[slot], get(fact_room)[slot])

        def kinds(index):
            core = jnp.where(index < 512, c, 1 - c)
            part = index % 512
            place = (part // 256) * 512 + core * 256 + ((part // 64) % 2) * 128
            place = (place + ((part // 128) % 2) * 64 + part % 64).astype(F32)
            found = []
            for row in range(2):
                ids = jnp.zeros_like(place)
                for p in range(1, PAIRS):
                    ids = ids + jnp.where(place >= table[row : row + 1, p : p + 1], 1.0, 0.0)
                found.append(ids)
            live = [jnp.where(place < table[row : row + 1, 0:1], 1.0, 0.0) for row in range(2)]
            return found + [place] + live

        across = kinds(lax.broadcasted_iota(jnp.int32, (1, 1024), 1))
        down = kinds(lax.broadcasted_iota(jnp.int32, (1024, 128), 0))
        rows, columns = get(fact_rows), get(fact_columns)
        rows[...] = jnp.zeros_like(rows)
        lane = lax.broadcasted_iota(jnp.int32, (1024, 128), 1)
        wide = jnp.zeros((1024, 128), F32)
        for i in range(5):
            rows[i : i + 1] = across[i]
            wide = jnp.where(lane == i, down[i], wide)
        columns[...] = wide
        call.save(get, fact_columns)

    def first_mid(stream, gain, shift):
        def mid(get, total):
            unit, scale = unit_of(get(stream)[...].astype(F32))
            vec = get(first_vectors.out)
            return (unit * vec[gain : gain + 1] + vec[shift : shift + 1]).astype(BF16)

        return mid

    job_a = Job(call, None, first_mid(stream_h, ENC_G, ENC_B), (None, None, None))
    job_c = Job(call, None, first_mid(target_h, DEC_G, DEC_B), (None, None, None))
    vectors = first_vectors.out

    plans = []
    for rows, base in ((job_a.gathered, 0), (job_c.gathered, SELF)):
        query, shared = Plain(call, 256), Shared(call, 512, 256)
        plans.append((call.fetch(rows), pick(call, spread_1.out, QKV, base), query, shared))
    enc_step = Attend(
        call, plans[0][2].out, plans[0][3].out, fact_rows, fact_columns, (SOURCE, SOURCE, False)
    )
    self_step = Attend(
        call, plans[1][2].out, plans[1][3].out, fact_rows, fact_columns, (TARGET, TARGET, True)
    )
    enc_o, self_o = pick(call, spread_o.out, FIRST_O), pick(call, spread_o.out, FIRST_O, SELF_O)
    mid = forward_mid(call, stream_h, ENC_G + 1, ENC_B + 1)
    job_b = Job(call, (enc_step.mixed, enc_o, [(0, 64)], 0), mid, (None, None, None))
    mid = forward_mid(call, target_h, DEC_G + 1, DEC_B + 1)
    cross_a, cross_b = pick(call, spread_3.out, Q), pick(call, spread_3.out, KV)
    cross_o = pick(call, spread_3.out, O)
    query, shared = Plain(call, 256), Shared(call, 512)
    job_d = Job(call, (self_step.mixed, self_o, [(0, 64)], 0), mid, (cross_a, [(0, 64)], query.store))
    enc_u, enc_d = pick(call, spread_2.out, UP), pick(call, spread_2.out, DOWN)
    feed = Feed(call, job_b.gathered, enc_u, enc_d)
    mid = forward_mid(call, job_b.kept, ENC_G + 2, ENC_B + 2)
    job_m = Job(call, feed, mid, (cross_b, [(0, 64), (64, 64)], shared.store))
    cross_step = Attend(
        call, query.out, shared.out, fact_rows, fact_columns, (TARGET, SOURCE, False)
    )
    mid = forward_mid(call, job_d.kept, DEC_G + 2, DEC_B + 2)
    job_e = Job(call, (cross_step.mixed, cross_o, [(0, 64)], 0), mid, (None, None, None))

    def onward(get, at):
        first_vectors.start(get, at)
        slots.start(get, at)
        pack_1.make(get)
        swap_1.start(get, at)
        count_facts(get)
        fact_copy = push(
            get(fact_own), get(fact_room), get(fact_send).at[0], get(fact_recv).at[0], at["x"]
        )
        fact_copy.start()
        first_vectors.second(get, at)
        swap_1.finish(get, at)
        spread_1.launch(get, at)
        for pack in (pack_o, pack_2):
            pack.make(get)
        first_vectors.finish(get, at)
        slots.finish(get, at)
        job_a.settle(get, at)
        job_c.settle(get, at)
        fact_copy.wait()
        place_facts(get, at)
        job_a.rows_forward(get, at)
        job_c.rows_forward(get, at)
        swap_o.start(get, at)
        swap_2.start(get, at)
        for pack in (pack_3, pack_4):
            pack.make(get)
        job_a.collect(get, at)
        job_c.collect(get, at)
        enc_step.prepare(get)
        swap_o.finish(get, at)
        swap_2.finish(get, at)
        job_a.drain()
        job_c.drain()
        spread_1.pass_on(get, at)
        spread_o.launch(get, at)
        spread_2.launch(get, at)
        swap_3.start(get, at)
        swap_4.start(get, at)
        spread_1.finish(get, at)
        for plan in plans:
            plan[1].start(get)
        for rows, weight, queries, keys in plans:
            weight.wait(get)
            for row in range(4):
                for m in range(3):
                    made = nt(get(rows)[row], weight.matrix(get, m * 64, 64))
                    (queries if m == 0 else keys).store(get, at, row, m * 256, made)
        for plan in plans:
            plan[3].finish(get)
        enc_step.pairs(get, 0, 2)
        call.save(get, enc_step.mixed)
        spread_o.pass_on(get, at)
        swap_3.finish(get, at)
        swap_4.finish(get, at)
        spread_o.finish(get, at)
        enc_o.start(get)
        self_o.start(get)
        job_b.sums(get, at)
        self_step.prepare(get)
        self_step.pairs(get, 0, 1)
        job_b.sum_forward(get, at)
        self_step.pairs(get, 1, 2)
        call.save(get, self_step.mixed)
        job_b.sum_own(get, at)
        job_d.sums(get, at)
        job_b.settle(get, at)
        job_d.sum_forward(get, at)
        job_d.sum_own(get, at)
        job_b.rows_forward(get, at)
        spread_2.pass_on(get, at)
        spread_3.launch(get, at)
        job_d.settle(get, at)
        spread_2.finish(get, at)
        enc_u.start(get)
        enc_d.start(get)
        job_b.collect(get, at)
        job_m.sums(get, at)
        job_d.rows_forward(get, at)
        job_m.sum_forward(get, at)
        job_m.sum_own(get, at)
        spread_3.pass_on(get, at)
        spread_4.launch(get, at)
        job_m.settle(get, at)
        spread_3.finish(get, at)
        for weight in (cross_a, cross_b, cross_o):
            weight.start(get)
        job_m.rows_forward(get, at)
        job_d.product(get, at, at["own_row"])
        job_d.collect(get, at)
        job_m.product(get, at, at["own_row"])
        job_m.collect(get, at)
        for job in (job_b, job_d, job_m):
            job.drain()
        shared.finish(get)
        cross_step.late(get, at)
        job_e.sums(get, at)
        job_e.sum_forward(get, at)
        job_e.sum_own(get, at)
        job_e.settle(get, at)
        spread_4.pass_on(get, at)
        job_e.rows_forward(get, at)
        job_e.collect(get, at)
        job_e.drain()
        spread_4.finish(get, at)

    (
        stream_in,
        target_in,
        vectors,
        fact_rows,
        fact_columns,
        unused,
        unused,
        unused,
        unused,
        unused,
        first_w,
        first_o,
        second_w,
        cross_w,
        third_w,
        rows_a,
        rows_c,
        enc_q,
        enc_kv,
        self_q,
        self_kv,
        enc_mixed,
        enc_total,
        self_mixed,
        self_total,
        stream_mid,
        rows_b,
        target_mid,
        cross_q,
        cross_kv,
        rows_d,
        enc_hidden,
        enc_slope,
        stream_end,
        memory,
        cross_mixed,
        cross_total,
        target_late,
        rows_e,
    ) = run_body(call, onward, ["all"], "onward", 0, 170 * MICROSECOND)

    call = Call()
    dec_u, dec_d = pick(call, third_w, UP), pick(call, third_w, DOWN)
    cross_o = pick(call, cross_w, O)
    feed = Feed(call, rows_e, dec_u, dec_d)
    slots = Slots(call, [by_owner(cotangent)], True)
    vec, res, cot = call.take(vectors), call.fetch(target_late), slots.outs[0]
    decoded_out, grad_end = call.keep((128, 1024), BF16), call.hold((128, 1024), F32)
    share_out = call.give((2, 1024), F32)

    def last_mid(get, total):
        stream = get(res)[...] + total
        gain, shift = get(vec)[DEC_G + 3 : DEC_G + 4], get(vec)[DEC_B + 3 : DEC_B + 4]
        unit, unused = unit_of(stream)
        get(decoded_out)[...] = (unit * gain + shift).astype(BF16)
        grad, shares = norm_back(stream, gain, get(cot)[...].astype(F32))
        get(grad_end)[...] = grad
        get(share_out)[...] = shares
        call.save(get, decoded_out)
        return grad.astype(BF16)

    active = deactivated(call, feed.slope)
    job_t = Job(call, feed, last_mid, (dec_d, [(0, 256)], active.store))
    mid = backward_mid(call, target_late, DEC_G + 2, grad_end)
    query = Plain(call, 256)
    job_c = Job(call, (active.out, dec_u, [(0, 256)], 0), mid, (cross_o, [(0, 64)], query.store))
    down_shares = Shares(call, [(feed.hidden, 0, job_t.gathered)], 256, False)
    joined = call.give((4, 4, 512, 128), BF16, pltpu.HBM)
    up_shares = Shares(call, [(active.out, 0, feed.rows)], 256, joined, 0)
    back = AttendBack(
        call,
        cross_q,
        cross_kv,
        query.out,
        cross_total,
        fact_rows,
        fact_columns,
        (TARGET, SOURCE, False),
    )
    cross_shares = Shares(
        call,
        [
            (back.out, 0, rows_d),
            (back.out, 256, memory),
            (back.out, 512, memory),
            (cross_mixed, 0, job_c.gathered),
        ],
        64,
        joined,
        256,
    )
    gather = Gather(call, down_shares.room, 256)

    def turning(get, at):
        for weight in (dec_u, dec_d, cross_o):
            weight.start(get)
        slots.start(get, at)
        job_t.sums(get, at)
        job_t.sum_forward(get, at)
        job_t.sum_own(get, at)
        slots.finish(get, at)
        job_t.settle(get, at)
        job_t.product(get, at, at["own_row"])
        job_t.rows_forward(get, at)
        job_t.collect(get, at)
        job_c.sums(get, at)
        job_c.sum_forward(get, at)
        job_c.sum_own(get, at)
        down_shares.middle(get, at)
        down_shares.finish(get, at)
        job_c.settle(get, at)
        gather.launch(get, at)
        job_c.product(get, at, at["own_row"])
        job_c.rows_forward(get, at)
        up_shares.middle(get, at)
        job_c.collect(get, at)
        up_shares.finish(get, at)
        job_t.drain()
        job_c.drain()
        back.late(get, at)
        cross_shares.middle(get, at)
        cross_shares.finish(get, at)
        gather.finish(get, at)

    (
        dec_hidden,
        dec_slope,
        unused,
        decoded,
        norm_3,
        dec_grad_act,
        grad_rows_e,
        grad_late,
        norm_2,
        cross_grad_mixed,
        grad_rows_d,
        joined_s,
        cross_grads,
        down_g,
    ) = run_body(call, turning, ["all"], "turning", 1, 62 * MICROSECOND)

    call = Call()
    cross_a, cross_b = pick(call, cross_w, Q), pick(call, cross_w, KV)
    self_o, enc_d = pick(call, first_o, FIRST_O, SELF_O), pick(call, second_w, DOWN)
    slots = Slots(call, [decoded], False)
    mid = backward_mid(call, target_mid, DEC_G + 1, grad_late)
    query = Plain(call, 256)
    job_t = Job(call, (cross_grads, cross_a, [(0, 64)], 0), mid, (self_o, [(0, 64)], query.store))
    mid = backward_mid(call, stream_end, ENC_G + 2)
    active = deactivated(call, call.fetch(enc_slope))
    job_s = Job(
        call,
        (cross_grads, cross_b, [(0, 64), (64, 64)], 256),
        mid,
        (enc_d, [(0, 256)], active.store),
    )
    shares = Shares(
        call, [(active.out, 0, rows_b), (enc_hidden, 0, job_s.gathered)], 256
    )
    gather, swap = Gather(call, joined_s, 512), Swap(call, down_g)

    def backing(get, at):
        gather.launch(get, at)
        for weight in (cross_b, cross_a, enc_d, self_o):
            weight.start(get)
        job_s.sums(get, at)
        job_t.sums(get, at)
        job_s.sum_forward(get, at)
        job_t.sum_forward(get, at)
        job_s.sum_own(get, at)
        job_s.settle(get, at)
        job_t.sum_own(get, at)
        job_t.settle(get, at)
        slots.start(get, at)
        job_s.product(get, at, at["own_row"])
        job_s.rows_forward(get, at)
        job_t.product(get, at, at["own_row"])
        job_t.rows_forward(get, at)
        swap.start(get, at)
        job_s.collect(get, at)
        shares.middle(get, at)
        job_t.collect(get, at)
        shares.finish(get, at)
        job_s.drain()
        job_t.drain()
        slots.finish(get, at)
        swap.finish(get, at)
        gather.finish(get, at)

    (
        decoded,
        grad_mid,
        norm_1,
        self_grad_mixed,
        grad_rows_c,
        grad_stream,
        enc_norm_2,
        enc_grad_act,
        grad_rows_b,
        feed_s,
        up_cross_g,
        down_g,
    ) = run_body(call, backing, ["x", "y", "core", "d", "ways"], "backing", 2, 46 * MICROSECOND)

    call = Call()
    enc_u, enc_o = pick(call, second_w, UP), pick(call, first_o, FIRST_O)
    self_a = pick(call, first_w, QKV, SELF)
    self_back = AttendBack(
        call,
        self_q,
        self_kv,
        self_grad_mixed,
        self_total,
        fact_rows,
        fact_columns,
        (TARGET, TARGET, True),
    )
    mid = backward_mid(call, stream_mid, ENC_G + 1, grad_stream)
    query = Plain(call, 256)
    job_s = Job(call, (enc_grad_act, enc_u, [(0, 256)], 0), mid, (enc_o, [(0, 64)], query.store))
    mid = backward_mid(call, target_in, DEC_G, grad_mid, BF16)
    job_t = Job(call, (self_back.out, self_a, [(0, 64), (64, 64), (128, 64)], 0), mid, None)
    self_shares = Shares(
        call,
        [
            (self_back.out, 0, rows_c),
            (self_back.out, 256, rows_c),
            (self_back.out, 512, rows_c),
            (self_mixed, 0, grad_rows_c),
        ],
        64,
        False,
    )
    enc_back = AttendBack(
        call,
        enc_q,
        enc_kv,
        query.out,
        enc_total,
        fact_rows,
        fact_columns,
        (SOURCE, SOURCE, False),
    )
    enc_shares = Shares(
        call,
        [
            (enc_back.out, 0, rows_a),
            (enc_back.out, 256, rows_a),
            (enc_back.out, 512, rows_a),
            (enc_mixed, 0, job_s.gathered),
        ],
        64,
        False,
    )
    enc_a = pick(call, first_w, QKV)
    mid = backward_mid(call, stream_in, ENC_G, job_s.kept, BF16)
    job_f = Job(call, (enc_back.out, enc_a, [(0, 64), (64, 64), (128, 64)], 0), mid, None)
    gather_f, gather_s = Gather(call, feed_s, 512), Gather(call, self_shares.room, 256)
    gather_e = Gather(call, enc_shares.room, 256)
    for gather, rows in ((gather_f, 512), (gather_s, 256), (gather_e, 256)):
        call.rows_of[gather.out] = rows
    swap, swap_f = Swap(call, up_cross_g), Swap(call, gather_f.out)
    swap_s, swap_e = Swap(call, gather_s.out), Swap(call, gather_e.out)
    target_slots, source_slots = Slots(call, [job_t.kept], False), Slots(call, [job_f.kept], False)
    others = [call.take(norm) for norm in (norm_1, norm_2, norm_3, enc_norm_2)]
    norm_sum = call.hold((16, 1024), F32)
    sums = Vectors(call, norm_sum, False)

    def selfward(get, at):
        gather_f.launch(get, at)
        for weight in (enc_u, self_a, enc_o, enc_a):
            weight.start(get)
        self_back.prepare(get)
        job_s.sums(get, at)
        self_back.pair(get, at, 0)
        job_s.sum_forward(get, at)
        self_back.pair(get, at, 1)
        self_back.end(get)
        job_s.sum_own(get, at)
        job_t.sums(get, at)
        job_s.settle(get, at)
        job_t.sum_forward(get, at)
        job_t.sum_own(get, at)
        self_shares.middle(get, at)
        self_shares.finish(get, at)
        gather_s.launch(get, at)
        job_s.product(get, at, at["own_row"])
        job_s.rows_forward(get, at)
        job_t.settle(get, at)
        target_slots.start(get, at)
        swap.start(get, at)
        job_s.collect(get, at)
        job_s.drain()
        job_t.drain()
        enc_back.late(get, at)
        enc_shares.middle(get, at)
        enc_shares.finish(get, at)
        gather_e.launch(get, at)
        job_f.sums(get, at)
        job_f.sum_forward(get, at)
        job_f.sum_own(get, at)
        job_f.settle(get, at)
        source_slots.start(get, at)
        total = get(norm_sum)
        for row, shares in (
            (0, get(job_f.shares)),
            (1, get(job_s.shares)),
            (2, get(others[3])),
            (6, get(job_t.shares)),
            (7, get(others[0])),
            (8, get(others[1])),
            (9, get(others[2])),
        ):
            below = row + (3 if row < 6 else 4)
            total[row : row + 1] = shares[0:1]
            total[below : below + 1] = shares[1:2]
        total[14:16] = jnp.zeros((2, 1024), F32)
        sums.start(get, at)
        job_f.drain()
        gather_f.finish(get, at)
        swap_f.start(get, at)
        sums.second(get, at)
        target_slots.finish(get, at)
        gather_s.finish(get, at)
        swap_s.start(get, at)
        sums.finish(get, at)
        source_slots.finish(get, at)
        swap.finish(get, at)
        swap_f.finish(get, at)
        gather_e.finish(get, at)
        swap_e.start(get, at)
        swap_s.finish(get, at)
        swap_e.finish(get, at)

    made = run_body(call, selfward, ["all"], "selfward", 3, 105 * MICROSECOND)
    up_cross_g, feed_g, self_g, enc_g, target_grad, source_grad, norm_grad = made[-7:]
    norm_grad = norm_grad.reshape(16, copies, 4, 32 // copies)
    if copies > 1:
        norm_grad = lax.psum_scatter(norm_grad, "k", scatter_dimension=1)
    norm_grad = norm_grad.reshape(16, 4, -1)
    norm_grad = lax.dynamic_index_in_dim(norm_grad, z, 1, False)

    (
        dec_d,
        dec_u,
        cross_a,
        cross_o,
        enc_u,
        enc_d,
        self_a,
        self_o,
        enc_a,
        enc_o,
        source_grad,
        target_grad,
    ) = unpacked(
        [down_g, up_cross_g, feed_g, self_g, enc_g],
        [source_grad, target_grad],
        [("down",), ("up", "q", "o"), ("up", "down"), ("q", "o"), ("q", "o")],
    )

    def narrow(array, axis):
        if copies == 1:
            return array
        return lax.psum_scatter(array, "k", scatter_dimension=axis, tiled=True)

    enc_a, self_a, cross_a = (narrow(array, 1) for array in (enc_a, self_a, cross_a))
    enc_o, self_o, cross_o = (narrow(array, 1) for array in (enc_o, self_o, cross_o))
    enc_u, dec_u = narrow(enc_u, 0), narrow(dec_u, 0)
    enc_d, dec_d = narrow(enc_d, 1), narrow(dec_d, 1)
    return (
        by_owner(decoded, True),
        by_owner(source_grad, True),
        by_owner(target_grad, True),
        enc_a,
        enc_o,
        enc_u,
        enc_d,
        norm_grad[:3],
        norm_grad[3:6],
        self_a,
        self_o,
        cross_a,
        cross_o,
        dec_u,
        dec_d,
        norm_grad[6:10],
        norm_grad[10:14],
    )


def solution(mesh):
    dp, seq, mp = (mesh.shape[name] for name in ("dp", "seq", "mp"))
    assert dp % 2 == 0 and seq == 4 and mp == 4
    fine = Mesh(mesh.devices.reshape(2, dp // 2, 2, 2, 4), AXES)
    d, s = ("hi", "k"), ("y", "c")
    rows = P(d, s + ("mp",), None)
    three, flat = P(None, d + s, "mp"), P("mp", d + s)
    up, vector = P(d + s, "mp"), P(None, d + s + ("mp",))
    attention, feeding = (three, flat), (up, flat)
    return jax.shard_map(
        local,
        mesh=fine,
        in_specs=(rows,) * 3
        + (P(d), P(d), P(d, None), P(d, None))
        + attention
        + feeding
        + (vector, vector)
        + attention * 2
        + feeding
        + (vector, vector),
        out_specs=(rows,) * 3
        + attention
        + feeding
        + (vector, vector)
        + attention * 2
        + feeding
        + (vector, vector),
        check_vma=False,
    )
```

time: 480 us -> 460 us (0.958)
  Pallas kernels: 416 us -> 439 us
  local copies, waits for them, and re-layouts: 24 us -> 9.38 us
  between operations: 15.2 us -> 1.21 us
  waiting for transfers between devices: 13.8 us -> 0 us
    pallas_call x10 -> x5, Pallas kernels: 416 us -> 439 us  [run(): pl.pallas_call(kernel, out_shape=tuple(self.shapes), in_specs=self.specs,...]
    all_gather x3 -> x0, waiting for transfers between devices: 9.38 us -> none  [gather_weights(): packed = lax.all_gather(packed, ('c', 'mp')).reshape(2, 4, 4, rows, 128)]
    unnamed x78 -> x17, local copies, waits for them, and re-layouts: 12.2 us -> 4.22 us
    slice x18 -> x0, local copies, waits for them, and re-layouts: 6.43 us -> none  [the longest x7 2.1 us: attend_shares(): return (jnp.swapaxes(grads[:3], 1, 2), grads[3])]
  transfers between devices with their start and end apart: 6 -> 0, of which waited for: 3 -> 0; matrix products, arithmetic and copies ran while one was open for 3% -> 0% of each run, Pallas kernels for 67% -> 0%
where the time goes in v5:
time: 460 us; the launch traced here: 452 us
  Pallas kernels  439 us (95%)
  local copies, waits for them, and re-layouts  9.38 us (2%)
    pallas_call x5, Pallas kernels, run(): pl.pallas_call(kernel, out_shape=tuple(self.shapes), in_specs=self.specs,...  439 us

profile of v5, /device:TPU:0, one launch (start us, length us, event | category | flops | bytes accessed | tf_op | source)
XLA Modules:
  0.0 452.0 jit_solution(15610069689220599442)
XLA Ops:
  0.7 0.1 broadcast_in_dim.33
  0.7 0.1 broadcast_in_dim.34
  0.8 0.7 slice.27
  1.5 2.2 concatenate.12
  3.7 0.1 broadcast_in_dim.37
  3.8 0.6 broadcast_select_fusion.refs_2_
  4.4 0.7 pad_add_fusion.1
  5.1 0.1 broadcast_in_dim.39
  5.2 1.3 pad_add_fusion.refs_3_
  6.5 185.8 %onward.1 = (bf16[128,1024]{1,0:T(8,128)(2,1)}, bf16[128,1024]{1,0:T(8,128)(2,1)}, f32[16,1024]{1,0:T(8,128)}, f32[8,1024]{1,0:T(8,128)}, f32[1024,128]{1,0:T(8,...) custom-call(bf16[2,64,1024]{2,1,0:T(8,128)(2,1)} %refs_0_.1, ...), custom_call_target="tpu_custom_call" | custom-call | flops 170000007168 | tf_op jit(solution)/shard_map/onward/pallas_call | solution.py:110
  192.4 0.0 copy-start
  192.4 0.8 copy-done
  193.2 0.0 copy-start.1
  193.2 0.8 copy-done.1
  194.0 0.0 copy-start.2
  194.0 0.7 copy-done.2
  194.7 76.2 %turning.1 = (bf16[4,128,1024]{2,1,0:T(8,128)(2,1)}, f32[4,128,1024]{2,1,0:T(8,128)}, bf16[128,1024]{1,0:T(8,128)(2,1)}, bf16[128,1024]{1,0:T(8,128)(2,1)}, f32[...) custom-call(bf16[2,4,4,512,128]{4,3,2,1,0:T(8,128)(2,1)} %get-tuple-, ...), custom_call_target="tpu_custom_call" | custom-call | flops 62000001024 | tf_op jit(solution)/shard_map/turning/pallas_call | solution.py:110
  271.0 0.0 copy-start.5
  271.0 0.0 copy-start.6
  271.0 59.2 %backing.1 = (bf16[2,64,1024]{2,1,0:T(8,128)(2,1)}, f32[128,1024]{1,0:T(8,128)}, f32[2,1024]{1,0:T(2,128)S(1)}, bf16[4,128,256]{2,1,0:T(8,128)(2,1)}, bf16[4,128...) custom-call(bf16[2,4,4,256,128]{4,3,2,1,0:T(8,128)(2,1)} %get-tuple-, ...), custom_call_target="tpu_custom_call" | custom-call | flops 46000001024 | tf_op jit(solution)/shard_map/backing/pallas_call | solution.py:110
  330.2 0.0 copy-done.5
  330.2 0.0 copy-done.6
  330.2 0.0 copy-start.3
  330.2 0.6 copy-done.3
  330.8 0.6 copy-done.4
  331.4 113.2 %selfward.1 = (bf16[4,128,768]{2,1,0:T(8,128)(2,1)}, f32[128,1024]{1,0:T(8,128)}, f32[2,1024]{1,0:T(2,128)}, bf16[4,128,256]{2,1,0:T(8,128)(2,1)}, bf16[4,128,10...) custom-call(bf16[2,4,4,512,128]{4,3,2,1,0:T(8,128)(2,1)} %get-tuple-, ...), custom_call_target="tpu_custom_call" | custom-call | flops 105000001536 | tf_op jit(solution)/shard_map/selfward/pallas_call | solution.py:110
  444.6 0.8 reshape_reshape.3
  445.4 0.6 copy_bitcast_fusion
  446.0 4.3 unpacked.1
  450.3 0.6 constant_dynamic-slice_fusion.3
  450.9 0.0 copy-done.7
  450.9 0.7 copy.47
  (5 shorter events, 0.0 us)
Async XLA Ops:
  192.4 0.8 copy-start
  193.2 0.8 copy-start.1
  194.0 0.7 copy-start.2
  271.0 59.2 %copy-start.5 = (f32[2,1024]{1,0:T(2,128)}, f32[2,1024]{1,0:T(2,128)S(1)}, u32[]{:S(2)}) copy-start(f32[2,1024]{1,0:T(2,128)S(1)} %get-tuple-element.137.refs_28_) | copy-start | bytes 24580
  271.0 59.2 %copy-start.6 = (f32[2,1024]{1,0:T(2,128)}, f32[2,1024]{1,0:T(2,128)S(1)}, u32[]{:S(2)}) copy-start(f32[2,1024]{1,0:T(2,128)S(1)} %get-tuple-element.136.refs_27_) | copy-start | bytes 24580
  330.2 0.6 copy-start.3
  330.8 0.6 copy-start.4
  446.0 4.9 %copy-start.7 = (bf16[2,64,1024]{2,1,0:T(8,128)(2,1)S(1)}, bf16[2,64,1024]{2,1,0:T(8,128)(2,1)}, u32[]{:S(2)}) copy-start(bf16[2,64,1024]{2,1,0:T(8,128)(2,1)} %get-tuple-element.182) | copy-start | bytes 786436
